TPU v7x, 512 devices: a whole 4x4x16 slice. The times are simulated.
512 devices in a mesh: ctx: 64 (over y, z), tp: 8 (over x, core).
Axes of the slice: x: 4, y: 4, z: 16, core: 2. Of those that a mesh axis runs over, the one named last changes fastest.
Arguments:
- inputs: bfloat16 [8192, 2048], P('ctx', 'tp'), may hold values from -6.5 to 6.5
- query_weight: bfloat16 [2048, 1024], P(None, 'tp'), may hold values from -0.125 to 0.125
- key_weight: bfloat16 [2048, 1024], P(None, 'tp'), may hold values from -0.125 to 0.125
- value_weight: bfloat16 [2048, 2048], P(None, 'tp'), may hold values from -0.125 to 0.125
- beta_weight: bfloat16 [2048, 16], P(None, 'tp'), may hold values from -1.5 to 1.5
- alpha_weight: bfloat16 [2048, 16], P(None, 'tp'), may hold values from -0.125 to 0.125
- query_filter: bfloat16 [4, 1024], P(None, 'tp'), may hold values from -3 to 3
- key_filter: bfloat16 [4, 1024], P(None, 'tp'), may hold values from -3 to 3
- value_filter: bfloat16 [4, 2048], P(None, 'tp'), may hold values from -3 to 3
- decay_log: float32 [16], P('tp'), may hold values from 0 to 2.77
- step_bias: float32 [16], P('tp'), may hold values from -16 to -2.3
- grad_core: bfloat16 [8192, 2048], P('ctx', 'tp'), may hold values from -6 to 6
Outputs:
- grad_inputs: bfloat16 [8192, 2048], P('ctx', 'tp')
All inputs are finite; a program needn't handle non-finite values.
Results may differ from a plain program's by a relative error of at most 0.019.
Values may be sent and summed in bfloat16 or wider, within the bound.
No kernel may reach another device: no remote copies, remote signals or barrier semaphores. Data moves between devices by JAX's collectives and lax.ppermute only.
A program may use at most 128 MiB of HBM per device.

v0:
```python
import jax
import jax.numpy as jnp
from jax import lax
from jax.sharding import PartitionSpec as P

DH = 128
CONV = 4
GROUP = 64


EPS = 1e-06


def from_behind(value, axis, steps):
    count = lax.axis_size(axis)
    leading, last = (max(0, -steps), min(count, count - steps))
    return lax.ppermute(value, axis, [(source, source + steps) for source in range(leading, last)])


def entering(value, axis, join, neutral, backward):
    count, mine = (lax.axis_size(axis), lax.axis_index(axis))
    pieces = jax.tree.map(lambda part: lax.all_gather(part, axis), value)
    if backward:
        pieces = jax.tree.map(lambda part: part[::-1], pieces)
        mine = count - 1 - mine
    subtotal = jax.tree.map(
        lambda part, zero: jnp.full_like(part, 0) + jnp.asarray(zero, part.dtype), value, neutral
    )

    def step(position, subtotal):
        longer = join(subtotal, jax.tree.map(lambda part: part[position], pieces))
        return jax.tree.map(lambda new, old: jnp.where(position < mine, new, old), longer, subtotal)

    return lax.fori_loop(0, count - 1, step, subtotal)


def contract(form, left_arr, right_arr):
    return jnp.einsum(
        form,
        left_arr,
        right_arr,
        precision=lax.Precision.HIGHEST,
        preferred_element_type=jnp.float32,
    )


def unit_lower_inverse(strict):
    size_now = strict.shape[-1]
    identity = jnp.eye(size_now, dtype=jnp.float32)
    result = identity - strict
    power_of = contract("...ij,...jk->...ik", strict, strict)
    covered = 2
    while covered < size_now:
        result = contract("...ij,...jk->...ik", result, identity + power_of)
        power_of = contract("...ij,...jk->...ik", power_of, power_of)
        covered = covered * 2
    return result


def conv_silu(padded, weight):
    tap_count = weight.shape[0]
    length = padded.shape[0] - tap_count + 1
    running = jnp.zeros((length, padded.shape[1]), jnp.float32)
    for tap_index in range(tap_count):
        running = (
            running + weight[tap_index].astype(jnp.float32) * padded[tap_index : tap_index + length]
        )
    return jax.nn.silu(running)


def normalized(rows_in, heads_count):
    shaped = rows_in.reshape(rows_in.shape[0], heads_count, -1)
    return shaped * lax.rsqrt(jnp.sum(shaped * shaped, axis=-1, keepdims=True) + EPS)


def to_blocks(rows_in, block_count):
    return rows_in.reshape(block_count, GROUP, rows_in.shape[1], -1).transpose(0, 2, 1, 3)


def prepare(
    query_pad,
    key_pad,
    value_pad,
    beta_raw,
    alpha_raw,
    query_filter,
    key_filter,
    value_filter,
    decay_log,
    step_bias,
):
    query_act = conv_silu(query_pad, query_filter)
    key_act = conv_silu(key_pad, key_filter)
    value_act = conv_silu(value_pad, value_filter)
    length = query_act.shape[0]
    key_heads = query_act.shape[1] // DH
    value_heads = value_act.shape[1] // DH
    ratio_kv = value_heads // key_heads
    block_count = length // GROUP
    query_unit = jnp.repeat(normalized(query_act, key_heads) * DH ** (-0.5), ratio_kv, axis=1)
    key_unit = jnp.repeat(normalized(key_act, key_heads), ratio_kv, axis=1)
    query_blk = to_blocks(query_unit, block_count)
    key_blk = to_blocks(key_unit, block_count)
    value_blk = to_blocks(value_act.reshape(length, value_heads, DH), block_count)
    beta_blk = jax.nn.sigmoid(beta_raw).reshape(block_count, GROUP, value_heads).transpose(0, 2, 1)
    log_decay = -jnp.exp(decay_log) * jax.nn.softplus(alpha_raw + step_bias)
    cum_decay = jnp.cumsum(
        log_decay.reshape(block_count, GROUP, value_heads).transpose(0, 2, 1), axis=-1
    )
    row_pos = lax.broadcasted_iota(jnp.int32, (GROUP, GROUP), 0)
    col_pos = lax.broadcasted_iota(jnp.int32, (GROUP, GROUP), 1)
    lower_mask = row_pos >= col_pos
    strictly = row_pos > col_pos
    gap_log = cum_decay[..., :, None] - cum_decay[..., None, :]
    decay_ij = jnp.where(lower_mask, jnp.exp(jnp.where(lower_mask, gap_log, 0.0)), 0.0)
    key_gram = contract("nhia,nhja->nhij", key_blk, key_blk)
    strict = jnp.where(strictly, beta_blk[..., :, None] * key_gram * decay_ij, 0.0)
    inverse = unit_lower_inverse(strict)
    gamma_at = jnp.exp(cum_decay)
    value_mix = contract("nhij,nhjb->nhib", inverse, beta_blk[..., None] * value_blk)
    key_weighted = contract("nhij,nhja->nhia", inverse, (beta_blk * gamma_at)[..., None] * key_blk)
    query_scaled = gamma_at[..., None] * query_blk
    key_tail = jnp.exp(cum_decay[..., -1:] - cum_decay)[..., None] * key_blk
    mixing = contract("nhia,nhja->nhij", query_blk, key_blk) * decay_ij
    end_decay = jnp.exp(cum_decay[..., -1])
    return (query_scaled, key_weighted, value_mix, key_tail, mixing, end_decay)


def transitions(pieces):
    query_scaled, key_weighted, value_mix, key_tail, mixing, end_decay = pieces
    unit_matrix = jnp.eye(key_tail.shape[-1], dtype=jnp.float32)
    trans_step = end_decay[..., None, None] * unit_matrix - contract(
        "nhca,nhcd->nhad", key_tail, key_weighted
    )
    inject_step = contract("nhca,nhcb->nhab", key_tail, value_mix)
    return (trans_step, inject_step)


def head_outputs(pieces, starts):
    query_scaled, key_weighted, value_mix, key_tail, mixing, end_decay = pieces
    fresh = value_mix - contract("nhca,nhab->nhcb", key_weighted, starts)
    return contract("nhca,nhab->nhcb", query_scaled, starts) + contract(
        "nhij,nhjb->nhib", mixing, fresh
    )


def slab_chain(pieces):
    trans_step, inject_step = transitions(pieces)
    heads_count = trans_step.shape[1]
    width_now = trans_step.shape[2]
    unit_matrix = jnp.broadcast_to(
        jnp.eye(width_now, dtype=jnp.float32), (heads_count, width_now, width_now)
    )
    zero_state = jnp.zeros(inject_step.shape[1:], jnp.float32)

    def advance(carried, step_pair):
        product, offset = carried
        step_trans, step_inject = step_pair
        moved = (
            contract("had,hde->hae", step_trans, product),
            contract("had,hdb->hab", step_trans, offset) + step_inject,
        )
        return (moved, carried)

    (slab_trans, slab_inject), (block_trans, block_seeds) = lax.scan(
        advance, (unit_matrix, zero_state), (trans_step, inject_step)
    )
    return (block_trans, block_seeds, slab_trans, slab_inject)


def finish(pieces, block_trans, block_seeds, incoming):
    starts = contract("nhad,hdb->nhab", block_trans, incoming) + block_seeds
    return head_outputs(pieces, starts)


def compose(earlier, later):
    return (
        contract("had,hde->hae", later[0], earlier[0]),
        contract("had,hdb->hab", later[0], earlier[1]) + later[1],
    )


def add_pair(first_item, second_item):
    return first_item + second_item


def local(
    inputs,
    query_weight,
    key_weight,
    value_weight,
    beta_weight,
    alpha_weight,
    query_filter,
    key_filter,
    value_filter,
    decay_log,
    step_bias,
    grad_core,
):
    rows_here = inputs.shape[0]
    conv_lag = CONV - 1
    weights = (query_weight, key_weight, value_weight, beta_weight, alpha_weight)

    def add_rows(shard_rows):
        return tuple(
            (jnp.dot(shard_rows, weight, preferred_element_type=jnp.float32) for weight in weights)
        )

    projected = add_rows(lax.all_gather(inputs, "tp", axis=1, tiled=True))
    rounded = lax.optimization_barrier(tuple((member.astype(jnp.bfloat16) for member in projected)))
    tail_rows = from_behind(
        (
            rounded[0][rows_here - conv_lag :],
            rounded[1][rows_here - conv_lag :],
            rounded[2][rows_here - conv_lag :],
        ),
        "ctx",
        1,
    )
    primals = tuple((member.astype(jnp.float32) for member in rounded)) + tuple(
        (member.astype(jnp.float32) for member in tail_rows)
    )

    def local_pieces(
        query_rows, key_rows, value_rows, beta_raw, alpha_raw, query_prev, key_prev, value_prev
    ):
        return prepare(
            jnp.concatenate([query_prev, query_rows], 0),
            jnp.concatenate([key_prev, key_rows], 0),
            jnp.concatenate([value_prev, value_rows], 0),
            beta_raw,
            alpha_raw,
            query_filter,
            key_filter,
            value_filter,
            decay_log,
            step_bias,
        )

    pieces, pieces_back = jax.vjp(local_pieces, *primals)
    chain_out, chain_back = jax.vjp(slab_chain, pieces)
    block_trans, block_seeds, slab_trans, slab_inject = chain_out
    heads_count = slab_trans.shape[0]
    width_now = slab_trans.shape[1]
    identity = (
        jnp.broadcast_to(
            jnp.eye(width_now, dtype=jnp.float32), (heads_count, width_now, width_now)
        ),
        jnp.zeros(slab_inject.shape, jnp.float32),
    )
    grad_heads = to_blocks(
        grad_core.astype(jnp.float32).reshape(rows_here, heads_count, -1), rows_here // GROUP
    )
    incoming = entering((slab_trans, slab_inject), "ctx", compose, identity, False)[1]
    _, finish_back = jax.vjp(finish, pieces, block_trans, block_seeds, incoming)
    grad_pieces_out, grad_block_trans, grad_block_seeds, after_grad = finish_back(grad_heads)
    later_grad = entering(
        (jnp.swapaxes(slab_trans, 1, 2), after_grad), "ctx", compose, identity, True
    )[1]
    grad_trans = contract("hab,hdb->had", later_grad, incoming)
    grad_chain = chain_back((grad_block_trans, grad_block_seeds, grad_trans, later_grad))[0]
    grad_pieces = jax.tree.map(add_pair, grad_pieces_out, grad_chain)
    gradients = pieces_back(grad_pieces)
    arriving = from_behind((gradients[5], gradients[6], gradients[7]), "ctx", -1)

    def with_tail(grad_rows, tail_part):
        return grad_rows + jnp.pad(tail_part, ((rows_here - conv_lag, 0), (0, 0)))

    full_grads = (
        with_tail(gradients[0], arriving[0]),
        with_tail(gradients[1], arriving[1]),
        with_tail(gradients[2], arriving[2]),
        gradients[3],
        gradients[4],
    )
    partial_value = jnp.zeros((rows_here, query_weight.shape[0]), jnp.float32)
    for grad_rows, weight in zip(full_grads, weights):
        partial_value = partial_value + lax.dot_general(
            grad_rows.astype(jnp.bfloat16),
            weight,
            (((1,), (1,)), ((), ())),
            preferred_element_type=jnp.float32,
        )
    summed = lax.psum(partial_value.astype(jnp.bfloat16), "tp").astype(jnp.float32)
    share_width = summed.shape[1] // lax.axis_size("tp")
    own_share = lax.dynamic_slice_in_dim(summed, lax.axis_index("tp") * share_width, share_width, 1)
    return own_share.astype(jnp.bfloat16)


def solution(mesh):
    return jax.shard_map(
        local,
        mesh=mesh,
        in_specs=(
            P("ctx", "tp"),
            P(None, "tp"),
            P(None, "tp"),
            P(None, "tp"),
            P(None, "tp"),
            P(None, "tp"),
            P(None, "tp"),
            P(None, "tp"),
            P(None, "tp"),
            P("tp"),
            P("tp"),
            P("ctx", "tp"),
        ),
        out_specs=P("ctx", "tp"),
        check_vma=False,
    )
```

profile of v0, /device:TPU:1, one launch (start us, length us, event | category | flops | bytes accessed | tf_op | source)
XLA Modules:
  0.0 901.2 jit_solution(13271062637945772358)
XLA Ops:
  6.5 20.2 %all_gather.27 = bf16[128,2048]{1,0:T(8,128)(2,1)S(1)} all-gather(bf16[128,256]{1,0:T(8,128)(2,1)} %param.20), channel_id=1, replica_groups=mesh['ctx'=64,'tp'=8] {'tp'}, dimensions={1}, use_global_device_ids=true | all-gather | bytes 589824 | tf_op jit(solution)/shard_map/all_gather | solution.py:210
  27.0 1.3 convolution_convert_fusion.1
  28.4 1.3 convolution_convert_fusion.2
  31.6 1.3 collective-permute-start
  32.9 1.3 collective-permute-start.1
  36.7 1.4 slice_convert_fusion.3
  45.9 1.4 fusion.92
  49.2 1.3 while.66
  52.0 3.0 collective-permute-start.2
  57.1 1.7 copy.160
  59.1 143.0 %all-gather.9.cloned.1.call-done = f32[128,128,128]{2,1,0:T(8,128)} async-done(((f32[2,128,128]{2,1,0:T(8,128)}), f32[128,128,128]{2,1,0:T(8,128)}) %all-gather.9.cloned.1.call-update) | async-done | bytes 8388624 | tf_op jit(solution)/shard_map/all_gather | solution.py:22
  202.1 154.8 %all-gather.11.cloned.1.call-done = f32[128,128,128]{2,1,0:T(8,128)} async-done(((f32[2,128,128]{2,1,0:T(8,128)}), f32[128,128,128]{2,1,0:T(8,128)}) %all-gather.11.cloned.1.call-update) | async-done | bytes 8388624 | tf_op jit(solution)/shard_map/all_gather | solution.py:22
  356.9 81.4 %while.67 = (s32[]{:T(128)}, f32[2,128,128]{2,1,0:T(8,128)S(1)}, s32[]{:T(128)}, f32[64,2,128,128]{3,2,1,0:T(8,128)}, f32[64,2,128,128]{3,2,1,0:T(8,128)}, /*index=5*/s32[]{:T(128)}, s32[]{:T(128)}) while((s32[]{:T(128)}, f32[2,128,128]{2,1,0:T(8,128)S(1)}, s32[]{:T(128)}, f32[64,2,128,128]{3,2,1,0:T(8,128)}, ...), condition=%wide.region_5.6_spmd.clone, body=%wide.region_4.5_spmd.clone.sunk | while | flops 50462724 | bytes 920159 | solution.py:34
  378.9 1.3 fusion.389
  382.8 1.2 fusion.389
  386.6 1.2 fusion.389
  394.4 1.2 fusion.389
  397.0 1.2 fusion.389
  398.3 1.2 fusion.389
  399.6 1.2 fusion.389
  400.9 1.2 fusion.389
  403.4 1.2 fusion.389
  408.6 1.2 fusion.389
  409.9 1.2 fusion.389
  421.5 1.2 fusion.389
  422.8 1.2 fusion.389
  424.1 1.2 fusion.389
  438.7 1.5 convolution_subtract_fusion.1
  443.0 1.4 broadcast_multiply_fusion.12
  446.5 1.3 convolution_bitcast_fusion.2
  447.9 64.1 %all-gather.13.cloned.1.call-done = f32[128,128,128]{2,1,0:T(8,128)} async-done(((f32[2,128,128]{2,1,0:T(8,128)}), f32[128,128,128]{2,1,0:T(8,128)}) %all-gather.13.cloned.1.call-update) | async-done | bytes 8388624 | tf_op jit(solution)/shard_map/all_gather | solution.py:22
  511.9 7.8 rev.6
  521.2 1.3 collective-permute-start.3
  523.1 1.6 fusion.86
  524.7 1.9 fusion.64
  527.7 138.8 %all-gather.15.cloned.1.call-done = f32[128,128,128]{2,1,0:T(8,128)} async-done(((f32[2,128,128]{2,1,0:T(8,128)}), f32[128,128,128]{2,1,0:T(8,128)}) %all-gather.15.cloned.1.call-update) | async-done | bytes 8388624 | tf_op jit(solution)/shard_map/all_gather | solution.py:22
  666.5 7.8 rev.7
  674.3 81.4 %while.68 = (s32[]{:T(128)}, f32[2,128,128]{2,1,0:T(8,128)S(1)}, s32[]{:T(128)}, f32[64,2,128,128]{3,2,1,0:T(8,128)}, f32[64,2,128,128]{3,2,1,0:T(8,128)}, /*index=5*/s32[]{:T(128)}, s32[]{:T(128)}) while((s32[]{:T(128)}, f32[2,128,128]{2,1,0:T(8,128)S(1)}, s32[]{:T(128)}, f32[64,2,128,128]{3,2,1,0:T(8,128)}, ...), condition=%wide.region_10.11_spmd.clone, body=%wide.region_9.10_spmd.clone.sunk | while | flops 50462724 | bytes 920159 | solution.py:34
  676.9 1.2 fusion.392
  685.9 1.2 fusion.392
  692.4 1.2 fusion.392
  695.0 1.2 fusion.392
  701.5 1.2 fusion.392
  710.5 1.2 fusion.392
  717.0 1.2 fusion.392
  756.8 6.4 while.65
  758.7 1.3 convolution_add_fusion.26
  762.0 1.3 convolution_add_fusion.26
  763.3 2.3 fusion.256
  765.7 1.4 convolution_add_fusion.9
  767.0 1.6 convolution_add_fusion.10
  770.1 1.3 convolution_add_fusion.21
  772.6 1.3 fusion.258
  779.2 1.3 convolution_add_fusion.19
  781.2 1.3 convolution_add_fusion.17
  783.3 1.3 convolution_add_fusion.15
  786.6 2.1 multiply_select_fusion
  798.0 1.4 fusion.53
  802.7 1.3 collective-permute-start.4
  804.0 1.3 collective-permute-start.5
  807.4 1.6 collective-permute-done.5
  810.7 1.9 fusion.44
  812.7 80.6 %all-reduce.19.cloned.1.call-done = bf16[128,2048]{1,0:T(8,128)(2,1)} async-done(((bf16[128,2048]{1,0:T(8,128)(2,1)}), bf16[128,2048]{1,0:T(8,128)(2,1)}) %all-reduce.19.cloned.1.call-update) | async-done | bytes 524304 | tf_op jit(solution)/shard_map/psum | solution.py:285
  893.2 1.5 convert_convert_fusion
  (498 shorter events, 191.4 us)
Async XLA Ops:
  6.5 20.2 %copy-start = (bf16[2048,256]{1,0:T(8,128)(2,1)S(1)}, bf16[2048,256]{1,0:T(8,128)(2,1)}, u32[]{:S(2)}) copy-start(bf16[2048,256]{1,0:T(8,128)(2,1)} %param.23) | copy-start | bytes 3145732
  6.5 195.6 %all-gather.9.cloned.1.call-start = ((), (), s32[]{:S(2)}) async-start(), calls=%async_computation.1 | async-start | bytes 8519680 | tf_op jit(solution)/shard_map/all_gather | solution.py:22
  30.6 8.7 copy-start.40
  31.6 7.7 copy-start.41
  31.6 7.8 collective-permute-start
  32.9 13.0 %collective-permute-start.1 = (bf16[3,256]{1,0:T(4,128)(2,1)S(1)}, bf16[3,256]{1,0:T(4,128)(2,1)S(1)}, u32[]{:S(2)}, u32[]{:S(2)}) collective-permute-start(bf16[3,256]{1,0:T(4,128)(2,1)S(1)} %slice.86), channel_id=1, source_target_pairs={{0,8},{8,16},{16,24},{24,32},{32,40},{40,48},{48,56},{56,64},{64,7... | collective-permute-start | bytes 4616 | tf_op jit(solution)/shard_map/ppermute | solution.py:17
  34.3 14.9 %copy-start.29 = (f32[128,128]{1,0:T(8,128)}, f32[128,128]{1,0:T(8,128)S(1)}, u32[]{:S(2)}) copy-start(f32[128,128]{1,0:T(8,128)S(1)} %fusion.201) | copy-start | bytes 196612
  35.1 9.0 copy-start.42
  35.1 9.0 copy-start.43
  35.1 9.0 copy-start.44
  35.1 9.0 copy-start.45
  35.8 3.5 copy-start.50
  38.1 11.1 %copy-start.37 = (f32[1,256]{1,0:T(1,128)}, f32[1,256]{1,0:T(1,128)S(1)}, u32[]{:S(2)}) copy-start(f32[1,256]{1,0:T(1,128)S(1)} %get-tuple-element.633) | copy-start | bytes 3076
  38.1 11.1 %copy-start.38 = (f32[1,256]{1,0:T(1,128)}, f32[1,256]{1,0:T(1,128)S(1)}, u32[]{:S(2)}) copy-start(f32[1,256]{1,0:T(1,128)S(1)} %get-tuple-element.635) | copy-start | bytes 3076
  39.6 1.7 copy-start.51
  39.6 7.7 copy-start.30
  39.6 6.3 copy-start.49
  40.5 4.6 copy-start.3
  40.6 3.0 copy-start.19
  41.0 6.2 copy-start.20
  41.4 5.9 copy-start.21
  41.4 13.6 %copy-start.48 = (bf16[4,128]{1,0:T(4,128)(2,1)S(1)}, bf16[4,128]{1,0:T(4,128)(2,1)}, u32[]{:S(2)}) copy-start(bf16[4,128]{1,0:T(4,128)(2,1)} %param.26) | copy-start | bytes 3076
  41.8 5.6 copy-start.22
  42.2 2.6 copy-start.14
  42.7 0.7 copy-start.25
  43.7 5.3 copy-start.23
  44.1 5.0 copy-start.24
  44.5 0.7 copy-start.15
  45.2 400.7 %copy-start.5 = (f32[2,2,64,128]{3,2,1,0:T(8,128)}, f32[2,2,64,128]{3,2,1,0:T(8,128)S(1)}, u32[]{:S(2)}) copy-start(f32[2,2,64,128]{3,2,1,0:T(8,128)S(1)} %fusion.71) | copy-start | bytes 393220
  47.4 309.6 %copy-start.10 = (f32[2,64,2,128]{3,2,1,0:T(2,128)}, f32[2,64,2,128]{3,2,1,0:T(2,128)S(1)}, u32[]{:S(2)}) copy-start(f32[2,64,2,128]{3,2,1,0:T(2,128)S(1)} %reshape.172) | copy-start | bytes 393220
  47.7 0.6 copy-start.8
  50.5 0.7 copy-start.1
  50.5 0.7 copy-start.2
  50.5 394.9 %copy-start.39 = (f32[2,2,64]{2,1,0:T(2,128)S(1)}, f32[2,2,64]{2,1,0:T(2,128)}, u32[]{:S(2)}) copy-start(f32[2,2,64]{2,1,0:T(2,128)} %get-tuple-element.628) | copy-start | bytes 3076
  51.1 305.8 %all-gather.11.cloned.1.call-start = ((), (), s32[]{:S(2)}) async-start(), calls=%async_computation.2 | async-start | bytes 8519680 | tf_op jit(solution)/shard_map/all_gather | solution.py:22
  51.9 460.0 %all-gather.13.cloned.1.call-start = ((), (), s32[]{:S(2)}) async-start(), calls=%async_computation.3 | async-start | bytes 8519680 | tf_op jit(solution)/shard_map/all_gather | solution.py:22
  52.0 5.1 collective-permute-start.2
  58.9 607.6 %all-gather.15.cloned.1.call-start = ((), (), s32[]{:S(2)}) async-start(), calls=%async_computation.4 | async-start | bytes 8519680 | tf_op jit(solution)/shard_map/all_gather | solution.py:22
  440.5 2.5 copy-start.16
  440.7 3.7 copy-start.33
  444.4 3.4 copy-start.12
  444.7 0.7 copy-start.32
  445.0 1.5 copy-start.26
  447.8 445.4 %all-reduce.19.cloned.1.call-start = ((), (), s32[]{:S(2)}) async-start(), calls=%async_computation | async-start | bytes 1048576 | tf_op jit(solution)/shard_map/psum | solution.py:285
  511.9 7.8 copy-start.46
  511.9 7.8 copy-start.47
  511.9 8.6 copy-start.31
  511.9 11.2 %copy-start.13 = (f32[128,128]{1,0:T(8,128)S(1)}, f32[128,128]{1,0:T(8,128)}, u32[]{:S(2)}) copy-start(f32[128,128]{1,0:T(8,128)} %copy-done.12) | copy-start | bytes 196612
  521.2 288.3 %collective-permute-start.3 = (f32[3,128]{1,0:T(4,128)}, f32[3,128]{1,0:T(4,128)}, u32[]{:S(2)}, u32[]{:S(2)}) collective-permute-start(f32[3,128]{1,0:T(4,128)} %pad_add_fusion.5), channel_id=1, source_target_pairs={{8,0},{16,8},{24,16},{32,24},{40,32},{48,40},{56,48},{64,56},{72,6... | collective-permute-start | bytes 4616 | tf_op jit(solution)/shard_map/ppermute | solution.py:17
  763.3 21.3 %copy-start.4 = (f32[2,2,64,64]{3,2,1,0:T(8,128)S(1)}, f32[2,2,64,64]{3,2,1,0:T(8,128)}, u32[]{:S(2)}) copy-start(f32[2,2,64,64]{3,2,1,0:T(8,128)} %copy-done.3) | copy-start | bytes 196612
  763.3 27.6 %copy-start.11 = (f32[2,64,2,128]{3,2,1,0:T(2,128)S(1)}, f32[2,64,2,128]{3,2,1,0:T(2,128)}, u32[]{:S(2)}) copy-start(f32[2,64,2,128]{3,2,1,0:T(2,128)} %copy-done.10) | copy-start | bytes 393220
  763.3 28.0 %copy-start.6 = (f32[2,2,64,128]{3,2,1,0:T(8,128)S(1)}, f32[2,2,64,128]{3,2,1,0:T(8,128)}, u32[]{:S(2)}) copy-start(f32[2,2,64,128]{3,2,1,0:T(8,128)} %copy-done.5) | copy-start | bytes 393220
  767.0 3.1 copy-start.27
  773.9 31.5 %copy-start.35 = (bf16[2048,2]{0,1:T(2,128)(2,1)S(1)}, bf16[2048,2]{0,1:T(2,128)(2,1)}, u32[]{:S(2)}) copy-start(bf16[2048,2]{0,1:T(2,128)(2,1)} %param.24) | copy-start | bytes 24580
  774.7 16.1 %copy-start.28 = (f32[2,2,64,128]{3,2,1,0:T(8,128)S(1)}, f32[2,2,64,128]{3,2,1,0:T(8,128)}, u32[]{:S(2)}) copy-start(f32[2,2,64,128]{3,2,1,0:T(8,128)} %copy-done.27) | copy-start | bytes 393220
  774.7 16.6 %copy-start.17 = (f32[2,2,64,128]{3,2,1,0:T(8,128)S(1)}, f32[2,2,64,128]{3,2,1,0:T(8,128)}, u32[]{:S(2)}) copy-start(f32[2,2,64,128]{3,2,1,0:T(8,128)} %fusion.257) | copy-start | bytes 393220
  774.7 16.6 %copy-start.34 = (f32[2,2,64,128]{3,2,1,0:T(8,128)S(1)}, f32[2,2,64,128]{3,2,1,0:T(8,128)}, u32[]{:S(2)}) copy-start(f32[2,2,64,128]{3,2,1,0:T(8,128)} %fusion.256) | copy-start | bytes 393220
  777.1 29.9 %copy-start.9 = (bf16[2048,128]{1,0:T(8,128)(2,1)S(1)}, bf16[2048,128]{1,0:T(8,128)(2,1)}, u32[]{:S(2)}) copy-start(bf16[2048,128]{1,0:T(8,128)(2,1)} %param.22) | copy-start | bytes 1572868
  779.1 18.8 %copy-start.18 = (f32[2,2,64,128]{3,2,1,0:T(8,128)S(1)}, f32[2,2,64,128]{3,2,1,0:T(8,128)}, u32[]{:S(2)}) copy-start(f32[2,2,64,128]{3,2,1,0:T(8,128)} %fusion.257) | copy-start | bytes 393220
  782.9 26.6 %copy-start.7 = (bf16[2048,128]{1,0:T(8,128)(2,1)S(1)}, bf16[2048,128]{1,0:T(8,128)(2,1)}, u32[]{:S(2)}) copy-start(bf16[2048,128]{1,0:T(8,128)(2,1)} %param.21) | copy-start | bytes 1572868
  789.9 20.8 %copy-start.36 = (bf16[2048,2]{0,1:T(2,128)(2,1)S(1)}, bf16[2048,2]{0,1:T(2,128)(2,1)}, u32[]{:S(2)}) copy-start(bf16[2048,2]{0,1:T(2,128)(2,1)} %param.25) | copy-start | bytes 24580
  802.7 4.3 collective-permute-start.4
  804.0 5.0 collective-permute-start.5
Sparse Core Ops, SparseCore 0:
  51.3 150.8 all-gather.8
  205.1 151.7 all-gather.10
  359.9 152.0 all-gather.12
  514.7 151.7 all-gather.14
  812.8 80.3 all-reduce.18
where the time goes:
time: 906 us; the launch traced here: 901 us
  waiting for transfers between devices  584 us (64%)
  matrix products  217 us (24%)
  local copies, waits for them, and re-layouts  26.3 us (3%)
  other arithmetic  24.2 us (3%)
  blocking collectives  20.2 us (2%)
  between operations  14.5 us (2%)
  starting transfers between devices  9.82 us (1%)
    all_gather x4, waiting for transfers between devices, entering(): pieces = jax.tree.map(lambda part: lax.all_gather(part, axis), value)  501 us
    dot_general x197, matrix products, contract(): jnp.einsum(form, left_arr, right_arr, precision=lax.Precision.HIGHEST, pr...  207 us
    psum x1, waiting for transfers between devices, local(): lax.psum(partial_value.astype(jnp.bfloat16), 'tp').astype(jnp.float32)  80.6 us
    all_gather x1, blocking collectives, local(): projected = add_rows(lax.all_gather(inputs, 'tp', axis=1, tiled=True))  20.2 us
  transfers between devices with their start and end apart: 11, of which 7 were waited for; matrix products, arithmetic and copies ran while one was open for 28% of the time, Pallas kernels for 0%

commit v1 on v0

v1 whole, which is shorter than its diff:
```python
import functools

import jax
import jax.numpy as jnp
from jax import lax
from jax.experimental import pallas as pl
from jax.experimental.pallas import tpu as pltpu
from jax.sharding import PartitionSpec as P

DH = 128
CONV = 4
EPS = 1e-06
SCALE = DH ** (-0.5)
RADIX = 4
PACK = 2 * DH + 16
F32 = jnp.float32
BF16 = jnp.bfloat16


def bf(value):
    return value.astype(BF16)


def dot(left, right, dims=(1, 0)):
    return lax.dot_general(
        bf(left), bf(right), (((dims[0],), (dims[1],)), ((), ())), preferred_element_type=F32
    )


def halves(value):
    high = bf(value)
    return high, bf(value - high.astype(F32))


def dot3(left, right, dims=(1, 0)):
    left_high, left_low = halves(left)
    right_high, right_low = halves(right)
    return dot(left_high, right_high, dims) + (
        dot(left_high, right_low, dims) + dot(left_low, right_high, dims)
    )


def dot_exact(left, right):
    return lax.dot_general(
        left, right, (((1,), (0,)), ((), ())),
        precision=lax.Precision.HIGHEST, preferred_element_type=F32,
    )


def positions(shape=(DH, DH)):
    return lax.broadcasted_iota(jnp.int32, shape, 0), lax.broadcasted_iota(jnp.int32, shape, 1)


def sigmoid(value):
    return 1.0 / (1.0 + jnp.exp(-value))


def softplus(value):
    return jnp.maximum(value, 0.0) + jnp.log1p(jnp.exp(-jnp.abs(value)))


def lanes_of(pieces):
    _, lane = positions()
    result = jnp.zeros((DH, DH), F32)
    for place, piece in enumerate(pieces):
        result = jnp.where(lane == place, piece, result)
    return result


def unit_lower_inverse(strict):
    row, col = positions()
    identity = jnp.where(row == col, 1.0, 0.0).astype(F32)
    inner = jnp.where(row // 8 == col // 8, strict, 0.0)
    square = dot3(inner, inner)
    result = dot3(identity - inner, identity + square)
    result = dot3(result, identity + dot3(square, square))
    size = 8
    while size < DH:
        off = (row // (2 * size) == col // (2 * size)) & (row // size != col // size)
        result = result - dot3(dot3(result, jnp.where(off, strict, 0.0)), result)
        size *= 2
    return result


def project_kernel(x_ref, wq_ref, wk_ref, wv_ref, wb_ref, wa_ref, proj_ref, ba_ref, tail_ref):
    parts = x_ref.shape[0]
    width = x_ref.shape[2]
    weights = (wq_ref, wk_ref, wv_ref, wb_ref, wa_ref)
    sums = [None] * 5
    for part in range(parts):
        rows = x_ref[part]
        for place, weight in enumerate(weights):
            piece = jnp.dot(
                rows, weight[part * width : (part + 1) * width, :], preferred_element_type=F32
            )
            sums[place] = piece if part == 0 else sums[place] + piece
    proj_ref[:, :DH] = bf(sums[0])
    proj_ref[:, DH : 2 * DH] = bf(sums[1])
    proj_ref[:, 2 * DH :] = bf(sums[2])
    tail_ref[:, :DH] = bf(sums[0][DH - 16 :])
    tail_ref[:, DH : 2 * DH] = bf(sums[1][DH - 16 :])
    tail_ref[:, 2 * DH :] = bf(sums[2][DH - 16 :])
    ba_ref[...] = bf(
        lanes_of([sums[3][:, 0:1], sums[3][:, 1:2], sums[4][:, 0:1], sums[4][:, 1:2]])
    )


def gate_rows(decay_ref, bias_ref):
    rate = lanes_of([0.0, 0.0, -jnp.exp(decay_ref[:, 0:1]), -jnp.exp(decay_ref[:, 1:2])])
    bias = lanes_of([0.0, 0.0, bias_ref[:, 0:1], bias_ref[:, 1:2]])
    return rate, bias


def split_decay(value):
    high = bf(value).astype(F32)
    middle = bf(value - high).astype(F32)
    low = value - high - middle
    row = lax.broadcasted_iota(jnp.int32, (16, DH), 0)
    return bf(jnp.where(row == 0, high, jnp.where(row == 1, middle, jnp.where(row == 2, low, 0.0))))


def slab_kernel(
    proj_ref, tail_ref, ba_ref, fq_ref, fk_ref, fv_ref, decay_ref, bias_ref, grad_ref,
    send_ref, pre_ref, unit_ref, cols_ref, inverse_ref, mixed_ref, weighted_ref,
    back_ref, gap_ref, gram_ref, cross_ref, pad_ref,
):
    row, col = positions()
    pad_ref[0:8] = tail_ref[8:16].astype(F32)
    pad_ref[8 : 8 + DH] = proj_ref[...].astype(F32)
    taps = jnp.concatenate(
        [fq_ref[...].astype(F32), fk_ref[...].astype(F32), fv_ref[...].astype(F32)], axis=1
    )
    pre = jnp.zeros((DH, 4 * DH), F32)
    for tap in range(CONV):
        start = 8 - (CONV - 1) + tap
        pre = pre + taps[tap : tap + 1] * pad_ref[start : start + DH]
    pre_ref[...] = pre
    act = pre * sigmoid(pre)
    query_act, key_act = act[:, :DH], act[:, DH : 2 * DH]
    query = query_act * (lax.rsqrt(jnp.sum(query_act * query_act, 1, keepdims=True) + EPS) * SCALE)
    key = key_act * lax.rsqrt(jnp.sum(key_act * key_act, 1, keepdims=True) + EPS)
    unit_ref[0] = query
    unit_ref[1] = key
    raw = ba_ref[...].astype(F32)
    rate, bias = gate_rows(decay_ref, bias_ref)
    log_decay = rate * softplus(raw + bias)
    lower = jnp.where(row >= col, 1.0, 0.0).astype(F32)
    summed = dot_exact(lower, log_decay)
    cols = jnp.where(col < 2, sigmoid(raw), summed)
    cols_ref[...] = cols
    rows = cols.T
    gram = dot3(key, key, (1, 1))
    cross = dot3(query, key, (1, 1))
    gram_ref[...] = gram
    cross_ref[...] = cross
    for head in range(2):
        beta = cols[:, head : head + 1]
        cum = cols[:, 2 + head : 3 + head]
        cum_row = rows[2 + head : 3 + head, :]
        value = act[:, (2 + head) * DH : (3 + head) * DH]
        grad = grad_ref[:, head * DH : (head + 1) * DH]
        gap = jnp.where(row >= col, jnp.exp(jnp.where(row >= col, cum - cum_row, 0.0)), 0.0)
        gap_ref[head] = gap
        gamma = jnp.exp(cum)
        last = cum[DH - 1 : DH, :]
        key_tail = jnp.exp(last - cum) * key
        strict = jnp.where(row > col, beta * gram * gap, 0.0)
        inverse = unit_lower_inverse(strict)
        mixed = dot3(inverse, beta * value)
        weighted = dot3(inverse, (beta * gamma) * key)
        back = dot(cross * gap, grad, (0, 0))
        inverse_ref[head] = bf(inverse)
        mixed_ref[head] = mixed
        weighted_ref[head] = bf(weighted)
        back_ref[head] = back
        moved = dot(key_tail, weighted, (0, 0))
        decay_rows = split_decay(jnp.exp(last))
        send_ref[2 * head, 0:DH] = bf(moved)
        send_ref[2 * head, DH : 2 * DH] = bf(dot(key_tail, mixed, (0, 0)))
        send_ref[2 * head, 2 * DH :] = decay_rows
        send_ref[2 * head + 1, 0:DH] = bf(moved.T)
        send_ref[2 * head + 1, DH : 2 * DH] = bf(
            dot(gamma * query, grad, (0, 0)) - dot(weighted, back, (0, 0))
        )
        send_ref[2 * head + 1, 2 * DH :] = decay_rows


def unpack(ref, place):
    decay = ref[place, 2 * DH :].astype(F32)
    return (
        decay[0:1, 0:1] + decay[1:2, 0:1] + decay[2:3, 0:1],
        ref[place, 0:DH],
        ref[place, DH : 2 * DH].astype(F32),
    )


def apply_map(later, state):
    decay, matrix, offset = later
    return decay * state - dot(matrix, state) + offset


def compose(later, earlier):
    decay, matrix, offset = later
    return (
        decay * earlier[0],
        decay * earlier[1] + earlier[0] * matrix.astype(F32) - dot(matrix, earlier[1]),
        apply_map(later, earlier[2]),
    )


def pack(ref, total):
    decay, matrix, offset = total
    packed = (bf(matrix), bf(offset), split_decay(decay))
    for place in range(RADIX):
        ref[place, 0:DH] = packed[0]
        ref[place, DH : 2 * DH] = packed[1]
        ref[place, 2 * DH :] = packed[2]


def widen(item):
    return item[0], item[1].astype(F32), item[2]


def in_order(step, backward):
    return jnp.where(backward, RADIX - 1 - step, step)


def group_kernel(got_ref, total_ref):
    backward = lax.axis_index("ctx") % 2 == 1
    total = widen(unpack(got_ref, in_order(0, backward)))
    for step in range(1, RADIX):
        total = compose(unpack(got_ref, in_order(step, backward)), total)
    pack(total_ref, total)


def row_kernel(got_ref, total_ref, before_ref):
    mine = lax.axis_index("ctx")
    backward = mine % 2 == 1
    place = in_order((mine // RADIX) % RADIX, backward)
    before_ref[0:DH] = jnp.zeros((DH, DH), F32)
    before_ref[DH : 2 * DH] = jnp.zeros((DH, DH), F32)
    before_ref[2 * DH :] = jnp.ones((8, DH), F32)
    total = widen(unpack(got_ref, in_order(0, backward)))
    for step in range(1, RADIX):

        @pl.when(place == step)
        def _(total=total):
            before_ref[0:DH] = total[1]
            before_ref[DH : 2 * DH] = total[2]
            before_ref[2 * DH :] = jnp.broadcast_to(total[0], (8, DH))

        total = compose(unpack(got_ref, in_order(step, backward)), total)
    pack(total_ref, total)


def states_kernel(rows_ref, before_ref, group_ref, out_ref):
    mine = lax.axis_index("ctx")
    backward = mine % 2 == 1
    place = in_order(mine // (RADIX * RADIX), backward)
    state = jnp.zeros((DH, DH), F32)
    for step in range(RADIX - 1):
        later = apply_map(unpack(rows_ref, in_order(step, backward)), state)
        state = jnp.where(step < place, later, state)
    before = (before_ref[2 * DH : 2 * DH + 1, 0:1], before_ref[0:DH], before_ref[DH : 2 * DH])
    state = apply_map(before, state)
    for step in range(RADIX):
        spot = in_order(step, backward)
        out_ref[spot] = bf(state)
        if step < RADIX - 1:
            state = apply_map(unpack(group_ref, spot), state)


def gradient_kernel(
    states_ref, pre_ref, unit_ref, cols_ref, ba_ref, inverse_ref, mixed_ref, weighted_ref,
    back_ref, gap_ref, gram_ref, cross_ref, grad_ref, fq_ref, fk_ref, fv_ref, decay_ref, bias_ref,
    full_ref, gates_ref, halo_ref, pad_ref,
):
    row, col = positions()
    cols = cols_ref[...]
    gram = gram_ref[...]
    cross = cross_ref[...]
    query = unit_ref[0]
    key = unit_ref[1]
    pre = pre_ref[...]
    gate = sigmoid(pre)
    act = pre * gate
    slope = gate * (1.0 + pre * (1.0 - gate))
    grad_query = jnp.zeros((DH, DH), F32)
    grad_key = jnp.zeros((DH, DH), F32)
    pieces = []
    columns = jnp.zeros((DH, DH), F32)
    sides = []
    for head in range(2):
        state = states_ref[2 * head]
        after = states_ref[2 * head + 1]
        beta = cols[:, head : head + 1]
        cum = cols[:, 2 + head : 3 + head]
        gamma = jnp.exp(cum)
        last = cum[DH - 1 : DH, :]
        rest = jnp.exp(last - cum)
        value = act[:, (2 + head) * DH : (3 + head) * DH]
        grad = grad_ref[:, head * DH : (head + 1) * DH]
        gap = gap_ref[head]
        fresh = mixed_ref[head] - dot(weighted_ref[head], state)
        grad_fresh = back_ref[head] + dot(rest * key, after)
        solved = dot(inverse_ref[head], grad_fresh, (0, 0))
        grad_strict = jnp.where(row > col, -dot(solved, fresh, (1, 1)), 0.0) * gap
        grad_cross = dot(grad, fresh, (1, 1)) * gap
        grad_weighted = -dot(solved, state, (1, 1))
        grad_scaled = dot(grad, state, (1, 1))
        grad_tail = dot(fresh, after, (1, 1))
        grad_query = grad_query + gamma * grad_scaled + dot(grad_cross, key)
        grad_gram = beta * grad_strict
        grad_key = grad_key + (
            dot(grad_cross, query, (0, 0))
            + dot(grad_gram, key)
            + dot(grad_gram, key, (0, 0))
            + (beta * gamma) * grad_weighted
            + rest * grad_tail
        )
        pieces.append(beta * solved)
        by_beta = jnp.sum(grad_strict * gram, 1, keepdims=True)
        by_key = gamma * jnp.sum(grad_weighted * key, 1, keepdims=True)
        grad_beta = jnp.sum(solved * value, 1, keepdims=True) + by_key + by_beta
        by_gap = grad_gram * gram + grad_cross * cross
        by_tail = rest * jnp.sum(grad_tail * key, 1, keepdims=True)
        at_end = jnp.sum(by_tail, 0, keepdims=True) + jnp.exp(last) * jnp.sum(
            jnp.sum(state.astype(F32) * after.astype(F32), 1, keepdims=True), 0, keepdims=True
        )
        grad_cum = (
            jnp.sum(by_gap, 1, keepdims=True)
            + gamma * jnp.sum(grad_scaled * query, 1, keepdims=True)
            + beta * by_key
            - by_tail
            + jnp.where(row[:, 0:1] == DH - 1, at_end, 0.0)
        )
        columns = jnp.where(row == 2 + head, jnp.sum(by_gap, 0, keepdims=True), columns)
        sides.append((grad_beta, grad_cum))
    raw = ba_ref[...].astype(F32)
    rate, bias = gate_rows(decay_ref, bias_ref)
    sides = lanes_of([sides[0][0], sides[1][0], sides[0][1], sides[1][1]]) - columns.T
    upper = jnp.where(row <= col, 1.0, 0.0).astype(F32)
    grad_log = dot_exact(upper, sides)
    beta = cols
    gates_ref[...] = bf(
        jnp.where(
            col < 2,
            sides * beta * (1.0 - beta),
            jnp.where(col < 4, grad_log * rate * sigmoid(raw + bias), 0.0),
        )
    )
    key_act = act[:, DH : 2 * DH]
    query_act = act[:, :DH]
    query_size = lax.rsqrt(jnp.sum(query_act * query_act, 1, keepdims=True) + EPS)
    key_size = lax.rsqrt(jnp.sum(key_act * key_act, 1, keepdims=True) + EPS)
    query_dir = query_act * query_size
    grad_query = grad_query * SCALE
    grad_query = query_size * (
        grad_query - query_dir * jnp.sum(grad_query * query_dir, 1, keepdims=True)
    )
    grad_key = key_size * (grad_key - key * jnp.sum(grad_key * key, 1, keepdims=True))
    pad_ref[0:8] = jnp.zeros((8, 4 * DH), F32)
    pad_ref[8 + DH :] = jnp.zeros((8, 4 * DH), F32)
    for place, piece in enumerate([grad_query, grad_key] + pieces):
        span = slice(place * DH, (place + 1) * DH)
        pad_ref[8 : 8 + DH, span] = piece * slope[:, span]
    taps = jnp.concatenate(
        [fq_ref[...].astype(F32), fk_ref[...].astype(F32), fv_ref[...].astype(F32)], axis=1
    )
    total = jnp.zeros((8 + DH, 4 * DH), F32)
    for tap in range(CONV):
        start = CONV - 1 - tap
        total = total + taps[tap : tap + 1] * pad_ref[start : start + 8 + DH]
    halo_ref[...] = total[0:8]
    full_ref[...] = total[8:]


def spread_kernel(full_ref, halo_ref, gates_ref, wq_ref, wk_ref, wv_ref, wb_ref, wa_ref, out_ref):
    full = full_ref[...]
    end = full[DH - 8 :] + halo_ref[...]
    grads = bf(jnp.concatenate([full[: DH - 8], end], axis=0))
    gates = gates_ref[...]
    width = out_ref.shape[2]
    for part in range(out_ref.shape[0]):
        span = slice(part * width, (part + 1) * width)
        total = dot(grads[:, :DH], wq_ref[span, :], (1, 1))
        total = total + dot(grads[:, DH : 2 * DH], wk_ref[span, :], (1, 1))
        total = total + dot(grads[:, 2 * DH :], wv_ref[span, :], (1, 1))
        total = total + dot(gates[:, 0:2], wb_ref[span, :], (1, 1))
        total = total + dot(gates[:, 2:4], wa_ref[span, :], (1, 1))
        out_ref[part] = bf(total)


def call(kernel, outs, scratch=()):
    return pl.pallas_call(
        kernel,
        out_shape=[jax.ShapeDtypeStruct(shape, kind) for shape, kind in outs],
        scratch_shapes=[pltpu.VMEM(shape, F32) for shape in scratch],
        compiler_params=pltpu.CompilerParams(vmem_limit_bytes=48 * 1024 * 1024),
    )


def project(gathered, weights):
    return call(
        project_kernel, [((DH, 4 * DH), BF16), ((DH, DH), BF16), ((16, 4 * DH), BF16)]
    )(gathered, *weights)


def slab(proj, tail, gates, filters, decay, bias, grad):
    square = (DH, DH)
    return call(
        slab_kernel,
        [
            ((4, PACK, DH), BF16), ((DH, 4 * DH), F32), ((2,) + square, F32), (square, F32),
            ((2,) + square, BF16), ((2,) + square, F32), ((2,) + square, BF16),
            ((2,) + square, F32), ((2,) + square, F32), (square, F32), (square, F32),
        ],
        [(8 + DH, 4 * DH)],
    )(proj, tail, gates, *filters, decay, bias, grad)


def gradient(states, kept, gates, filters, decay, bias, grad):
    pre, unit, cols, inverse, mixed, weighted, back, gap, gram, cross = kept
    return call(
        gradient_kernel,
        [((DH, 4 * DH), F32), ((DH, DH), BF16), ((8, 4 * DH), F32)],
        [(16 + DH, 4 * DH)],
    )(
        states, pre, unit, cols, gates, inverse, mixed, weighted, back, gap, gram, cross,
        grad, *filters, decay, bias,
    )


def spread(full, halo, gates, weights, parts):
    width = weights[0].shape[0] // parts
    return call(spread_kernel, [((parts, DH, width), BF16)])(full, halo, gates, *weights)[0]


def local(
    inputs, query_weight, key_weight, value_weight, beta_weight, alpha_weight,
    query_filter, key_filter, value_filter, decay_log, step_bias, grad_core,
):
    weights = (query_weight, key_weight, value_weight, beta_weight, alpha_weight)
    filters = (query_filter, key_filter, value_filter)
    decay = decay_log.reshape(1, 2)
    bias = step_bias.reshape(1, 2)
    count = lax.axis_size("ctx")
    parts = lax.axis_size("tp")
    slabs = range(count)
    group = [[s for s in slabs if s // RADIX == g] for g in range(count // RADIX)]
    row = [
        [s for s in slabs if s // 16 == y and s % RADIX == low]
        for y in range(count // 16) for low in range(RADIX)
    ]
    rank = [[s for s in slabs if s % 16 == z] for z in range(16)]

    def exchange(value, groups):
        return lax.all_to_all(value, "ctx", 0, 0, axis_index_groups=groups)

    gathered = lax.all_gather(inputs, "tp", axis=0)
    proj, gates, tail = project(gathered, weights)
    tail = lax.ppermute(tail, "ctx", [(s, s + 1) for s in range(count - 1)])
    send, *kept = slab(proj, tail, gates, filters, decay, bias, grad_core)
    got = exchange(send, group)
    total = call(group_kernel, [((RADIX, PACK, DH), BF16)])(got)[0]
    total, before = call(
        row_kernel, [((RADIX, PACK, DH), BF16), ((2 * DH + 8, DH), F32)]
    )(exchange(total, row))
    states = call(states_kernel, [((RADIX, DH, DH), BF16)])(exchange(total, rank), before, got)[0]
    states = exchange(states, group)
    full, grad_gates, halo = gradient(states, kept, gates, filters, decay, bias, grad_core)
    halo = lax.ppermute(halo, "ctx", [(s + 1, s) for s in range(count - 1)])
    shares = spread(full, halo, grad_gates, weights, parts)
    shares = lax.all_to_all(shares, "tp", 0, 0)
    return jnp.sum(shares.astype(F32), axis=0).astype(BF16)


def solution(mesh):
    sharded = P("ctx", "tp")
    kept = P(None, "tp")
    return jax.shard_map(
        local,
        mesh=mesh,
        in_specs=(sharded,) + (kept,) * 8 + (P("tp"), P("tp"), sharded),
        out_specs=sharded,
        check_vma=False,
    )
```

time: 906 us -> 120 us (0.13)
  waiting for transfers between devices: 584 us -> 4.03 us
  matrix products: 217 us -> 0 us
  blocking collectives: 20.2 us -> 98.8 us
  other arithmetic: 24.2 us -> 0.7 us
  local copies, waits for them, and re-layouts: 26.3 us -> 3.15 us
  between operations: 14.5 us -> 0.11 us
  Pallas kernels: 0 us -> 10.2 us
    all_gather x4 -> x0, waiting for transfers between devices: 501 us -> none  [entering(): pieces = jax.tree.map(lambda part: lax.all_gather(part, axis), value)]
    dot_general x207 -> x0, matrix products: 217 us -> none  [the longest x197 207 us: contract(): jnp.einsum(form, left_arr, right_arr, precision=lax.Precision.HIGHEST, pr...]
    psum x1 -> x0, waiting for transfers between devices: 80.6 us -> none  [local(): lax.psum(partial_value.astype(jnp.bfloat16), 'tp').astype(jnp.float32)]
    all_to_all x0 -> x5, blocking collectives: none -> 78.7 us  [the longest x4 56.8 us: exchange(): return lax.all_to_all(value, 'ctx', 0, 0, axis_index_groups=groups)]
    rev x2 -> x0, local copies, waits for them, and re-layouts: 15.6 us -> none  [entering(): pieces = jax.tree.map(lambda part: part[::-1], pieces)]
    mul x16 -> x0, other arithmetic: 10.6 us -> none  [the longest x9 8.32 us: conv_silu(): weight[tap_index].astype(jnp.float32) * padded[tap_index:tap_index + length]]
    pallas_call x0 -> x7, Pallas kernels: none -> 10.2 us  [the longest x1 4.75 us: slab(): call(slab_kernel, [((4, PACK, DH), BF16), ((DH, 4 * DH), F32), ((2,) + sq...]
  transfers between devices with their start and end apart: 11 -> 2, of which waited for: 7 -> 2; matrix products, arithmetic and copies ran while one was open for 28% -> 0% of each run, Pallas kernels for 0% -> 0%
where the time goes in v1:
time: 120 us
  blocking collectives  98.8 us (82%)
  Pallas kernels  10.2 us (8%)
  waiting for transfers between devices  4.03 us (3%)
  local copies, waits for them, and re-layouts  3.15 us (3%)
  starting transfers between devices  2.58 us (2%)
    all_to_all x4, blocking collectives, exchange(): return lax.all_to_all(value, 'ctx', 0, 0, axis_index_groups=groups)  56.8 us
    all_to_all x1, blocking collectives, local(): shares = lax.all_to_all(shares, 'tp', 0, 0)  22 us
    all_gather x1, blocking collectives, local(): gathered = lax.all_gather(inputs, 'tp', axis=0)  20 us
    pallas_call x1, Pallas kernels, slab(): call(slab_kernel, [((4, PACK, DH), BF16), ((DH, 4 * DH), F32), ((2,) + sq...  4.75 us
    ppermute x1, waiting for transfers between devices, local(): halo = lax.ppermute(halo, 'ctx', [(s + 1, s) for s in range(count - 1)])  3.18 us
    unnamed x24, local copies, waits for them, and re-layouts  3.15 us
  transfers between devices with their start and end apart: 2, of which 2 were waited for; matrix products, arithmetic and copies ran while one was open for 0% of the time, Pallas kernels for 0%

profile of v1, /device:TPU:1, one launch (start us, length us, event | category | flops | bytes accessed | tf_op | source)
XLA Modules:
  0.0 119.5 jit_solution(31733897347879392)
XLA Ops:
  0.0 0.0 copy-start.10
  0.0 0.0 copy-start
  0.0 1.1 copy.13.wb_ref
  1.1 0.0 copy-done.10
  1.1 0.0 copy-start.1
  1.1 0.3 copy.14.wa_ref
  1.4 20.0 %all-gather = bf16[1024,256]{1,0:T(8,128)(2,1)S(1)} all-gather(bf16[128,256]{1,0:T(8,128)(2,1)} %param.12), channel_id=2, replica_groups=mesh['ctx'=64,'tp'=8] {'tp'}, dimensions={0}, use_global_device_ids=true | all-gather | bytes 589824 | tf_op jit(solution)/shard_map/all_gather | solution.py:460
  21.5 0.0 copy-done
  21.5 0.0 copy-done.1
  21.5 0.0 copy-start.2
  21.5 1.0 copy-done.2
  22.5 0.0 copy-start.4
  22.5 0.0 copy-start.7
  22.5 0.0 copy-start.9
  22.5 0.9 shard_map.118
  23.4 1.3 %collective-permute-start = (bf16[16,512]{1,0:T(8,128)(2,1)S(1)}, bf16[16,512]{1,0:T(8,128)(2,1)S(1)}, u32[]{:S(2)}, u32[]{:S(2)}) collective-permute-start(bf16[16,512]{1,0:T(8,128)(2,1)S(1)} %get-tuple-element.25), channel_id=1, source_target_pairs={{0,8},{8,16},{16,24},{24,32},{32,40},{40,48},{48,56},{56,64},{64,7... | collective-permute-start | bytes 49160 | tf_op jit(solution)/shard_map/ppermute | solution.py:462
  24.7 0.9 collective-permute-done.tail_ref
  25.6 0.0 copy-start.5
  25.6 0.0 copy-start.6
  25.6 0.0 copy-start.8
  25.6 0.0 copy-done.4
  25.6 0.0 copy-done.7
  25.6 0.0 copy-done.9
  25.6 0.7 copy-done.5
  26.3 0.0 copy-done.6
  26.3 0.0 copy-done.8
  26.3 4.7 %shard_map.119 = (bf16[4,272,128]{2,1,0:T(8,128)(2,1)S(1)}, f32[128,512]{1,0:T(8,128)S(1)}, f32[2,128,128]{2,1,0:T(8,128)S(1)}, f32[128,128]{1,0:T(8,128)S(1)}, ...) custom-call(bf16[128,512]{1,0:T(8,128)(2,1)S(1)} %get-tuple-element., ...), custom_call_target="tpu_custom_call" | custom-call | tf_op jit(solution)/shard_map/pallas_call | solution.py:411
  31.0 11.1 %all_to_all.25.got_ref.group_ref = bf16[4,272,128]{2,1,0:T(8,128)(2,1)S(1)} all-to-all(bf16[4,272,128]{2,1,0:T(8,128)(2,1)S(1)} %get-tuple-element.27), channel_id=1, replica_groups={{0,8,16,24},{32,40,48,56},{64,72,80,88},{96,104,112,120},{128,136,144,1..., dimensions={0} | all-to-all | bytes 557056 | tf_op jit(solution)/shard_map/all_to_all | solution.py:458
  42.1 0.4 shard_map.120
  42.6 27.3 %all_to_all.26.got_ref = bf16[4,272,128]{2,1,0:T(8,128)(2,1)S(1)} all-to-all(bf16[4,272,128]{2,1,0:T(8,128)(2,1)S(1)} %shard_map.120), channel_id=1, replica_groups={{0,32,64,96},{8,40,72,104},{16,48,80,112},{24,56,88,120},{128,160,192,2..., dimensions={0} | all-to-all | bytes 557056 | tf_op jit(solution)/shard_map/all_to_all | solution.py:458
  69.9 0.5 shard_map.121
  70.3 9.6 %all_to_all.27.rows_ref = bf16[4,272,128]{2,1,0:T(8,128)(2,1)S(1)} all-to-all(bf16[4,272,128]{2,1,0:T(8,128)(2,1)S(1)} %get-tuple-element.28), channel_id=1, replica_groups={{0,128,256,384},{8,136,264,392},{16,144,272,400},{24,152,280,408},{32,1..., dimensions={0} | all-to-all | bytes 557056 | tf_op jit(solution)/shard_map/all_to_all | solution.py:458
  79.9 0.9 shard_map.122
  80.9 8.8 %all_to_all.28.states_ref = bf16[4,128,128]{2,1,0:T(8,128)(2,1)S(1)} all-to-all(bf16[4,128,128]{2,1,0:T(8,128)(2,1)S(1)} %shard_map.122), channel_id=1, replica_groups={{0,8,16,24},{32,40,48,56},{64,72,80,88},{96,104,112,120},{128,136,144,1..., dimensions={0} | all-to-all | bytes 262144 | tf_op jit(solution)/shard_map/all_to_all | solution.py:458
  89.7 0.0 copy-start.3
  89.7 1.6 %shard_map.123 = (f32[128,512]{1,0:T(8,128)S(1)}, bf16[128,128]{1,0:T(8,128)(2,1)S(1)}, f32[8,512]{1,0:T(8,128)S(1)}) custom-call(bf16[4,128,128]{2,1,0:T(8,128)(2,1)S(1)} %all_to_all.28.states_ref, f32[128,512]{1,0:T(8,128)S(1)} %get-tuple-element.30.pre_ref, f32[2,128,128]{2,1,0:T(8,128)S(1)} %get-tuple-element.31.unit_ref, ...), custom_call_target="tpu_custom_call" | custom-call | tf_op jit(solution)/shard_map/pallas_call | solution.py:424
  91.3 1.3 %collective-permute-start.1 = (f32[8,512]{1,0:T(8,128)S(1)}, f32[8,512]{1,0:T(8,128)S(1)}, u32[]{:S(2)}, u32[]{:S(2)}) collective-permute-start(f32[8,512]{1,0:T(8,128)S(1)} %get-tuple-element.41), channel_id=1, source_target_pairs={{8,0},{16,8},{24,16},{32,24},{40,32},{48,40},{56,48},{64,56},{72,6... | collective-permute-start | bytes 49160 | tf_op jit(solution)/shard_map/ppermute | solution.py:472
  92.6 3.2 %collective-permute-done.1.halo_ref = f32[8,512]{1,0:T(8,128)S(1)} collective-permute-done((f32[8,512]{1,0:T(8,128)S(1)}, f32[8,512]{1,0:T(8,128)S(1)}, u32[]{:S(2)}, u32[]{:S(2)}) %collective-permute-start.1) | collective-permute-done | bytes 16416 | tf_op jit(solution)/shard_map/ppermute | solution.py:472
  95.8 0.0 copy-done.3
  95.8 1.1 shard_map.124
  96.9 22.0 %all_to_all.29 = bf16[8,128,256]{2,1,0:T(8,128)(2,1)S(1)} all-to-all(bf16[8,128,256]{2,1,0:T(8,128)(2,1)S(1)} %shard_map.124), channel_id=1, replica_groups=mesh['ctx'=64,'tp'=8] {'tp'}, dimensions={0} | all-to-all | bytes 1048576 | tf_op jit(solution)/shard_map/all_to_all | solution.py:474
  118.8 0.7 reduce_sum.12
Async XLA Ops:
  0.0 1.1 copy-start.10
  0.0 21.5 %copy-start = (bf16[2048,256]{1,0:T(8,128)(2,1)S(1)}, bf16[2048,256]{1,0:T(8,128)(2,1)}, u32[]{:S(2)}) copy-start(bf16[2048,256]{1,0:T(8,128)(2,1)} %wv_ref.3) | copy-start | bytes 3145732
  1.1 20.4 %copy-start.1 = (bf16[2048,128]{1,0:T(8,128)(2,1)S(1)}, bf16[2048,128]{1,0:T(8,128)(2,1)}, u32[]{:S(2)}) copy-start(bf16[2048,128]{1,0:T(8,128)(2,1)} %wq_ref.3) | copy-start | bytes 1572868
  21.5 1.0 copy-start.2
  22.5 3.1 %copy-start.4 = (bf16[128,256]{1,0:T(8,128)(2,1)S(1)}, bf16[128,256]{1,0:T(8,128)(2,1)}, u32[]{:S(2)}) copy-start(bf16[128,256]{1,0:T(8,128)(2,1)} %grad_ref.3) | copy-start | bytes 196612
  22.5 3.1 %copy-start.7 = (bf16[4,128]{1,0:T(4,128)(2,1)S(1)}, bf16[4,128]{1,0:T(4,128)(2,1)}, u32[]{:S(2)}) copy-start(bf16[4,128]{1,0:T(4,128)(2,1)} %fk_ref.3) | copy-start | bytes 3076
  22.5 3.1 %copy-start.9 = (f32[2]{0:T(128)S(1)}, f32[2]{0:T(128)}, u32[]{:S(2)}) copy-start(f32[2]{0:T(128)} %param.22) | copy-start | bytes 28
  23.4 2.1 %collective-permute-start = (bf16[16,512]{1,0:T(8,128)(2,1)S(1)}, bf16[16,512]{1,0:T(8,128)(2,1)S(1)}, u32[]{:S(2)}, u32[]{:S(2)}) collective-permute-start(bf16[16,512]{1,0:T(8,128)(2,1)S(1)} %get-tuple-element.25), channel_id=1, source_target_pairs={{0,8},{8,16},{16,24},{24,32},{32,40},{40,48},{48,56},{56,64},{64,7... | collective-permute-start | bytes 49160 | tf_op jit(solution)/shard_map/ppermute | solution.py:462
  25.6 0.7 copy-start.5
  25.6 0.7 copy-start.6
  25.6 0.7 copy-start.8
  89.7 6.1 %copy-start.3 = (bf16[2048,128]{1,0:T(8,128)(2,1)S(1)}, bf16[2048,128]{1,0:T(8,128)(2,1)}, u32[]{:S(2)}) copy-start(bf16[2048,128]{1,0:T(8,128)(2,1)} %wk_ref.3) | copy-start | bytes 1572868
  91.3 4.5 %collective-permute-start.1 = (f32[8,512]{1,0:T(8,128)S(1)}, f32[8,512]{1,0:T(8,128)S(1)}, u32[]{:S(2)}, u32[]{:S(2)}) collective-permute-start(f32[8,512]{1,0:T(8,128)S(1)} %get-tuple-element.41), channel_id=1, source_target_pairs={{8,0},{16,8},{24,16},{32,24},{40,32},{48,40},{56,48},{64,56},{72,6... | collective-permute-start | bytes 49160 | tf_op jit(solution)/shard_map/ppermute | solution.py:472

commit v2 on v1

--- a/solution.py
+++ b/solution.py
@@ -11,7 +11,6 @@
 CONV = 4
 EPS = 1e-06
 SCALE = DH ** (-0.5)
-RADIX = 4
 PACK = 2 * DH + 16
 F32 = jnp.float32
 BF16 = jnp.bfloat16
@@ -85,15 +84,14 @@
 def project_kernel(x_ref, wq_ref, wk_ref, wv_ref, wb_ref, wa_ref, proj_ref, ba_ref, tail_ref):
     parts = x_ref.shape[0]
     width = x_ref.shape[2]
-    weights = (wq_ref, wk_ref, wv_ref, wb_ref, wa_ref)
-    sums = [None] * 5
+    sums = [0.0] * 5
     for part in range(parts):
         rows = x_ref[part]
-        for place, weight in enumerate(weights):
-            piece = jnp.dot(
-                rows, weight[part * width : (part + 1) * width, :], preferred_element_type=F32
-            )
-            sums[place] = piece if part == 0 else sums[place] + piece
+        span = slice(part * width, (part + 1) * width)
+        for place, weight in enumerate((wq_ref, wk_ref, wv_ref)):
+            sums[place] = sums[place] + dot(rows, weight[span, :])
+        for place, weight in enumerate((wb_ref, wa_ref), 3):
+            sums[place] = sums[place] + dot(rows, weight[:, span], (1, 1))
     proj_ref[:, :DH] = bf(sums[0])
     proj_ref[:, DH : 2 * DH] = bf(sums[1])
     proj_ref[:, 2 * DH :] = bf(sums[2])
@@ -121,8 +119,8 @@
 
 def slab_kernel(
     proj_ref, tail_ref, ba_ref, fq_ref, fk_ref, fv_ref, decay_ref, bias_ref, grad_ref,
-    send_ref, pre_ref, unit_ref, cols_ref, inverse_ref, mixed_ref, weighted_ref,
-    back_ref, gap_ref, gram_ref, cross_ref, pad_ref,
+    own_ref, send_ref, pre_ref, unit_ref, cols_ref, inverse_ref, mixed_ref, weighted_ref,
+    back_ref, gap_ref, gram_ref, cross_ref, pad_ref, maps_ref,
 ):
     row, col = positions()
     pad_ref[0:8] = tail_ref[8:16].astype(F32)
@@ -173,25 +171,31 @@
         mixed_ref[head] = mixed
         weighted_ref[head] = bf(weighted)
         back_ref[head] = back
-        moved = dot(key_tail, weighted, (0, 0))
-        decay_rows = split_decay(jnp.exp(last))
-        send_ref[2 * head, 0:DH] = bf(moved)
-        send_ref[2 * head, DH : 2 * DH] = bf(dot(key_tail, mixed, (0, 0)))
-        send_ref[2 * head, 2 * DH :] = decay_rows
-        send_ref[2 * head + 1, 0:DH] = bf(moved.T)
-        send_ref[2 * head + 1, DH : 2 * DH] = bf(
+        maps_ref[head, 0:DH] = bf(dot(key_tail, weighted, (0, 0)))
+        maps_ref[head, DH : 2 * DH] = bf(dot(key_tail, mixed, (0, 0)))
+        maps_ref[head, 2 * DH : 3 * DH] = bf(
             dot(gamma * query, grad, (0, 0)) - dot(weighted, back, (0, 0))
         )
-        send_ref[2 * head + 1, 2 * DH :] = decay_rows
-
-
-def unpack(ref, place):
-    decay = ref[place, 2 * DH :].astype(F32)
+        maps_ref[head, 3 * DH :] = split_decay(jnp.exp(last))
+    mine = bit(0)
+    own_ref[...] = maps_ref[mine]
+    send_ref[...] = maps_ref[1 - mine]
+
+
+def unpack(ref):
+    decay = ref[2 * DH :].astype(F32)
     return (
         decay[0:1, 0:1] + decay[1:2, 0:1] + decay[2:3, 0:1],
-        ref[place, 0:DH],
-        ref[place, DH : 2 * DH].astype(F32),
-    )
+        ref[0:DH].astype(F32),
+        ref[DH : 2 * DH].astype(F32),
+    )
+
+
+def pack(ref, total):
+    decay, matrix, offset = total
+    ref[0:DH] = bf(matrix)
+    ref[DH : 2 * DH] = bf(offset)
+    ref[2 * DH :] = split_decay(decay)
 
 
 def apply_map(later, state):
@@ -203,75 +207,80 @@
     decay, matrix, offset = later
     return (
         decay * earlier[0],
-        decay * earlier[1] + earlier[0] * matrix.astype(F32) - dot(matrix, earlier[1]),
+        decay * earlier[1] + earlier[0] * matrix - dot(matrix, earlier[1]),
         apply_map(later, earlier[2]),
     )
 
 
-def pack(ref, total):
-    decay, matrix, offset = total
-    packed = (bf(matrix), bf(offset), split_decay(decay))
-    for place in range(RADIX):
-        ref[place, 0:DH] = packed[0]
-        ref[place, DH : 2 * DH] = packed[1]
-        ref[place, 2 * DH :] = packed[2]
-
-
-def widen(item):
-    return item[0], item[1].astype(F32), item[2]
-
-
-def in_order(step, backward):
-    return jnp.where(backward, RADIX - 1 - step, step)
-
-
-def group_kernel(got_ref, total_ref):
-    backward = lax.axis_index("ctx") % 2 == 1
-    total = widen(unpack(got_ref, in_order(0, backward)))
-    for step in range(1, RADIX):
-        total = compose(unpack(got_ref, in_order(step, backward)), total)
-    pack(total_ref, total)
-
-
-def row_kernel(got_ref, total_ref, before_ref):
-    mine = lax.axis_index("ctx")
-    backward = mine % 2 == 1
-    place = in_order((mine // RADIX) % RADIX, backward)
-    before_ref[0:DH] = jnp.zeros((DH, DH), F32)
-    before_ref[DH : 2 * DH] = jnp.zeros((DH, DH), F32)
-    before_ref[2 * DH :] = jnp.ones((8, DH), F32)
-    total = widen(unpack(got_ref, in_order(0, backward)))
-    for step in range(1, RADIX):
-
-        @pl.when(place == step)
-        def _(total=total):
-            before_ref[0:DH] = total[1]
-            before_ref[DH : 2 * DH] = total[2]
-            before_ref[2 * DH :] = jnp.broadcast_to(total[0], (8, DH))
-
-        total = compose(unpack(got_ref, in_order(step, backward)), total)
-    pack(total_ref, total)
-
-
-def states_kernel(rows_ref, before_ref, group_ref, out_ref):
-    mine = lax.axis_index("ctx")
-    backward = mine % 2 == 1
-    place = in_order(mine // (RADIX * RADIX), backward)
-    state = jnp.zeros((DH, DH), F32)
-    for step in range(RADIX - 1):
-        later = apply_map(unpack(rows_ref, in_order(step, backward)), state)
-        state = jnp.where(step < place, later, state)
-    before = (before_ref[2 * DH : 2 * DH + 1, 0:1], before_ref[0:DH], before_ref[DH : 2 * DH])
-    state = apply_map(before, state)
-    for step in range(RADIX):
-        spot = in_order(step, backward)
-        out_ref[spot] = bf(state)
-        if step < RADIX - 1:
-            state = apply_map(unpack(group_ref, spot), state)
+def bit(place):
+    return (lax.axis_index("ctx") >> place) & 1
+
+
+def pair_maps(own_ref, got_ref):
+    second = bit(0) == 1
+    maps = []
+    for flip in (second, jnp.logical_not(second)):
+        parts = jnp.where(flip, got_ref[...].astype(F32), own_ref[...].astype(F32))
+        decay = parts[3 * DH : 3 * DH + 1, 0:1] + parts[3 * DH + 1 : 3 * DH + 2, 0:1]
+        decay = decay + parts[3 * DH + 2 : 3 * DH + 3, 0:1]
+        maps.append((decay, parts[0:DH], parts[DH : 2 * DH], parts[2 * DH : 3 * DH]))
+    return maps
+
+
+def pair_kernel(own_ref, got_ref, send_ref, keep_ref):
+    first, second = pair_maps(own_ref, got_ref)
+    decay, matrix, offset = compose(second[:3], first[:3])
+    adjoint = first[0] * second[3] - dot(first[1], second[3], (0, 0)) + first[3]
+    turned = matrix.T
+    backward = bit(1) == 1
+    pack(send_ref, (decay, jnp.where(backward, matrix, turned), jnp.where(backward, offset, adjoint)))
+    pack(keep_ref, (decay, jnp.where(backward, turned, matrix), jnp.where(backward, adjoint, offset)))
+
+
+def group_kernel(keep_ref, got_ref, total_ref):
+    pack(total_ref, compose(unpack(got_ref), unpack(keep_ref)))
+
+
+def first_window_kernel(total_ref, got_ref, wider_ref):
+    pack(wider_ref, compose(unpack(total_ref), unpack(got_ref)))
+
+
+def window_kernel(total_ref, before_ref, got_ref, wider_ref, past_ref):
+    got = unpack(got_ref)
+    pack(wider_ref, compose(unpack(total_ref), got))
+    pack(past_ref, compose(unpack(before_ref), got))
+
+
+def last_window_kernel(total_ref, before_ref, got_ref, wider_ref, past_ref):
+    got = unpack(got_ref)
+    wider_ref[...] = bf(apply_map(unpack(total_ref), got[2]))
+    pack(past_ref, compose(unpack(before_ref), got))
+
+
+def start_kernel(past_ref, got_ref, keep_ref, mine_ref, send_ref):
+    state = apply_map(unpack(past_ref), got_ref[...].astype(F32))
+    mine_ref[...] = bf(state)
+    send_ref[...] = bf(apply_map(unpack(keep_ref), state))
+
+
+def states_kernel(mine_ref, got_ref, own_ref, partner_ref, here_ref, send_ref):
+    first, second = pair_maps(own_ref, partner_ref)
+    backward = bit(1) == 1
+    mine = mine_ref[...].astype(F32)
+    got = got_ref[...].astype(F32)
+    state = jnp.where(backward, got, mine)
+    after = jnp.where(backward, mine, got)
+    later_state = apply_map(first[:3], state)
+    earlier_after = second[0] * after - dot(second[1], after, (0, 0)) + second[3]
+    odd = bit(0) == 1
+    here_ref[0] = bf(jnp.where(odd, later_state, state))
+    here_ref[1] = bf(jnp.where(odd, after, earlier_after))
+    send_ref[0] = bf(jnp.where(odd, state, later_state))
+    send_ref[1] = bf(jnp.where(odd, earlier_after, after))
 
 
 def gradient_kernel(
-    states_ref, pre_ref, unit_ref, cols_ref, ba_ref, inverse_ref, mixed_ref, weighted_ref,
+    here_ref, there_ref, pre_ref, unit_ref, cols_ref, ba_ref, inverse_ref, mixed_ref, weighted_ref,
     back_ref, gap_ref, gram_ref, cross_ref, grad_ref, fq_ref, fk_ref, fv_ref, decay_ref, bias_ref,
     full_ref, gates_ref, halo_ref, pad_ref,
 ):
@@ -291,8 +300,9 @@
     columns = jnp.zeros((DH, DH), F32)
     sides = []
     for head in range(2):
-        state = states_ref[2 * head]
-        after = states_ref[2 * head + 1]
+        held = bit(0) == head
+        state = jnp.where(held, here_ref[0], there_ref[0])
+        after = jnp.where(held, here_ref[1], there_ref[1])
         beta = cols[:, head : head + 1]
         cum = cols[:, 2 + head : 3 + head]
         gamma = jnp.exp(cum)
@@ -386,8 +396,8 @@
         total = dot(grads[:, :DH], wq_ref[span, :], (1, 1))
         total = total + dot(grads[:, DH : 2 * DH], wk_ref[span, :], (1, 1))
         total = total + dot(grads[:, 2 * DH :], wv_ref[span, :], (1, 1))
-        total = total + dot(gates[:, 0:2], wb_ref[span, :], (1, 1))
-        total = total + dot(gates[:, 2:4], wa_ref[span, :], (1, 1))
+        total = total + dot(gates[:, 0:2], wb_ref[:, span])
+        total = total + dot(gates[:, 2:4], wa_ref[:, span])
         out_ref[part] = bf(total)
 
 
@@ -395,7 +405,7 @@
     return pl.pallas_call(
         kernel,
         out_shape=[jax.ShapeDtypeStruct(shape, kind) for shape, kind in outs],
-        scratch_shapes=[pltpu.VMEM(shape, F32) for shape in scratch],
+        scratch_shapes=[pltpu.VMEM(shape, kind) for shape, kind in scratch],
         compiler_params=pltpu.CompilerParams(vmem_limit_bytes=48 * 1024 * 1024),
     )
 
@@ -411,22 +421,23 @@
     return call(
         slab_kernel,
         [
-            ((4, PACK, DH), BF16), ((DH, 4 * DH), F32), ((2,) + square, F32), (square, F32),
+            ((PACK + DH, DH), BF16), ((PACK + DH, DH), BF16),
+            ((DH, 4 * DH), F32), ((2,) + square, F32), (square, F32),
             ((2,) + square, BF16), ((2,) + square, F32), ((2,) + square, BF16),
             ((2,) + square, F32), ((2,) + square, F32), (square, F32), (square, F32),
         ],
-        [(8 + DH, 4 * DH)],
+        [((8 + DH, 4 * DH), F32), ((2, PACK + DH, DH), BF16)],
     )(proj, tail, gates, *filters, decay, bias, grad)
 
 
-def gradient(states, kept, gates, filters, decay, bias, grad):
+def gradient(here, there, kept, gates, filters, decay, bias, grad):
     pre, unit, cols, inverse, mixed, weighted, back, gap, gram, cross = kept
     return call(
         gradient_kernel,
         [((DH, 4 * DH), F32), ((DH, DH), BF16), ((8, 4 * DH), F32)],
-        [(16 + DH, 4 * DH)],
+        [((16 + DH, 4 * DH), F32)],
     )(
-        states, pre, unit, cols, gates, inverse, mixed, weighted, back, gap, gram, cross,
+        here, there, pre, unit, cols, gates, inverse, mixed, weighted, back, gap, gram, cross,
         grad, *filters, decay, bias,
     )
 
@@ -440,35 +451,37 @@
     inputs, query_weight, key_weight, value_weight, beta_weight, alpha_weight,
     query_filter, key_filter, value_filter, decay_log, step_bias, grad_core,
 ):
-    weights = (query_weight, key_weight, value_weight, beta_weight, alpha_weight)
+    weights = (query_weight, key_weight, value_weight, beta_weight.T, alpha_weight.T)
     filters = (query_filter, key_filter, value_filter)
     decay = decay_log.reshape(1, 2)
     bias = step_bias.reshape(1, 2)
     count = lax.axis_size("ctx")
     parts = lax.axis_size("tp")
-    slabs = range(count)
-    group = [[s for s in slabs if s // RADIX == g] for g in range(count // RADIX)]
-    row = [
-        [s for s in slabs if s // 16 == y and s % RADIX == low]
-        for y in range(count // 16) for low in range(RADIX)
-    ]
-    rank = [[s for s in slabs if s % 16 == z] for z in range(16)]
-
-    def exchange(value, groups):
-        return lax.all_to_all(value, "ctx", 0, 0, axis_index_groups=groups)
+    packed = ((PACK, DH), BF16)
+    square = ((DH, DH), BF16)
+
+    def swap(value, distance):
+        return lax.ppermute(value, "ctx", [(s, s ^ distance) for s in range(count)])
+
+    def onward(value, distance):
+        steps = [(s, s - distance if s & 2 else s + distance) for s in range(count)]
+        return lax.ppermute(value, "ctx", [(s, t) for s, t in steps if 0 <= t < count])
 
     gathered = lax.all_gather(inputs, "tp", axis=0)
     proj, gates, tail = project(gathered, weights)
     tail = lax.ppermute(tail, "ctx", [(s, s + 1) for s in range(count - 1)])
-    send, *kept = slab(proj, tail, gates, filters, decay, bias, grad_core)
-    got = exchange(send, group)
-    total = call(group_kernel, [((RADIX, PACK, DH), BF16)])(got)[0]
-    total, before = call(
-        row_kernel, [((RADIX, PACK, DH), BF16), ((2 * DH + 8, DH), F32)]
-    )(exchange(total, row))
-    states = call(states_kernel, [((RADIX, DH, DH), BF16)])(exchange(total, rank), before, got)[0]
-    states = exchange(states, group)
-    full, grad_gates, halo = gradient(states, kept, gates, filters, decay, bias, grad_core)
+    own, send, *kept = slab(proj, tail, gates, filters, decay, bias, grad_core)
+    partner = swap(send, 1)
+    send, keep = call(pair_kernel, [packed, packed])(own, partner)
+    total = call(group_kernel, [packed])(keep, swap(send, 2))[0]
+    before = onward(total, 4)
+    total = call(first_window_kernel, [packed])(total, before)[0]
+    total, before = call(window_kernel, [packed, packed])(total, before, onward(total, 8))
+    total, before = call(last_window_kernel, [square, packed])(total, before, onward(total, 16))
+    mine, send = call(start_kernel, [square, square])(before, onward(total, 32), keep)
+    here, send = call(states_kernel, [((2, DH, DH), BF16)] * 2)(mine, swap(send, 2), own, partner)
+    there = swap(send, 1)
+    full, grad_gates, halo = gradient(here, there, kept, gates, filters, decay, bias, grad_core)
     halo = lax.ppermute(halo, "ctx", [(s + 1, s) for s in range(count - 1)])
     shares = spread(full, halo, grad_gates, weights, parts)
     shares = lax.all_to_all(shares, "tp", 0, 0)

time: 120 us -> 129 us (1.075); the launches traced: 120 us -> 127 us
  blocking collectives: 98.8 us -> 42.9 us
  starting transfers between devices: 2.58 us -> 49.3 us
  waiting for transfers between devices: 4.03 us -> 21.1 us
    all_to_all x4 -> x0, blocking collectives: 56.8 us -> none  [exchange(): return lax.all_to_all(value, 'ctx', 0, 0, axis_index_groups=groups)]
    ppermute x0 -> x8, starting transfers between devices: none -> 46.7 us  [the longest x4 35.9 us: onward(): lax.ppermute(value, 'ctx', [(s, t) for s, t in steps if 0 <= t < count])]
    ppermute x0 -> x8, waiting for transfers between devices: none -> 17.1 us  [the longest x4 11.4 us: swap(): return lax.ppermute(value, 'ctx', [(s, s ^ distance) for s in range(count)])]
    pallas_call x4 -> x8, Pallas kernels: 6.62 us -> 6.09 us  [the longest x1 4.7 us: slab(): call(slab_kernel, [((PACK + DH, DH), BF16), ((PACK + DH, DH), BF16), ((DH...]
    unnamed x24 -> x26, local copies, waits for them, and re-layouts: 3.15 us -> 2.96 us
  transfers between devices with their start and end apart: 2 -> 10, of which waited for: 2 -> 10; matrix products, arithmetic and copies ran while one was open for 0% -> 0% of each run, Pallas kernels for 0% -> 0%
where the time goes in v2:
time: 129 us; the launch traced here: 127 us
  starting transfers between devices  49.3 us (38%)
  blocking collectives  42.9 us (33%)
  waiting for transfers between devices  21.1 us (16%)
  Pallas kernels  9.64 us (7%)
  local copies, waits for them, and re-layouts  2.96 us (2%)
    ppermute x4, starting transfers between devices, onward(): lax.ppermute(value, 'ctx', [(s, t) for s, t in steps if 0 <= t < count])  35.9 us
    all_to_all x1, blocking collectives, local(): shares = lax.all_to_all(shares, 'tp', 0, 0)  22.7 us
    all_gather x1, blocking collectives, local(): gathered = lax.all_gather(inputs, 'tp', axis=0)  20.1 us
    ppermute x4, waiting for transfers between devices, swap(): return lax.ppermute(value, 'ctx', [(s, s ^ distance) for s in range(count)])  11.4 us
    ppermute x4, starting transfers between devices, swap(): return lax.ppermute(value, 'ctx', [(s, s ^ distance) for s in range(count)])  10.7 us
    ppermute x4, waiting for transfers between devices, onward(): lax.ppermute(value, 'ctx', [(s, t) for s, t in steps if 0 <= t < count])  5.68 us
    pallas_call x1, Pallas kernels, slab(): call(slab_kernel, [((PACK + DH, DH), BF16), ((PACK + DH, DH), BF16), ((DH...  4.7 us
    ppermute x1, waiting for transfers between devices, local(): halo = lax.ppermute(halo, 'ctx', [(s + 1, s) for s in range(count - 1)])  3.18 us
  transfers between devices with their start and end apart: 10, of which 10 were waited for; matrix products, arithmetic and copies ran while one was open for 0% of the time, Pallas kernels for 0%

profile of v2, /device:TPU:1, one launch (start us, length us, event | category | flops | bytes accessed | tf_op | source)
XLA Modules:
  0.0 126.8 jit_solution(11723712492470569224)
XLA Ops:
  0.0 0.0 copy-start.2
  0.0 0.0 copy-start.6
  0.0 0.0 copy-start.7
  0.0 20.1 %all-gather = bf16[1024,256]{1,0:T(8,128)(2,1)S(1)} all-gather(bf16[128,256]{1,0:T(8,128)(2,1)} %param.12), channel_id=2, replica_groups=mesh['ctx'=64,'tp'=8] {'tp'}, dimensions={0}, use_global_device_ids=true | all-gather | bytes 589824 | tf_op jit(solution)/shard_map/all_gather | solution.py:470
  20.2 0.0 copy-done.2
  20.2 0.0 copy-done.6
  20.2 0.0 copy-done.7
  20.2 0.0 copy-start
  20.2 1.2 copy-done
  21.4 0.0 copy-start.3
  21.4 1.0 copy-done.3
  22.4 0.0 copy-start.5
  22.4 0.0 copy-start.10
  22.4 0.0 copy-start.12
  22.4 0.9 shard_map.118
  23.4 1.3 %collective-permute-start = (bf16[16,512]{1,0:T(8,128)(2,1)S(1)}, bf16[16,512]{1,0:T(8,128)(2,1)S(1)}, u32[]{:S(2)}, u32[]{:S(2)}) collective-permute-start(bf16[16,512]{1,0:T(8,128)(2,1)S(1)} %get-tuple-element.34), channel_id=1, source_target_pairs={{0,8},{8,16},{16,24},{24,32},{32,40},{40,48},{48,56},{56,64},{64,7... | collective-permute-start | bytes 49160 | tf_op jit(solution)/shard_map/ppermute | solution.py:472
  24.7 0.9 collective-permute-done.tail_ref
  25.5 0.0 copy-start.8
  25.5 0.0 copy-start.9
  25.5 0.0 copy-start.11
  25.5 0.0 copy-done.5
  25.5 0.0 copy-done.10
  25.5 0.0 copy-done.12
  25.6 0.7 copy-done.8
  26.2 0.0 copy-done.9
  26.2 0.0 copy-done.11
  26.2 4.7 %shard_map.119 = (bf16[400,128]{1,0:T(8,128)(2,1)S(1)}, bf16[400,128]{1,0:T(8,128)(2,1)S(1)}, f32[128,512]{1,0:T(8,128)S(1)}, f32[2,128,128]{2,1,0:T(8,128)S(1)}...) custom-call(bf16[128,512]{1,0:T(8,128)(2,1)S(1)} %get-tuple-element., ...), custom_call_target="tpu_custom_call" | custom-call | tf_op jit(solution)/shard_map/pallas_call | solution.py:421
  30.9 3.6 %collective-permute-start.1 = (bf16[400,128]{1,0:T(8,128)(2,1)S(1)}, bf16[400,128]{1,0:T(8,128)(2,1)S(1)}, u32[]{:S(2)}, u32[]{:S(2)}) collective-permute-start(bf16[400,128]{1,0:T(8,128)(2,1)S(1)} %get-tuple-element.37), channel_id=1, source_target_pairs={{0,8},{8,0},{16,24},{24,16},{32,40},{40,32},{48,56},{56,48},{64,72... | collective-permute-start | bytes 307208 | tf_op jit(solution)/shard_map/ppermute | solution.py:464
  34.6 2.0 %collective-permute-done.1.got_ref.partner_ref = bf16[400,128]{1,0:T(8,128)(2,1)S(1)} collective-permute-done((bf16[400,128]{1,0:T(8,128)(2,1)S(1)}, bf16[400,128]{1,0:T(8,128)(2,1)S(1)}, u32[]{:S(2)}, u32[]{:S(2)}) %collective-permute-start.1) | collective-permute-done | bytes 102432 | tf_op jit(solution)/shard_map/ppermute | solution.py:464
  36.6 0.3 shard_map.120
  36.8 3.3 %collective-permute-start.2 = (bf16[272,128]{1,0:T(8,128)(2,1)S(1)}, bf16[272,128]{1,0:T(8,128)(2,1)S(1)}, u32[]{:S(2)}, u32[]{:S(2)}) collective-permute-start(bf16[272,128]{1,0:T(8,128)(2,1)S(1)} %get-tuple-element.39), channel_id=1, source_target_pairs={{0,16},{8,24},{16,0},{24,8},{32,48},{40,56},{48,32},{56,40},{64,80... | collective-permute-start | bytes 208904 | tf_op jit(solution)/shard_map/ppermute | solution.py:464
  40.1 2.7 %collective-permute-done.2.got_ref = bf16[272,128]{1,0:T(8,128)(2,1)S(1)} collective-permute-done((bf16[272,128]{1,0:T(8,128)(2,1)S(1)}, bf16[272,128]{1,0:T(8,128)(2,1)S(1)}, u32[]{:S(2)}, u32[]{:S(2)}) %collective-permute-start.2) | collective-permute-done | bytes 69664 | tf_op jit(solution)/shard_map/ppermute | solution.py:464
  42.8 0.2 shard_map.121.total_ref
  43.0 7.8 %collective-permute-start.3 = (bf16[272,128]{1,0:T(8,128)(2,1)S(1)}, bf16[272,128]{1,0:T(8,128)(2,1)S(1)}, u32[]{:S(2)}, u32[]{:S(2)}) collective-permute-start(bf16[272,128]{1,0:T(8,128)(2,1)S(1)} %shard_map.121.total_ref), channel_id=1, source_target_pairs={{0,32},{8,40},{32,64},{40,72},{48,16},{56,24},{64,96},{72,104},{80... | collective-permute-start | bytes 208904 | tf_op jit(solution)/shard_map/ppermute | solution.py:468
  50.8 1.3 %collective-permute-done.3.got_ref.before_ref = bf16[272,128]{1,0:T(8,128)(2,1)S(1)} collective-permute-done((bf16[272,128]{1,0:T(8,128)(2,1)S(1)}, bf16[272,128]{1,0:T(8,128)(2,1)S(1)}, u32[]{:S(2)}, u32[]{:S(2)}) %collective-permute-start.3) | collective-permute-done | bytes 69664 | tf_op jit(solution)/shard_map/ppermute | solution.py:468
  52.1 0.2 shard_map.122.total_ref
  52.3 14.0 %collective-permute-start.4 = (bf16[272,128]{1,0:T(8,128)(2,1)S(1)}, bf16[272,128]{1,0:T(8,128)(2,1)S(1)}, u32[]{:S(2)}, u32[]{:S(2)}) collective-permute-start(bf16[272,128]{1,0:T(8,128)(2,1)S(1)} %shard_map.122.total_ref), channel_id=1, source_target_pairs={{0,64},{8,72},{32,96},{40,104},{64,128},{72,136},{80,16},{88,24},{... | collective-permute-start | bytes 208904 | tf_op jit(solution)/shard_map/ppermute | solution.py:468
  66.3 2.0 %collective-permute-done.4.got_ref = bf16[272,128]{1,0:T(8,128)(2,1)S(1)} collective-permute-done((bf16[272,128]{1,0:T(8,128)(2,1)S(1)}, bf16[272,128]{1,0:T(8,128)(2,1)S(1)}, u32[]{:S(2)}, u32[]{:S(2)}) %collective-permute-start.4) | collective-permute-done | bytes 69664 | tf_op jit(solution)/shard_map/ppermute | solution.py:468
  68.2 0.2 shard_map.123
  68.4 0.0 copy-start.1
  68.4 7.9 %collective-permute-start.5 = (bf16[272,128]{1,0:T(8,128)(2,1)S(1)}, bf16[272,128]{1,0:T(8,128)(2,1)S(1)}, u32[]{:S(2)}, u32[]{:S(2)}) collective-permute-start(bf16[272,128]{1,0:T(8,128)(2,1)S(1)} %get-tuple-element.40.total_ref), channel_id=1, source_target_pairs={{0,128},{8,136},{32,160},{40,168},{64,192},{72,200},{96,224},{104,... | collective-permute-start | bytes 208904 | tf_op jit(solution)/shard_map/ppermute | solution.py:468
  76.4 1.3 %collective-permute-done.5.got_ref = bf16[272,128]{1,0:T(8,128)(2,1)S(1)} collective-permute-done((bf16[272,128]{1,0:T(8,128)(2,1)S(1)}, bf16[272,128]{1,0:T(8,128)(2,1)S(1)}, u32[]{:S(2)}, u32[]{:S(2)}) %collective-permute-start.5) | collective-permute-done | bytes 69664 | tf_op jit(solution)/shard_map/ppermute | solution.py:468
  77.7 0.2 shard_map.124
  77.9 6.2 %collective-permute-start.6 = (bf16[128,128]{1,0:T(8,128)(2,1)S(1)}, bf16[128,128]{1,0:T(8,128)(2,1)S(1)}, u32[]{:S(2)}, u32[]{:S(2)}) collective-permute-start(bf16[128,128]{1,0:T(8,128)(2,1)S(1)} %get-tuple-element.43), channel_id=1, source_target_pairs={{0,256},{8,264},{32,288},{40,296},{64,320},{72,328},{96,352},{104,... | collective-permute-start | bytes 98312 | tf_op jit(solution)/shard_map/ppermute | solution.py:468
  84.1 1.0 collective-permute-done.6.got_ref
  85.2 0.3 shard_map.125
  85.4 1.9 %collective-permute-start.7 = (bf16[128,128]{1,0:T(8,128)(2,1)S(1)}, bf16[128,128]{1,0:T(8,128)(2,1)S(1)}, u32[]{:S(2)}, u32[]{:S(2)}) collective-permute-start(bf16[128,128]{1,0:T(8,128)(2,1)S(1)} %get-tuple-element.45), channel_id=1, source_target_pairs={{0,16},{8,24},{16,0},{24,8},{32,48},{40,56},{48,32},{56,40},{64,80... | collective-permute-start | bytes 98312 | tf_op jit(solution)/shard_map/ppermute | solution.py:464
  87.4 3.6 %collective-permute-done.7.got_ref = bf16[128,128]{1,0:T(8,128)(2,1)S(1)} collective-permute-done((bf16[128,128]{1,0:T(8,128)(2,1)S(1)}, bf16[128,128]{1,0:T(8,128)(2,1)S(1)}, u32[]{:S(2)}, u32[]{:S(2)}) %collective-permute-start.7) | collective-permute-done | bytes 32800 | tf_op jit(solution)/shard_map/ppermute | solution.py:464
  91.0 0.2 shard_map.126
  91.2 1.9 %collective-permute-start.8 = (bf16[2,128,128]{2,1,0:T(8,128)(2,1)S(1)}, bf16[2,128,128]{2,1,0:T(8,128)(2,1)S(1)}, u32[]{:S(2)}, u32[]{:S(2)}) collective-permute-start(bf16[2,128,128]{2,1,0:T(8,128)(2,1)S(1)} %get-tuple-element.47), channel_id=1, source_target_pairs={{0,8},{8,0},{16,24},{24,16},{32,40},{40,32},{48,56},{56,48},{64,72... | collective-permute-start | bytes 196616 | tf_op jit(solution)/shard_map/ppermute | solution.py:464
  93.1 3.1 %collective-permute-done.8.there_ref = bf16[2,128,128]{2,1,0:T(8,128)(2,1)S(1)} collective-permute-done((bf16[2,128,128]{2,1,0:T(8,128)(2,1)S(1)}, bf16[2,128,128]{2,1,0:T(8,128)(2,1)S(1)}, u32[]{:S(2)}, u32[]{:S(2)}) %collective-permute-start.8) | collective-permute-done | bytes 65568 | tf_op jit(solution)/shard_map/ppermute | solution.py:464
  96.2 0.0 copy-start.4
  96.2 1.6 %shard_map.127 = (f32[128,512]{1,0:T(8,128)S(1)}, bf16[128,128]{1,0:T(8,128)(2,1)S(1)}, f32[8,512]{1,0:T(8,128)S(1)}) custom-call(bf16[2,128,128]{2,1,0:T(8,128)(2,1)S(1)} %get-tuple-element.46.here_ref, bf16[2,128,128]{2,1,0:T(8,128)(2,1)S(1)} %collective-permute-done.8.there_ref, f32[128,512]{1,0:T(8,128)S(1)} %get-tuple-element.48.pre_ref, ...), custom_call_target="tpu_custom_call" | custom-call | tf_op jit(solution)/shard_map/pallas_call | solution.py:435
  97.8 1.3 %collective-permute-start.9 = (f32[8,512]{1,0:T(8,128)S(1)}, f32[8,512]{1,0:T(8,128)S(1)}, u32[]{:S(2)}, u32[]{:S(2)}) collective-permute-start(f32[8,512]{1,0:T(8,128)S(1)} %get-tuple-element.59), channel_id=1, source_target_pairs={{8,0},{16,8},{24,16},{32,24},{40,32},{48,40},{56,48},{64,56},{72,6... | collective-permute-start | bytes 49160 | tf_op jit(solution)/shard_map/ppermute | solution.py:485
  99.1 3.2 %collective-permute-done.9.halo_ref = f32[8,512]{1,0:T(8,128)S(1)} collective-permute-done((f32[8,512]{1,0:T(8,128)S(1)}, f32[8,512]{1,0:T(8,128)S(1)}, u32[]{:S(2)}, u32[]{:S(2)}) %collective-permute-start.9) | collective-permute-done | bytes 16416 | tf_op jit(solution)/shard_map/ppermute | solution.py:485
  102.3 0.0 copy-done.1
  102.3 0.0 copy-done.4
  102.3 1.0 shard_map.128
  103.4 22.7 %all_to_all.5 = bf16[8,128,256]{2,1,0:T(8,128)(2,1)S(1)} all-to-all(bf16[8,128,256]{2,1,0:T(8,128)(2,1)S(1)} %shard_map.128), channel_id=1, replica_groups=mesh['ctx'=64,'tp'=8] {'tp'}, dimensions={0} | all-to-all | bytes 1048576 | tf_op jit(solution)/shard_map/all_to_all | solution.py:487
  126.1 0.7 reduce_sum.12
Async XLA Ops:
  0.0 20.2 %copy-start.2 = (bf16[2048,128]{1,0:T(8,128)(2,1)S(1)}, bf16[2048,128]{1,0:T(8,128)(2,1)}, u32[]{:S(2)}) copy-start(bf16[2048,128]{1,0:T(8,128)(2,1)} %wq_ref.3) | copy-start | bytes 1572868
  0.0 20.2 %copy-start.6 = (bf16[2048,2]{0,1:T(2,128)(2,1)S(1)}, bf16[2048,2]{0,1:T(2,128)(2,1)}, u32[]{:S(2)}) copy-start(bf16[2048,2]{0,1:T(2,128)(2,1)} %param.16) | copy-start | bytes 24580
  0.0 20.2 %copy-start.7 = (bf16[2048,2]{0,1:T(2,128)(2,1)S(1)}, bf16[2048,2]{0,1:T(2,128)(2,1)}, u32[]{:S(2)}) copy-start(bf16[2048,2]{0,1:T(2,128)(2,1)} %param.17) | copy-start | bytes 24580
  20.2 1.2 copy-start
  21.4 1.0 copy-start.3
  22.4 3.1 %copy-start.5 = (bf16[128,256]{1,0:T(8,128)(2,1)S(1)}, bf16[128,256]{1,0:T(8,128)(2,1)}, u32[]{:S(2)}) copy-start(bf16[128,256]{1,0:T(8,128)(2,1)} %grad_ref.3) | copy-start | bytes 196612
  22.4 3.1 %copy-start.10 = (bf16[4,128]{1,0:T(4,128)(2,1)S(1)}, bf16[4,128]{1,0:T(4,128)(2,1)}, u32[]{:S(2)}) copy-start(bf16[4,128]{1,0:T(4,128)(2,1)} %fk_ref.3) | copy-start | bytes 3076
  22.4 3.1 %copy-start.12 = (f32[2]{0:T(128)S(1)}, f32[2]{0:T(128)}, u32[]{:S(2)}) copy-start(f32[2]{0:T(128)} %param.22) | copy-start | bytes 28
  23.4 2.1 %collective-permute-start = (bf16[16,512]{1,0:T(8,128)(2,1)S(1)}, bf16[16,512]{1,0:T(8,128)(2,1)S(1)}, u32[]{:S(2)}, u32[]{:S(2)}) collective-permute-start(bf16[16,512]{1,0:T(8,128)(2,1)S(1)} %get-tuple-element.34), channel_id=1, source_target_pairs={{0,8},{8,16},{16,24},{24,32},{32,40},{40,48},{48,56},{56,64},{64,7... | collective-permute-start | bytes 49160 | tf_op jit(solution)/shard_map/ppermute | solution.py:472
  25.5 0.7 copy-start.8
  25.5 0.7 copy-start.9
  25.5 0.7 copy-start.11
  30.9 5.7 %collective-permute-start.1 = (bf16[400,128]{1,0:T(8,128)(2,1)S(1)}, bf16[400,128]{1,0:T(8,128)(2,1)S(1)}, u32[]{:S(2)}, u32[]{:S(2)}) collective-permute-start(bf16[400,128]{1,0:T(8,128)(2,1)S(1)} %get-tuple-element.37), channel_id=1, source_target_pairs={{0,8},{8,0},{16,24},{24,16},{32,40},{40,32},{48,56},{56,48},{64,72... | collective-permute-start | bytes 307208 | tf_op jit(solution)/shard_map/ppermute | solution.py:464
  36.8 6.0 %collective-permute-start.2 = (bf16[272,128]{1,0:T(8,128)(2,1)S(1)}, bf16[272,128]{1,0:T(8,128)(2,1)S(1)}, u32[]{:S(2)}, u32[]{:S(2)}) collective-permute-start(bf16[272,128]{1,0:T(8,128)(2,1)S(1)} %get-tuple-element.39), channel_id=1, source_target_pairs={{0,16},{8,24},{16,0},{24,8},{32,48},{40,56},{48,32},{56,40},{64,80... | collective-permute-start | bytes 208904 | tf_op jit(solution)/shard_map/ppermute | solution.py:464
  43.0 9.2 %collective-permute-start.3 = (bf16[272,128]{1,0:T(8,128)(2,1)S(1)}, bf16[272,128]{1,0:T(8,128)(2,1)S(1)}, u32[]{:S(2)}, u32[]{:S(2)}) collective-permute-start(bf16[272,128]{1,0:T(8,128)(2,1)S(1)} %shard_map.121.total_ref), channel_id=1, source_target_pairs={{0,32},{8,40},{32,64},{40,72},{48,16},{56,24},{64,96},{72,104},{80... | collective-permute-start | bytes 208904 | tf_op jit(solution)/shard_map/ppermute | solution.py:468
  52.3 15.9 %collective-permute-start.4 = (bf16[272,128]{1,0:T(8,128)(2,1)S(1)}, bf16[272,128]{1,0:T(8,128)(2,1)S(1)}, u32[]{:S(2)}, u32[]{:S(2)}) collective-permute-start(bf16[272,128]{1,0:T(8,128)(2,1)S(1)} %shard_map.122.total_ref), channel_id=1, source_target_pairs={{0,64},{8,72},{32,96},{40,104},{64,128},{72,136},{80,16},{88,24},{... | collective-permute-start | bytes 208904 | tf_op jit(solution)/shard_map/ppermute | solution.py:468
  68.4 33.9 %copy-start.1 = (bf16[2048,256]{1,0:T(8,128)(2,1)S(1)}, bf16[2048,256]{1,0:T(8,128)(2,1)}, u32[]{:S(2)}) copy-start(bf16[2048,256]{1,0:T(8,128)(2,1)} %wv_ref.3) | copy-start | bytes 3145732
  68.4 9.3 %collective-permute-start.5 = (bf16[272,128]{1,0:T(8,128)(2,1)S(1)}, bf16[272,128]{1,0:T(8,128)(2,1)S(1)}, u32[]{:S(2)}, u32[]{:S(2)}) collective-permute-start(bf16[272,128]{1,0:T(8,128)(2,1)S(1)} %get-tuple-element.40.total_ref), channel_id=1, source_target_pairs={{0,128},{8,136},{32,160},{40,168},{64,192},{72,200},{96,224},{104,... | collective-permute-start | bytes 208904 | tf_op jit(solution)/shard_map/ppermute | solution.py:468
  77.9 7.2 %collective-permute-start.6 = (bf16[128,128]{1,0:T(8,128)(2,1)S(1)}, bf16[128,128]{1,0:T(8,128)(2,1)S(1)}, u32[]{:S(2)}, u32[]{:S(2)}) collective-permute-start(bf16[128,128]{1,0:T(8,128)(2,1)S(1)} %get-tuple-element.43), channel_id=1, source_target_pairs={{0,256},{8,264},{32,288},{40,296},{64,320},{72,328},{96,352},{104,... | collective-permute-start | bytes 98312 | tf_op jit(solution)/shard_map/ppermute | solution.py:468
  85.4 5.6 %collective-permute-start.7 = (bf16[128,128]{1,0:T(8,128)(2,1)S(1)}, bf16[128,128]{1,0:T(8,128)(2,1)S(1)}, u32[]{:S(2)}, u32[]{:S(2)}) collective-permute-start(bf16[128,128]{1,0:T(8,128)(2,1)S(1)} %get-tuple-element.45), channel_id=1, source_target_pairs={{0,16},{8,24},{16,0},{24,8},{32,48},{40,56},{48,32},{56,40},{64,80... | collective-permute-start | bytes 98312 | tf_op jit(solution)/shard_map/ppermute | solution.py:464
  91.2 5.0 %collective-permute-start.8 = (bf16[2,128,128]{2,1,0:T(8,128)(2,1)S(1)}, bf16[2,128,128]{2,1,0:T(8,128)(2,1)S(1)}, u32[]{:S(2)}, u32[]{:S(2)}) collective-permute-start(bf16[2,128,128]{2,1,0:T(8,128)(2,1)S(1)} %get-tuple-element.47), channel_id=1, source_target_pairs={{0,8},{8,0},{16,24},{24,16},{32,40},{40,32},{48,56},{56,48},{64,72... | collective-permute-start | bytes 196616 | tf_op jit(solution)/shard_map/ppermute | solution.py:464
  96.2 6.1 %copy-start.4 = (bf16[2048,128]{1,0:T(8,128)(2,1)S(1)}, bf16[2048,128]{1,0:T(8,128)(2,1)}, u32[]{:S(2)}) copy-start(bf16[2048,128]{1,0:T(8,128)(2,1)} %wk_ref.3) | copy-start | bytes 1572868
  97.8 4.5 %collective-permute-start.9 = (f32[8,512]{1,0:T(8,128)S(1)}, f32[8,512]{1,0:T(8,128)S(1)}, u32[]{:S(2)}, u32[]{:S(2)}) collective-permute-start(f32[8,512]{1,0:T(8,128)S(1)} %get-tuple-element.59), channel_id=1, source_target_pairs={{8,0},{16,8},{24,16},{32,24},{40,32},{48,40},{56,48},{64,56},{72,6... | collective-permute-start | bytes 49160 | tf_op jit(solution)/shard_map/ppermute | solution.py:485

commit v3 on v1

--- a/solution.py
+++ b/solution.py
@@ -82,27 +82,35 @@
     return result
 
 
-def project_kernel(x_ref, wq_ref, wk_ref, wv_ref, wb_ref, wa_ref, proj_ref, ba_ref, tail_ref):
-    parts = x_ref.shape[0]
-    width = x_ref.shape[2]
-    weights = (wq_ref, wk_ref, wv_ref, wb_ref, wa_ref)
-    sums = [None] * 5
+def project_kernel(
+    x_ref, wq_ref, wk_ref, wv_ref, wb_ref, wa_ref, proj_ref, ba_ref, tail_ref, held_ref, sems
+):
+    parts, _, width = x_ref.shape
+    places = (slice(0, DH), slice(DH, 2 * DH), slice(2 * DH, 4 * DH))
+    copies = []
+    for part in range(parts):
+        span = slice(part * width, (part + 1) * width)
+        for place, weight in enumerate((wq_ref, wk_ref, wv_ref)):
+            copies.append(
+                pltpu.make_async_copy(
+                    weight.at[span, :], held_ref.at[span, places[place]], sems.at[part, place]
+                )
+            )
+            copies[-1].start()
+    total = jnp.zeros((DH, 4 * DH), F32)
+    beta = jnp.zeros((DH, 2), F32)
+    alpha = jnp.zeros((DH, 2), F32)
     for part in range(parts):
         rows = x_ref[part]
-        for place, weight in enumerate(weights):
-            piece = jnp.dot(
-                rows, weight[part * width : (part + 1) * width, :], preferred_element_type=F32
-            )
-            sums[place] = piece if part == 0 else sums[place] + piece
-    proj_ref[:, :DH] = bf(sums[0])
-    proj_ref[:, DH : 2 * DH] = bf(sums[1])
-    proj_ref[:, 2 * DH :] = bf(sums[2])
-    tail_ref[:, :DH] = bf(sums[0][DH - 16 :])
-    tail_ref[:, DH : 2 * DH] = bf(sums[1][DH - 16 :])
-    tail_ref[:, 2 * DH :] = bf(sums[2][DH - 16 :])
-    ba_ref[...] = bf(
-        lanes_of([sums[3][:, 0:1], sums[3][:, 1:2], sums[4][:, 0:1], sums[4][:, 1:2]])
-    )
+        span = slice(part * width, (part + 1) * width)
+        beta = beta + dot(rows, wb_ref[:, span], (1, 1))
+        alpha = alpha + dot(rows, wa_ref[:, span], (1, 1))
+        for copy in copies[3 * part : 3 * part + 3]:
+            copy.wait()
+        total = total + dot(rows, held_ref[span, :])
+    proj_ref[...] = bf(total)
+    tail_ref[...] = bf(total[DH - 16 :])
+    ba_ref[...] = bf(lanes_of([beta[:, 0:1], beta[:, 1:2], alpha[:, 0:1], alpha[:, 1:2]]))
 
 
 def gate_rows(decay_ref, bias_ref):
@@ -185,12 +193,12 @@
         send_ref[2 * head + 1, 2 * DH :] = decay_rows
 
 
-def unpack(ref, place):
-    decay = ref[place, 2 * DH :].astype(F32)
+def unpack(ref):
+    decay = ref[2 * DH :].astype(F32)
     return (
         decay[0:1, 0:1] + decay[1:2, 0:1] + decay[2:3, 0:1],
-        ref[place, 0:DH],
-        ref[place, DH : 2 * DH].astype(F32),
+        ref[0:DH].astype(F32),
+        ref[DH : 2 * DH].astype(F32),
     )
 
 
@@ -203,22 +211,18 @@
     decay, matrix, offset = later
     return (
         decay * earlier[0],
-        decay * earlier[1] + earlier[0] * matrix.astype(F32) - dot(matrix, earlier[1]),
+        decay * earlier[1] + earlier[0] * matrix - dot(matrix, earlier[1]),
         apply_map(later, earlier[2]),
     )
 
 
-def pack(ref, total):
+def pack(total):
     decay, matrix, offset = total
-    packed = (bf(matrix), bf(offset), split_decay(decay))
-    for place in range(RADIX):
-        ref[place, 0:DH] = packed[0]
-        ref[place, DH : 2 * DH] = packed[1]
-        ref[place, 2 * DH :] = packed[2]
-
-
-def widen(item):
-    return item[0], item[1].astype(F32), item[2]
+    return jnp.concatenate([bf(matrix), bf(offset), split_decay(decay)], axis=0)
+
+
+def is_backward():
+    return lax.axis_index("ctx") % 2 == 1
 
 
 def in_order(step, backward):
@@ -226,40 +230,29 @@
 
 
 def group_kernel(got_ref, total_ref):
-    backward = lax.axis_index("ctx") % 2 == 1
-    total = widen(unpack(got_ref, in_order(0, backward)))
+    backward = is_backward()
+    total = unpack(got_ref.at[in_order(0, backward)])
     for step in range(1, RADIX):
-        total = compose(unpack(got_ref, in_order(step, backward)), total)
-    pack(total_ref, total)
-
-
-def row_kernel(got_ref, total_ref, before_ref):
-    mine = lax.axis_index("ctx")
-    backward = mine % 2 == 1
-    place = in_order((mine // RADIX) % RADIX, backward)
-    before_ref[0:DH] = jnp.zeros((DH, DH), F32)
-    before_ref[DH : 2 * DH] = jnp.zeros((DH, DH), F32)
-    before_ref[2 * DH :] = jnp.ones((8, DH), F32)
-    total = widen(unpack(got_ref, in_order(0, backward)))
-    for step in range(1, RADIX):
-
-        @pl.when(place == step)
-        def _(total=total):
-            before_ref[0:DH] = total[1]
-            before_ref[DH : 2 * DH] = total[2]
-            before_ref[2 * DH :] = jnp.broadcast_to(total[0], (8, DH))
-
-        total = compose(unpack(got_ref, in_order(step, backward)), total)
-    pack(total_ref, total)
+        total = compose(unpack(got_ref.at[in_order(step, backward)]), total)
+    total_ref[...] = pack(total)
+
+
+def window_kernel(total_ref, last_ref, middle_ref, first_ref, wider_ref, before_ref):
+    before = compose(unpack(last_ref), compose(unpack(middle_ref), unpack(first_ref)))
+    before_ref[0:DH] = before[1]
+    before_ref[DH : 2 * DH] = before[2]
+    before_ref[2 * DH :] = jnp.broadcast_to(before[0], (8, DH))
+    wider = pack(compose(unpack(total_ref), before))
+    for place in range(RADIX):
+        wider_ref[place] = wider
 
 
 def states_kernel(rows_ref, before_ref, group_ref, out_ref):
-    mine = lax.axis_index("ctx")
-    backward = mine % 2 == 1
-    place = in_order(mine // (RADIX * RADIX), backward)
+    backward = is_backward()
+    place = in_order(lax.axis_index("ctx") // (RADIX * RADIX), backward)
     state = jnp.zeros((DH, DH), F32)
     for step in range(RADIX - 1):
-        later = apply_map(unpack(rows_ref, in_order(step, backward)), state)
+        later = apply_map(unpack(rows_ref.at[in_order(step, backward)]), state)
         state = jnp.where(step < place, later, state)
     before = (before_ref[2 * DH : 2 * DH + 1, 0:1], before_ref[0:DH], before_ref[DH : 2 * DH])
     state = apply_map(before, state)
@@ -267,7 +260,7 @@
         spot = in_order(step, backward)
         out_ref[spot] = bf(state)
         if step < RADIX - 1:
-            state = apply_map(unpack(group_ref, spot), state)
+            state = apply_map(unpack(group_ref.at[spot]), state)
 
 
 def gradient_kernel(
@@ -386,23 +379,34 @@
         total = dot(grads[:, :DH], wq_ref[span, :], (1, 1))
         total = total + dot(grads[:, DH : 2 * DH], wk_ref[span, :], (1, 1))
         total = total + dot(grads[:, 2 * DH :], wv_ref[span, :], (1, 1))
-        total = total + dot(gates[:, 0:2], wb_ref[span, :], (1, 1))
-        total = total + dot(gates[:, 2:4], wa_ref[span, :], (1, 1))
+        total = total + dot(gates[:, 0:2], wb_ref[:, span])
+        total = total + dot(gates[:, 2:4], wa_ref[:, span])
         out_ref[part] = bf(total)
 
 
-def call(kernel, outs, scratch=()):
+def call(kernel, outs, scratch=(), specs=None):
+    extra = {} if specs is None else {"in_specs": specs}
     return pl.pallas_call(
         kernel,
         out_shape=[jax.ShapeDtypeStruct(shape, kind) for shape, kind in outs],
-        scratch_shapes=[pltpu.VMEM(shape, F32) for shape in scratch],
+        scratch_shapes=list(scratch),
         compiler_params=pltpu.CompilerParams(vmem_limit_bytes=48 * 1024 * 1024),
+        **extra,
     )
 
 
 def project(gathered, weights):
+    parts = gathered.shape[0]
+    inside = pl.BlockSpec(memory_space=pltpu.VMEM)
+    outside = pl.BlockSpec(memory_space=pl.ANY)
     return call(
-        project_kernel, [((DH, 4 * DH), BF16), ((DH, DH), BF16), ((16, 4 * DH), BF16)]
+        project_kernel,
+        [((DH, 4 * DH), BF16), ((DH, DH), BF16), ((16, 4 * DH), BF16)],
+        [
+            pltpu.VMEM((weights[0].shape[0], 4 * DH), BF16),
+            pltpu.SemaphoreType.DMA((parts, 3)),
+        ],
+        [inside] + [outside] * 3 + [inside] * 2,
     )(gathered, *weights)
 
 
@@ -415,7 +419,7 @@
             ((2,) + square, BF16), ((2,) + square, F32), ((2,) + square, BF16),
             ((2,) + square, F32), ((2,) + square, F32), (square, F32), (square, F32),
         ],
-        [(8 + DH, 4 * DH)],
+        [pltpu.VMEM((8 + DH, 4 * DH), F32)],
     )(proj, tail, gates, *filters, decay, bias, grad)
 
 
@@ -424,7 +428,7 @@
     return call(
         gradient_kernel,
         [((DH, 4 * DH), F32), ((DH, DH), BF16), ((8, 4 * DH), F32)],
-        [(16 + DH, 4 * DH)],
+        [pltpu.VMEM((16 + DH, 4 * DH), F32)],
     )(
         states, pre, unit, cols, gates, inverse, mixed, weighted, back, gap, gram, cross,
         grad, *filters, decay, bias,
@@ -440,7 +444,7 @@
     inputs, query_weight, key_weight, value_weight, beta_weight, alpha_weight,
     query_filter, key_filter, value_filter, decay_log, step_bias, grad_core,
 ):
-    weights = (query_weight, key_weight, value_weight, beta_weight, alpha_weight)
+    weights = (query_weight, key_weight, value_weight, beta_weight.T, alpha_weight.T)
     filters = (query_filter, key_filter, value_filter)
     decay = decay_log.reshape(1, 2)
     bias = step_bias.reshape(1, 2)
@@ -448,24 +452,25 @@
     parts = lax.axis_size("tp")
     slabs = range(count)
     group = [[s for s in slabs if s // RADIX == g] for g in range(count // RADIX)]
-    row = [
-        [s for s in slabs if s // 16 == y and s % RADIX == low]
-        for y in range(count // 16) for low in range(RADIX)
-    ]
     rank = [[s for s in slabs if s % 16 == z] for z in range(16)]
 
     def exchange(value, groups):
         return lax.all_to_all(value, "ctx", 0, 0, axis_index_groups=groups)
+
+    def onward(value, distance):
+        steps = [(s, s - distance if s % 2 else s + distance) for s in slabs]
+        return lax.ppermute(value, "ctx", [(s, t) for s, t in steps if 0 <= t < count])
 
     gathered = lax.all_gather(inputs, "tp", axis=0)
     proj, gates, tail = project(gathered, weights)
     tail = lax.ppermute(tail, "ctx", [(s, s + 1) for s in range(count - 1)])
     send, *kept = slab(proj, tail, gates, filters, decay, bias, grad_core)
     got = exchange(send, group)
-    total = call(group_kernel, [((RADIX, PACK, DH), BF16)])(got)[0]
+    total = call(group_kernel, [((PACK, DH), BF16)])(got)[0]
+    earlier = [onward(total, RADIX * step) for step in range(1, RADIX)]
     total, before = call(
-        row_kernel, [((RADIX, PACK, DH), BF16), ((2 * DH + 8, DH), F32)]
-    )(exchange(total, row))
+        window_kernel, [((RADIX, PACK, DH), BF16), ((2 * DH + 8, DH), F32)]
+    )(total, *earlier)
     states = call(states_kernel, [((RADIX, DH, DH), BF16)])(exchange(total, rank), before, got)[0]
     states = exchange(states, group)
     full, grad_gates, halo = gradient(states, kept, gates, filters, decay, bias, grad_core)

time: 120 us -> 120 us (level)
  blocking collectives: 98.8 us -> 73.4 us
  starting transfers between devices: 2.58 us -> 25.3 us
  waiting for transfers between devices: 4.03 us -> 5.73 us
    all_to_all x4 -> x3, blocking collectives: 56.8 us -> 32.3 us  [exchange(): return lax.all_to_all(value, 'ctx', 0, 0, axis_index_groups=groups)]
    ppermute x0 -> x3, starting transfers between devices: none -> 22.7 us  [onward(): lax.ppermute(value, 'ctx', [(s, t) for s, t in steps if 0 <= t < count])]
    ppermute x0 -> x3, waiting for transfers between devices: none -> 1.33 us  [onward(): lax.ppermute(value, 'ctx', [(s, t) for s, t in steps if 0 <= t < count])]
    unnamed x24 -> x26, local copies, waits for them, and re-layouts: 3.15 us -> 2.96 us
  transfers between devices with their start and end apart: 2 -> 5, of which waited for: 2 -> 3; matrix products, arithmetic and copies ran while one was open for 0% -> 0% of each run, Pallas kernels for 0% -> 0%
where the time goes in v3:
time: 120 us; the launch traced here: 119 us
  blocking collectives  73.4 us (61%)
  starting transfers between devices  25.3 us (21%)
  Pallas kernels  10.9 us (9%)
  waiting for transfers between devices  5.73 us (5%)
  local copies, waits for them, and re-layouts  2.96 us (2%)
    all_to_all x3, blocking collectives, exchange(): return lax.all_to_all(value, 'ctx', 0, 0, axis_index_groups=groups)  32.3 us
    ppermute x3, starting transfers between devices, onward(): lax.ppermute(value, 'ctx', [(s, t) for s, t in steps if 0 <= t < count])  22.7 us
    all_to_all x1, blocking collectives, local(): shares = lax.all_to_all(shares, 'tp', 0, 0)  21 us
    all_gather x1, blocking collectives, local(): gathered = lax.all_gather(inputs, 'tp', axis=0)  20.1 us
    pallas_call x1, Pallas kernels, slab(): call(slab_kernel, [((4, PACK, DH), BF16), ((DH, 4 * DH), F32), ((2,) + sq...  4.75 us
    ppermute x1, waiting for transfers between devices, local(): halo = lax.ppermute(halo, 'ctx', [(s + 1, s) for s in range(count - 1)])  3.55 us
    unnamed x26, local copies, waits for them, and re-layouts  2.96 us
  transfers between devices with their start and end apart: 5, of which 3 were waited for; matrix products, arithmetic and copies ran while one was open for 0% of the time, Pallas kernels for 0%

profile of v3, /device:TPU:1, one launch (start us, length us, event | category | flops | bytes accessed | tf_op | source)
XLA Modules:
  0.0 119.1 jit_solution(15474853436966684534)
XLA Ops:
  0.0 0.0 copy-start.2
  0.0 0.0 copy-start.6
  0.0 0.0 copy-start.7
  0.0 20.1 %all-gather = bf16[1024,256]{1,0:T(8,128)(2,1)S(1)} all-gather(bf16[128,256]{1,0:T(8,128)(2,1)} %param.12), channel_id=2, replica_groups=mesh['ctx'=64,'tp'=8] {'tp'}, dimensions={0}, use_global_device_ids=true | all-gather | bytes 589824 | tf_op jit(solution)/shard_map/all_gather | solution.py:464
  20.2 0.0 copy-done.2
  20.2 0.0 copy-done.6
  20.2 0.0 copy-done.7
  20.2 0.0 copy-start
  20.2 1.2 %copy-done = bf16[2048,256]{1,0:T(8,128)(2,1)S(1)} copy-done((bf16[2048,256]{1,0:T(8,128)(2,1)S(1)}, bf16[2048,256]{1,0:T(8,128)(2,1)}, u32[]{:S(2)}) %copy-start) | copy-done | bytes 1048600
  21.4 0.0 copy-start.3
  21.4 1.0 copy-done.3
  22.4 0.0 copy-start.5
  22.4 0.0 copy-start.10
  22.4 0.0 copy-start.12
  22.4 1.6 %shard_map.118 = (bf16[128,512]{1,0:T(8,128)(2,1)S(1)}, bf16[128,128]{1,0:T(8,128)(2,1)S(1)}, bf16[16,512]{1,0:T(8,128)(2,1)S(1)}) custom-call(bf16[8,128,256]{2,1,0:T(8,128)(2,1)S(1)} %bitcast.5, bf16[2048,128]{1,0:T(8,128)(2,1)S(1)} %copy-done.2, bf16[2048,128]{1,0:T(8,128)(2,1)S(1)} %copy-done.3, bf16[2048,256]{1,0:T(8,128)(2,1)S(1)} %copy-done, ...), custom_call_target="tpu_custom_call" | custom-call | tf_op jit(solution)/shard_map/pallas_call | solution.py:402
  24.1 1.3 %collective-permute-start = (bf16[16,512]{1,0:T(8,128)(2,1)S(1)}, bf16[16,512]{1,0:T(8,128)(2,1)S(1)}, u32[]{:S(2)}, u32[]{:S(2)}) collective-permute-start(bf16[16,512]{1,0:T(8,128)(2,1)S(1)} %get-tuple-element.25), channel_id=1, source_target_pairs={{0,8},{8,16},{16,24},{24,32},{32,40},{40,48},{48,56},{56,64},{64,7... | collective-permute-start | bytes 49160 | tf_op jit(solution)/shard_map/ppermute | solution.py:466
  25.4 0.9 collective-permute-done.tail_ref
  26.2 0.0 copy-start.8
  26.2 0.0 copy-start.9
  26.2 0.0 copy-start.11
  26.2 0.0 copy-done.5
  26.2 0.0 copy-done.10
  26.3 0.0 copy-done.12
  26.3 0.7 copy-done.8
  26.9 0.0 copy-done.9
  26.9 0.0 copy-done.11
  26.9 4.7 %shard_map.119 = (bf16[4,272,128]{2,1,0:T(8,128)(2,1)S(1)}, f32[128,512]{1,0:T(8,128)S(1)}, f32[2,128,128]{2,1,0:T(8,128)S(1)}, f32[128,128]{1,0:T(8,128)S(1)}, ...) custom-call(bf16[128,512]{1,0:T(8,128)(2,1)S(1)} %get-tuple-element., ...), custom_call_target="tpu_custom_call" | custom-call | tf_op jit(solution)/shard_map/pallas_call | solution.py:415
  31.7 11.1 %all_to_all.20.got_ref.group_ref = bf16[4,272,128]{2,1,0:T(8,128)(2,1)S(1)} all-to-all(bf16[4,272,128]{2,1,0:T(8,128)(2,1)S(1)} %get-tuple-element.27), channel_id=1, replica_groups={{0,8,16,24},{32,40,48,56},{64,72,80,88},{96,104,112,120},{128,136,144,1..., dimensions={0} | all-to-all | bytes 557056 | tf_op jit(solution)/shard_map/all_to_all | solution.py:458
  42.8 0.4 shard_map.120.total_ref
  43.2 9.5 %collective-permute-start.3 = (bf16[272,128]{1,0:T(8,128)(2,1)S(1)}, bf16[272,128]{1,0:T(8,128)(2,1)S(1)}, u32[]{:S(2)}, u32[]{:S(2)}) collective-permute-start(bf16[272,128]{1,0:T(8,128)(2,1)S(1)} %shard_map.120.total_ref), channel_id=1, source_target_pairs={{0,96},{16,112},{32,128},{48,144},{64,160},{80,176},{96,192},{104,... | collective-permute-start | bytes 208904 | tf_op jit(solution)/shard_map/ppermute | solution.py:462
  52.7 7.4 %collective-permute-start.2 = (bf16[272,128]{1,0:T(8,128)(2,1)S(1)}, bf16[272,128]{1,0:T(8,128)(2,1)S(1)}, u32[]{:S(2)}, u32[]{:S(2)}) collective-permute-start(bf16[272,128]{1,0:T(8,128)(2,1)S(1)} %shard_map.120.total_ref), channel_id=1, source_target_pairs={{0,64},{16,80},{32,96},{48,112},{64,128},{72,8},{80,144},{88,24},{... | collective-permute-start | bytes 208904 | tf_op jit(solution)/shard_map/ppermute | solution.py:462
  60.1 5.9 %collective-permute-start.1 = (bf16[272,128]{1,0:T(8,128)(2,1)S(1)}, bf16[272,128]{1,0:T(8,128)(2,1)S(1)}, u32[]{:S(2)}, u32[]{:S(2)}) collective-permute-start(bf16[272,128]{1,0:T(8,128)(2,1)S(1)} %shard_map.120.total_ref), channel_id=1, source_target_pairs={{0,32},{16,48},{32,64},{40,8},{48,80},{56,24},{64,96},{72,40},{80,... | collective-permute-start | bytes 208904 | tf_op jit(solution)/shard_map/ppermute | solution.py:462
  66.0 0.0 collective-permute-done.3.first_ref
  66.0 0.0 collective-permute-done.2.middle_ref
  66.0 1.3 %collective-permute-done.1.last_ref = bf16[272,128]{1,0:T(8,128)(2,1)S(1)} collective-permute-done((bf16[272,128]{1,0:T(8,128)(2,1)S(1)}, bf16[272,128]{1,0:T(8,128)(2,1)S(1)}, u32[]{:S(2)}, u32[]{:S(2)}) %collective-permute-start.1) | collective-permute-done | bytes 69664 | tf_op jit(solution)/shard_map/ppermute | solution.py:462
  67.3 0.4 shard_map.121
  67.8 13.1 %all_to_all.21.rows_ref = bf16[4,272,128]{2,1,0:T(8,128)(2,1)S(1)} all-to-all(bf16[4,272,128]{2,1,0:T(8,128)(2,1)S(1)} %get-tuple-element.28), channel_id=1, replica_groups={{0,128,256,384},{8,136,264,392},{16,144,272,400},{24,152,280,408},{32,1..., dimensions={0} | all-to-all | bytes 557056 | tf_op jit(solution)/shard_map/all_to_all | solution.py:458
  80.9 0.0 copy-start.1
  80.9 0.9 shard_map.122
  81.8 8.0 %all_to_all.22.states_ref = bf16[4,128,128]{2,1,0:T(8,128)(2,1)S(1)} all-to-all(bf16[4,128,128]{2,1,0:T(8,128)(2,1)S(1)} %shard_map.122), channel_id=1, replica_groups={{0,8,16,24},{32,40,48,56},{64,72,80,88},{96,104,112,120},{128,136,144,1..., dimensions={0} | all-to-all | bytes 262144 | tf_op jit(solution)/shard_map/all_to_all | solution.py:458
  89.9 0.0 copy-start.4
  89.9 1.6 %shard_map.123 = (f32[128,512]{1,0:T(8,128)S(1)}, bf16[128,128]{1,0:T(8,128)(2,1)S(1)}, f32[8,512]{1,0:T(8,128)S(1)}) custom-call(bf16[4,128,128]{2,1,0:T(8,128)(2,1)S(1)} %all_to_all.22.states_ref, f32[128,512]{1,0:T(8,128)S(1)} %get-tuple-element.30.pre_ref, f32[2,128,128]{2,1,0:T(8,128)S(1)} %get-tuple-element.31.unit_ref, ...), custom_call_target="tpu_custom_call" | custom-call | tf_op jit(solution)/shard_map/pallas_call | solution.py:428
  91.5 1.3 %collective-permute-start.4 = (f32[8,512]{1,0:T(8,128)S(1)}, f32[8,512]{1,0:T(8,128)S(1)}, u32[]{:S(2)}, u32[]{:S(2)}) collective-permute-start(f32[8,512]{1,0:T(8,128)S(1)} %get-tuple-element.41), channel_id=1, source_target_pairs={{8,0},{16,8},{24,16},{32,24},{40,32},{48,40},{56,48},{64,56},{72,6... | collective-permute-start | bytes 49160 | tf_op jit(solution)/shard_map/ppermute | solution.py:477
  92.8 3.5 %collective-permute-done.4.halo_ref = f32[8,512]{1,0:T(8,128)S(1)} collective-permute-done((f32[8,512]{1,0:T(8,128)S(1)}, f32[8,512]{1,0:T(8,128)S(1)}, u32[]{:S(2)}, u32[]{:S(2)}) %collective-permute-start.4) | collective-permute-done | bytes 16416 | tf_op jit(solution)/shard_map/ppermute | solution.py:477
  96.3 0.0 copy-done.1
  96.3 0.0 copy-done.4
  96.3 1.0 shard_map.124
  97.4 21.0 %all_to_all.23 = bf16[8,128,256]{2,1,0:T(8,128)(2,1)S(1)} all-to-all(bf16[8,128,256]{2,1,0:T(8,128)(2,1)S(1)} %shard_map.124), channel_id=1, replica_groups=mesh['ctx'=64,'tp'=8] {'tp'}, dimensions={0} | all-to-all | bytes 1048576 | tf_op jit(solution)/shard_map/all_to_all | solution.py:479
  118.4 0.7 reduce_sum.12
Async XLA Ops:
  0.0 20.2 %copy-start.2 = (bf16[2048,128]{1,0:T(8,128)(2,1)S(1)}, bf16[2048,128]{1,0:T(8,128)(2,1)}, u32[]{:S(2)}) copy-start(bf16[2048,128]{1,0:T(8,128)(2,1)} %wq_ref.3) | copy-start | bytes 1572868
  0.0 20.2 %copy-start.6 = (bf16[2048,2]{0,1:T(2,128)(2,1)S(1)}, bf16[2048,2]{0,1:T(2,128)(2,1)}, u32[]{:S(2)}) copy-start(bf16[2048,2]{0,1:T(2,128)(2,1)} %param.16) | copy-start | bytes 24580
  0.0 20.2 %copy-start.7 = (bf16[2048,2]{0,1:T(2,128)(2,1)S(1)}, bf16[2048,2]{0,1:T(2,128)(2,1)}, u32[]{:S(2)}) copy-start(bf16[2048,2]{0,1:T(2,128)(2,1)} %param.17) | copy-start | bytes 24580
  20.2 1.2 %copy-start = (bf16[2048,256]{1,0:T(8,128)(2,1)S(1)}, bf16[2048,256]{1,0:T(8,128)(2,1)}, u32[]{:S(2)}) copy-start(bf16[2048,256]{1,0:T(8,128)(2,1)} %wv_ref.3) | copy-start | bytes 3145732
  21.4 1.0 copy-start.3
  22.4 3.8 %copy-start.5 = (bf16[128,256]{1,0:T(8,128)(2,1)S(1)}, bf16[128,256]{1,0:T(8,128)(2,1)}, u32[]{:S(2)}) copy-start(bf16[128,256]{1,0:T(8,128)(2,1)} %grad_ref.3) | copy-start | bytes 196612
  22.4 3.8 %copy-start.10 = (bf16[4,128]{1,0:T(4,128)(2,1)S(1)}, bf16[4,128]{1,0:T(4,128)(2,1)}, u32[]{:S(2)}) copy-start(bf16[4,128]{1,0:T(4,128)(2,1)} %fk_ref.3) | copy-start | bytes 3076
  22.4 3.8 %copy-start.12 = (f32[2]{0:T(128)S(1)}, f32[2]{0:T(128)}, u32[]{:S(2)}) copy-start(f32[2]{0:T(128)} %param.22) | copy-start | bytes 28
  24.1 2.1 %collective-permute-start = (bf16[16,512]{1,0:T(8,128)(2,1)S(1)}, bf16[16,512]{1,0:T(8,128)(2,1)S(1)}, u32[]{:S(2)}, u32[]{:S(2)}) collective-permute-start(bf16[16,512]{1,0:T(8,128)(2,1)S(1)} %get-tuple-element.25), channel_id=1, source_target_pairs={{0,8},{8,16},{16,24},{24,32},{32,40},{40,48},{48,56},{56,64},{64,7... | collective-permute-start | bytes 49160 | tf_op jit(solution)/shard_map/ppermute | solution.py:466
  26.2 0.7 copy-start.8
  26.2 0.7 copy-start.9
  26.2 0.7 copy-start.11
  43.2 22.7 %collective-permute-start.3 = (bf16[272,128]{1,0:T(8,128)(2,1)S(1)}, bf16[272,128]{1,0:T(8,128)(2,1)S(1)}, u32[]{:S(2)}, u32[]{:S(2)}) collective-permute-start(bf16[272,128]{1,0:T(8,128)(2,1)S(1)} %shard_map.120.total_ref), channel_id=1, source_target_pairs={{0,96},{16,112},{32,128},{48,144},{64,160},{80,176},{96,192},{104,... | collective-permute-start | bytes 208904 | tf_op jit(solution)/shard_map/ppermute | solution.py:462
  52.7 13.2 %collective-permute-start.2 = (bf16[272,128]{1,0:T(8,128)(2,1)S(1)}, bf16[272,128]{1,0:T(8,128)(2,1)S(1)}, u32[]{:S(2)}, u32[]{:S(2)}) collective-permute-start(bf16[272,128]{1,0:T(8,128)(2,1)S(1)} %shard_map.120.total_ref), channel_id=1, source_target_pairs={{0,64},{16,80},{32,96},{48,112},{64,128},{72,8},{80,144},{88,24},{... | collective-permute-start | bytes 208904 | tf_op jit(solution)/shard_map/ppermute | solution.py:462
  60.1 7.2 %collective-permute-start.1 = (bf16[272,128]{1,0:T(8,128)(2,1)S(1)}, bf16[272,128]{1,0:T(8,128)(2,1)S(1)}, u32[]{:S(2)}, u32[]{:S(2)}) collective-permute-start(bf16[272,128]{1,0:T(8,128)(2,1)S(1)} %shard_map.120.total_ref), channel_id=1, source_target_pairs={{0,32},{16,48},{32,64},{40,8},{48,80},{56,24},{64,96},{72,40},{80,... | collective-permute-start | bytes 208904 | tf_op jit(solution)/shard_map/ppermute | solution.py:462
  80.9 15.4 %copy-start.1 = (bf16[2048,256]{1,0:T(8,128)(2,1)S(1)}, bf16[2048,256]{1,0:T(8,128)(2,1)}, u32[]{:S(2)}) copy-start(bf16[2048,256]{1,0:T(8,128)(2,1)} %wv_ref.3) | copy-start | bytes 3145732
  89.9 6.5 %copy-start.4 = (bf16[2048,128]{1,0:T(8,128)(2,1)S(1)}, bf16[2048,128]{1,0:T(8,128)(2,1)}, u32[]{:S(2)}) copy-start(bf16[2048,128]{1,0:T(8,128)(2,1)} %wk_ref.3) | copy-start | bytes 1572868
  91.5 4.8 %collective-permute-start.4 = (f32[8,512]{1,0:T(8,128)S(1)}, f32[8,512]{1,0:T(8,128)S(1)}, u32[]{:S(2)}, u32[]{:S(2)}) collective-permute-start(f32[8,512]{1,0:T(8,128)S(1)} %get-tuple-element.41), channel_id=1, source_target_pairs={{8,0},{16,8},{24,16},{32,24},{40,32},{48,40},{56,48},{64,56},{72,6... | collective-permute-start | bytes 49160 | tf_op jit(solution)/shard_map/ppermute | solution.py:477

commit v4 on v3

--- a/solution.py
+++ b/solution.py
@@ -67,56 +67,73 @@
     return result
 
 
-def unit_lower_inverse(strict):
+def unit_lower_inverses(stricts):
     row, col = positions()
     identity = jnp.where(row == col, 1.0, 0.0).astype(F32)
-    inner = jnp.where(row // 8 == col // 8, strict, 0.0)
-    square = dot3(inner, inner)
-    result = dot3(identity - inner, identity + square)
-    result = dot3(result, identity + dot3(square, square))
+    inners = [jnp.where(row // 8 == col // 8, strict, 0.0) for strict in stricts]
+    squares = [dot3(inner, inner) for inner in inners]
+    results = [dot3(identity - inner, identity + square) for inner, square in zip(inners, squares)]
+    fourths = [dot3(square, square) for square in squares]
+    results = [dot3(result, identity + fourth) for result, fourth in zip(results, fourths)]
     size = 8
     while size < DH:
         off = (row // (2 * size) == col // (2 * size)) & (row // size != col // size)
-        result = result - dot3(dot3(result, jnp.where(off, strict, 0.0)), result)
+        products = [
+            dot3(result, jnp.where(off, strict, 0.0)) for result, strict in zip(results, stricts)
+        ]
+        results = [
+            result - dot3(product, result) for result, product in zip(results, products)
+        ]
         size *= 2
-    return result
+    return results
 
 
 def project_kernel(
-    x_ref, wq_ref, wk_ref, wv_ref, wb_ref, wa_ref, proj_ref, ba_ref, tail_ref, held_ref, sems
+    x_ref, wq_ref, wk_ref, wv_ref, wb_ref, wa_ref, fq_ref, fk_ref, fv_ref, decay_ref, bias_ref,
+    proj_ref, ba_ref, tail_ref, taps_ref, scales_ref, held_ref, narrow_ref, filter_ref, pair_ref,
+    sems,
 ):
     parts, _, width = x_ref.shape
     places = (slice(0, DH), slice(DH, 2 * DH), slice(2 * DH, 4 * DH))
     copies = []
+
+    def fetch(source, target):
+        copies.append(pltpu.make_async_copy(source, target, sems.at[len(copies)]))
+        copies[-1].start()
+
     for part in range(parts):
         span = slice(part * width, (part + 1) * width)
-        for place, weight in enumerate((wq_ref, wk_ref, wv_ref)):
-            copies.append(
-                pltpu.make_async_copy(
-                    weight.at[span, :], held_ref.at[span, places[place]], sems.at[part, place]
-                )
-            )
-            copies[-1].start()
+        for place, weight in zip(places, (wq_ref, wk_ref, wv_ref)):
+            fetch(weight.at[span, :], held_ref.at[span, place])
+    fetch(wb_ref, narrow_ref.at[0])
+    fetch(wa_ref, narrow_ref.at[1])
+    for place, taps in zip(places, (fq_ref, fk_ref, fv_ref)):
+        fetch(taps, filter_ref.at[:, place])
+    fetch(decay_ref, pair_ref.at[0])
+    fetch(bias_ref, pair_ref.at[1])
     total = jnp.zeros((DH, 4 * DH), F32)
+    for part in range(parts):
+        span = slice(part * width, (part + 1) * width)
+        for copy in copies[3 * part : 3 * part + 3]:
+            copy.wait()
+        total = total + dot(x_ref[part], held_ref[span, :])
+    for copy in copies[3 * parts :]:
+        copy.wait()
     beta = jnp.zeros((DH, 2), F32)
     alpha = jnp.zeros((DH, 2), F32)
     for part in range(parts):
-        rows = x_ref[part]
         span = slice(part * width, (part + 1) * width)
-        beta = beta + dot(rows, wb_ref[:, span], (1, 1))
-        alpha = alpha + dot(rows, wa_ref[:, span], (1, 1))
-        for copy in copies[3 * part : 3 * part + 3]:
-            copy.wait()
-        total = total + dot(rows, held_ref[span, :])
+        beta = beta + dot(x_ref[part], narrow_ref[0, :, span], (1, 1))
+        alpha = alpha + dot(x_ref[part], narrow_ref[1, :, span], (1, 1))
     proj_ref[...] = bf(total)
     tail_ref[...] = bf(total[DH - 16 :])
     ba_ref[...] = bf(lanes_of([beta[:, 0:1], beta[:, 1:2], alpha[:, 0:1], alpha[:, 1:2]]))
-
-
-def gate_rows(decay_ref, bias_ref):
-    rate = lanes_of([0.0, 0.0, -jnp.exp(decay_ref[:, 0:1]), -jnp.exp(decay_ref[:, 1:2])])
-    bias = lanes_of([0.0, 0.0, bias_ref[:, 0:1], bias_ref[:, 1:2]])
-    return rate, bias
+    taps_ref[0:CONV] = filter_ref[...].astype(F32)
+    taps_ref[CONV:] = jnp.zeros((8 - CONV, 4 * DH), F32)
+    decay = pair_ref[0]
+    bias = pair_ref[1]
+    scales_ref[0] = lanes_of([0.0, 0.0, -jnp.exp(decay[:, 0:1]), -jnp.exp(decay[:, 1:2])])
+    scales_ref[1] = lanes_of([0.0, 0.0, bias[:, 0:1], bias[:, 1:2]])
 
 
 def split_decay(value):
@@ -127,21 +144,31 @@
     return bf(jnp.where(row == 0, high, jnp.where(row == 1, middle, jnp.where(row == 2, low, 0.0))))
 
 
+def gate_kernel(ba_ref, scales_ref, cols_ref, gap_ref):
+    row, col = positions()
+    raw = ba_ref[...].astype(F32)
+    log_decay = scales_ref[0] * softplus(raw + scales_ref[1])
+    lower = jnp.where(row >= col, 1.0, 0.0).astype(F32)
+    cols = jnp.where(col < 2, sigmoid(raw), dot_exact(lower, log_decay))
+    cols_ref[...] = cols
+    rows = cols.T
+    for head in range(2):
+        between = cols[:, 2 + head : 3 + head] - rows[2 + head : 3 + head, :]
+        gap_ref[head] = jnp.where(row >= col, jnp.exp(jnp.where(row >= col, between, 0.0)), 0.0)
+
+
 def slab_kernel(
-    proj_ref, tail_ref, ba_ref, fq_ref, fk_ref, fv_ref, decay_ref, bias_ref, grad_ref,
-    send_ref, pre_ref, unit_ref, cols_ref, inverse_ref, mixed_ref, weighted_ref,
-    back_ref, gap_ref, gram_ref, cross_ref, pad_ref,
+    proj_ref, tail_ref, taps_ref, cols_ref, gap_ref, grad_ref,
+    send_ref, pre_ref, unit_ref, inverse_ref, mixed_ref, weighted_ref,
+    back_ref, gram_ref, cross_ref, pad_ref,
 ):
     row, col = positions()
     pad_ref[0:8] = tail_ref[8:16].astype(F32)
     pad_ref[8 : 8 + DH] = proj_ref[...].astype(F32)
-    taps = jnp.concatenate(
-        [fq_ref[...].astype(F32), fk_ref[...].astype(F32), fv_ref[...].astype(F32)], axis=1
-    )
     pre = jnp.zeros((DH, 4 * DH), F32)
     for tap in range(CONV):
         start = 8 - (CONV - 1) + tap
-        pre = pre + taps[tap : tap + 1] * pad_ref[start : start + DH]
+        pre = pre + taps_ref[tap : tap + 1] * pad_ref[start : start + DH]
     pre_ref[...] = pre
     act = pre * sigmoid(pre)
     query_act, key_act = act[:, :DH], act[:, DH : 2 * DH]
@@ -149,42 +176,40 @@
     key = key_act * lax.rsqrt(jnp.sum(key_act * key_act, 1, keepdims=True) + EPS)
     unit_ref[0] = query
     unit_ref[1] = key
-    raw = ba_ref[...].astype(F32)
-    rate, bias = gate_rows(decay_ref, bias_ref)
-    log_decay = rate * softplus(raw + bias)
-    lower = jnp.where(row >= col, 1.0, 0.0).astype(F32)
-    summed = dot_exact(lower, log_decay)
-    cols = jnp.where(col < 2, sigmoid(raw), summed)
-    cols_ref[...] = cols
-    rows = cols.T
+    cols = cols_ref[...]
     gram = dot3(key, key, (1, 1))
     cross = dot3(query, key, (1, 1))
     gram_ref[...] = gram
     cross_ref[...] = cross
+    betas = [cols[:, head : head + 1] for head in range(2)]
+    inverses = unit_lower_inverses(
+        [
+            jnp.where(row > col, beta * gram * gap_ref[head], 0.0)
+            for head, beta in enumerate(betas)
+        ]
+    )
     for head in range(2):
-        beta = cols[:, head : head + 1]
+        beta = betas[head]
+        inverse = inverses[head]
         cum = cols[:, 2 + head : 3 + head]
-        cum_row = rows[2 + head : 3 + head, :]
         value = act[:, (2 + head) * DH : (3 + head) * DH]
         grad = grad_ref[:, head * DH : (head + 1) * DH]
-        gap = jnp.where(row >= col, jnp.exp(jnp.where(row >= col, cum - cum_row, 0.0)), 0.0)
-        gap_ref[head] = gap
         gamma = jnp.exp(cum)
         last = cum[DH - 1 : DH, :]
         key_tail = jnp.exp(last - cum) * key
-        strict = jnp.where(row > col, beta * gram * gap, 0.0)
-        inverse = unit_lower_inverse(strict)
-        mixed = dot3(inverse, beta * value)
-        weighted = dot3(inverse, (beta * gamma) * key)
-        back = dot(cross * gap, grad, (0, 0))
+        both = dot3(inverse, jnp.concatenate([beta * value, (beta * gamma) * key], axis=1))
+        mixed = both[:, :DH]
+        weighted = both[:, DH:]
+        back = dot(cross * gap_ref[head], grad, (0, 0))
         inverse_ref[head] = bf(inverse)
         mixed_ref[head] = mixed
         weighted_ref[head] = bf(weighted)
         back_ref[head] = back
-        moved = dot(key_tail, weighted, (0, 0))
+        ahead = dot(key_tail, both, (0, 0))
+        moved = ahead[:, DH:]
         decay_rows = split_decay(jnp.exp(last))
         send_ref[2 * head, 0:DH] = bf(moved)
-        send_ref[2 * head, DH : 2 * DH] = bf(dot(key_tail, mixed, (0, 0)))
+        send_ref[2 * head, DH : 2 * DH] = bf(ahead[:, :DH])
         send_ref[2 * head, 2 * DH :] = decay_rows
         send_ref[2 * head + 1, 0:DH] = bf(moved.T)
         send_ref[2 * head + 1, DH : 2 * DH] = bf(
@@ -265,7 +290,7 @@
 
 def gradient_kernel(
     states_ref, pre_ref, unit_ref, cols_ref, ba_ref, inverse_ref, mixed_ref, weighted_ref,
-    back_ref, gap_ref, gram_ref, cross_ref, grad_ref, fq_ref, fk_ref, fv_ref, decay_ref, bias_ref,
+    back_ref, gap_ref, gram_ref, cross_ref, grad_ref, taps_ref, scales_ref,
     full_ref, gates_ref, halo_ref, pad_ref,
 ):
     row, col = positions()
@@ -330,7 +355,8 @@
         columns = jnp.where(row == 2 + head, jnp.sum(by_gap, 0, keepdims=True), columns)
         sides.append((grad_beta, grad_cum))
     raw = ba_ref[...].astype(F32)
-    rate, bias = gate_rows(decay_ref, bias_ref)
+    rate = scales_ref[0]
+    bias = scales_ref[1]
     sides = lanes_of([sides[0][0], sides[1][0], sides[0][1], sides[1][1]]) - columns.T
     upper = jnp.where(row <= col, 1.0, 0.0).astype(F32)
     grad_log = dot_exact(upper, sides)
@@ -357,13 +383,10 @@
     for place, piece in enumerate([grad_query, grad_key] + pieces):
         span = slice(place * DH, (place + 1) * DH)
         pad_ref[8 : 8 + DH, span] = piece * slope[:, span]
-    taps = jnp.concatenate(
-        [fq_ref[...].astype(F32), fk_ref[...].astype(F32), fv_ref[...].astype(F32)], axis=1
-    )
     total = jnp.zeros((8 + DH, 4 * DH), F32)
     for tap in range(CONV):
         start = CONV - 1 - tap
-        total = total + taps[tap : tap + 1] * pad_ref[start : start + 8 + DH]
+        total = total + taps_ref[tap : tap + 1] * pad_ref[start : start + 8 + DH]
     halo_ref[...] = total[0:8]
     full_ref[...] = total[8:]
 
@@ -395,43 +418,54 @@
     )
 
 
-def project(gathered, weights):
+def stay(array):
+    return pltpu.with_memory_space_constraint(array, pltpu.HBM)
+
+
+def project(gathered, weights, filters, decay, bias):
     parts = gathered.shape[0]
     inside = pl.BlockSpec(memory_space=pltpu.VMEM)
-    outside = pl.BlockSpec(memory_space=pl.ANY)
+    outside = pl.BlockSpec(memory_space=pltpu.HBM)
+    model = weights[0].shape[0]
     return call(
         project_kernel,
-        [((DH, 4 * DH), BF16), ((DH, DH), BF16), ((16, 4 * DH), BF16)],
         [
-            pltpu.VMEM((weights[0].shape[0], 4 * DH), BF16),
-            pltpu.SemaphoreType.DMA((parts, 3)),
+            ((DH, 4 * DH), BF16), ((DH, DH), BF16), ((16, 4 * DH), BF16), ((8, 4 * DH), F32),
+            ((2, DH, DH), F32),
         ],
-        [inside] + [outside] * 3 + [inside] * 2,
-    )(gathered, *weights)
-
-
-def slab(proj, tail, gates, filters, decay, bias, grad):
+        [
+            pltpu.VMEM((model, 4 * DH), BF16),
+            pltpu.VMEM((2, 2, model), BF16),
+            pltpu.VMEM((CONV, 4 * DH), BF16),
+            pltpu.VMEM((2, 1, 2), F32),
+            pltpu.SemaphoreType.DMA((3 * parts + 7,)),
+        ],
+        [inside] + [outside] * 10,
+    )(gathered, *[stay(array) for array in (*weights, *filters, decay, bias)])
+
+
+def slab(proj, tail, taps, cols, gap, grad):
     square = (DH, DH)
     return call(
         slab_kernel,
         [
-            ((4, PACK, DH), BF16), ((DH, 4 * DH), F32), ((2,) + square, F32), (square, F32),
+            ((4, PACK, DH), BF16), ((DH, 4 * DH), F32), ((2,) + square, F32),
             ((2,) + square, BF16), ((2,) + square, F32), ((2,) + square, BF16),
-            ((2,) + square, F32), ((2,) + square, F32), (square, F32), (square, F32),
+            ((2,) + square, F32), (square, F32), (square, F32),
         ],
         [pltpu.VMEM((8 + DH, 4 * DH), F32)],
-    )(proj, tail, gates, *filters, decay, bias, grad)
-
-
-def gradient(states, kept, gates, filters, decay, bias, grad):
-    pre, unit, cols, inverse, mixed, weighted, back, gap, gram, cross = kept
+    )(proj, tail, taps, cols, gap, grad)
+
+
+def gradient(states, kept, cols, gap, gates, taps, scales, grad):
+    pre, unit, inverse, mixed, weighted, back, gram, cross = kept
     return call(
         gradient_kernel,
         [((DH, 4 * DH), F32), ((DH, DH), BF16), ((8, 4 * DH), F32)],
         [pltpu.VMEM((16 + DH, 4 * DH), F32)],
     )(
         states, pre, unit, cols, gates, inverse, mixed, weighted, back, gap, gram, cross,
-        grad, *filters, decay, bias,
+        grad, taps, scales,
     )
 
 
@@ -462,9 +496,11 @@
         return lax.ppermute(value, "ctx", [(s, t) for s, t in steps if 0 <= t < count])
 
     gathered = lax.all_gather(inputs, "tp", axis=0)
-    proj, gates, tail = project(gathered, weights)
+    proj, gates, tail, taps, scales = project(gathered, weights, filters, decay, bias)
     tail = lax.ppermute(tail, "ctx", [(s, s + 1) for s in range(count - 1)])
-    send, *kept = slab(proj, tail, gates, filters, decay, bias, grad_core)
+    square = (DH, DH)
+    cols, gap = call(gate_kernel, [(square, F32), ((2,) + square, F32)])(gates, scales)
+    send, *kept = slab(proj, tail, taps, cols, gap, grad_core)
     got = exchange(send, group)
     total = call(group_kernel, [((PACK, DH), BF16)])(got)[0]
     earlier = [onward(total, RADIX * step) for step in range(1, RADIX)]
@@ -473,7 +509,9 @@
     )(total, *earlier)
     states = call(states_kernel, [((RADIX, DH, DH), BF16)])(exchange(total, rank), before, got)[0]
     states = exchange(states, group)
-    full, grad_gates, halo = gradient(states, kept, gates, filters, decay, bias, grad_core)
+    full, grad_gates, halo = gradient(
+        states, kept, cols, gap, gates, taps, scales, grad_core
+    )
     halo = lax.ppermute(halo, "ctx", [(s + 1, s) for s in range(count - 1)])
     shares = spread(full, halo, grad_gates, weights, parts)
     shares = lax.all_to_all(shares, "tp", 0, 0)

time: 120 us -> 116 us (0.967)
  local copies, waits for them, and re-layouts: 2.96 us -> 0.03 us
    unnamed x26 -> x12, local copies, waits for them, and re-layouts: 2.96 us -> 0.03 us
    pallas_call x1, Pallas kernels: 4.75 us -> 3.19 us  [slab(): call(slab_kernel, [((4, PACK, DH), BF16), ((DH, 4 * DH), F32), ((2,) + sq...]
where the time goes in v4:
time: 116 us; the launch traced here: 115 us
  blocking collectives  73.4 us (63%)
  starting transfers between devices  25.3 us (22%)
  Pallas kernels  10.6 us (9%)
  waiting for transfers between devices  5.36 us (5%)
    all_to_all x3, blocking collectives, exchange(): return lax.all_to_all(value, 'ctx', 0, 0, axis_index_groups=groups)  32.4 us
    ppermute x3, starting transfers between devices, onward(): lax.ppermute(value, 'ctx', [(s, t) for s, t in steps if 0 <= t < count])  22.7 us
    all_to_all x1, blocking collectives, local(): shares = lax.all_to_all(shares, 'tp', 0, 0)  21 us
    all_gather x1, blocking collectives, local(): gathered = lax.all_gather(inputs, 'tp', axis=0)  20 us
    ppermute x1, waiting for transfers between devices, local(): halo = lax.ppermute(halo, 'ctx', [(s + 1, s) for s in range(count - 1)])  3.58 us
    pallas_call x1, Pallas kernels, slab(): call(slab_kernel, [((4, PACK, DH), BF16), ((DH, 4 * DH), F32), ((2,) + sq...  3.19 us
    pallas_call x1, Pallas kernels, project(): call(project_kernel, [((DH, 4 * DH), BF16), ((DH, DH), BF16), ((16, 4 * D...  2.61 us
  transfers between devices with their start and end apart: 5, of which 3 were waited for; matrix products, arithmetic and copies ran while one was open for 0% of the time, Pallas kernels for 0%

profile of v4, /device:TPU:1, one launch (start us, length us, event | category | flops | bytes accessed | tf_op | source)
XLA Modules:
  0.0 115.5 jit_solution(8306083253089908754)
XLA Ops:
  0.0 20.0 %all-gather = bf16[1024,256]{1,0:T(8,128)(2,1)S(1)} all-gather(bf16[128,256]{1,0:T(8,128)(2,1)} %param.12), channel_id=2, replica_groups=mesh['ctx'=64,'tp'=8] {'tp'}, dimensions={0}, use_global_device_ids=true | all-gather | bytes 589824 | tf_op jit(solution)/shard_map/all_gather | solution.py:498
  20.0 2.6 %shard_map.118 = (bf16[128,512]{1,0:T(8,128)(2,1)S(1)}, bf16[128,128]{1,0:T(8,128)(2,1)S(1)}, bf16[16,512]{1,0:T(8,128)(2,1)S(1)}, f32[8,512]{1,0:T(8,128)S(1)}, f32[2,128,128]{2,1,0:T(8,128)S(1)}) custom-call(bf16[8,128,256]{2,1,0:T(8,128)(2,1)S(1)} %bitcast.5, bf16[2048,128]{1,0:T(8,128)(2,1)} %wq_ref.3, bf16[2048,128]{1,0:T(8,128)(2,1)} %wk_ref.3, ...), custom_call_target="tpu_custom_call" | custom-call | tf_op jit(solution)/shard_map/pallas_call | solution.py:430
  22.6 1.3 %collective-permute-start = (bf16[16,512]{1,0:T(8,128)(2,1)S(1)}, bf16[16,512]{1,0:T(8,128)(2,1)S(1)}, u32[]{:S(2)}, u32[]{:S(2)}) collective-permute-start(bf16[16,512]{1,0:T(8,128)(2,1)S(1)} %get-tuple-element.27), channel_id=1, source_target_pairs={{0,8},{8,16},{16,24},{24,32},{32,40},{40,48},{48,56},{56,64},{64,7... | collective-permute-start | bytes 49160 | tf_op jit(solution)/shard_map/ppermute | solution.py:500
  23.9 0.0 copy-start.3
  23.9 0.4 shard_map.119
  24.3 0.5 collective-permute-done.tail_ref
  24.8 0.0 copy-done.3
  24.8 3.2 %shard_map.120 = (bf16[4,272,128]{2,1,0:T(8,128)(2,1)S(1)}, f32[128,512]{1,0:T(8,128)S(1)}, f32[2,128,128]{2,1,0:T(8,128)S(1)}, bf16[2,128,128]{2,1,0:T(8,128)(2...) custom-call(bf16[128,512]{1,0:T(8,128)(2,1)S(1)} %get-tuple-element., ...), custom_call_target="tpu_custom_call" | custom-call | tf_op jit(solution)/shard_map/pallas_call | solution.py:449
  28.0 11.1 %all_to_all.20.got_ref.group_ref = bf16[4,272,128]{2,1,0:T(8,128)(2,1)S(1)} all-to-all(bf16[4,272,128]{2,1,0:T(8,128)(2,1)S(1)} %get-tuple-element.33), channel_id=1, replica_groups={{0,8,16,24},{32,40,48,56},{64,72,80,88},{96,104,112,120},{128,136,144,1..., dimensions={0} | all-to-all | bytes 557056 | tf_op jit(solution)/shard_map/all_to_all | solution.py:492
  39.1 0.4 shard_map.121.total_ref
  39.5 9.5 %collective-permute-start.3 = (bf16[272,128]{1,0:T(8,128)(2,1)S(1)}, bf16[272,128]{1,0:T(8,128)(2,1)S(1)}, u32[]{:S(2)}, u32[]{:S(2)}) collective-permute-start(bf16[272,128]{1,0:T(8,128)(2,1)S(1)} %shard_map.121.total_ref), channel_id=1, source_target_pairs={{0,96},{16,112},{32,128},{48,144},{64,160},{80,176},{96,192},{104,... | collective-permute-start | bytes 208904 | tf_op jit(solution)/shard_map/ppermute | solution.py:496
  49.0 7.3 %collective-permute-start.2 = (bf16[272,128]{1,0:T(8,128)(2,1)S(1)}, bf16[272,128]{1,0:T(8,128)(2,1)S(1)}, u32[]{:S(2)}, u32[]{:S(2)}) collective-permute-start(bf16[272,128]{1,0:T(8,128)(2,1)S(1)} %shard_map.121.total_ref), channel_id=1, source_target_pairs={{0,64},{16,80},{32,96},{48,112},{64,128},{72,8},{80,144},{88,24},{... | collective-permute-start | bytes 208904 | tf_op jit(solution)/shard_map/ppermute | solution.py:496
  56.4 5.9 %collective-permute-start.1 = (bf16[272,128]{1,0:T(8,128)(2,1)S(1)}, bf16[272,128]{1,0:T(8,128)(2,1)S(1)}, u32[]{:S(2)}, u32[]{:S(2)}) collective-permute-start(bf16[272,128]{1,0:T(8,128)(2,1)S(1)} %shard_map.121.total_ref), channel_id=1, source_target_pairs={{0,32},{16,48},{32,64},{40,8},{48,80},{56,24},{64,96},{72,40},{80,... | collective-permute-start | bytes 208904 | tf_op jit(solution)/shard_map/ppermute | solution.py:496
  62.2 0.0 collective-permute-done.3.first_ref
  62.2 0.0 collective-permute-done.2.middle_ref
  62.3 1.3 %collective-permute-done.1.last_ref = bf16[272,128]{1,0:T(8,128)(2,1)S(1)} collective-permute-done((bf16[272,128]{1,0:T(8,128)(2,1)S(1)}, bf16[272,128]{1,0:T(8,128)(2,1)S(1)}, u32[]{:S(2)}, u32[]{:S(2)}) %collective-permute-start.1) | collective-permute-done | bytes 69664 | tf_op jit(solution)/shard_map/ppermute | solution.py:496
  63.6 0.4 shard_map.122
  64.0 13.1 %all_to_all.21.rows_ref = bf16[4,272,128]{2,1,0:T(8,128)(2,1)S(1)} all-to-all(bf16[4,272,128]{2,1,0:T(8,128)(2,1)S(1)} %get-tuple-element.34), channel_id=1, replica_groups={{0,128,256,384},{8,136,264,392},{16,144,272,400},{24,152,280,408},{32,1..., dimensions={0} | all-to-all | bytes 557056 | tf_op jit(solution)/shard_map/all_to_all | solution.py:492
  77.1 0.0 copy-start.2
  77.1 0.9 shard_map.123
  78.1 0.0 copy-start
  78.1 8.2 %all_to_all.22.states_ref = bf16[4,128,128]{2,1,0:T(8,128)(2,1)S(1)} all-to-all(bf16[4,128,128]{2,1,0:T(8,128)(2,1)S(1)} %shard_map.123), channel_id=1, replica_groups={{0,8,16,24},{32,40,48,56},{64,72,80,88},{96,104,112,120},{128,136,144,1..., dimensions={0} | all-to-all | bytes 262144 | tf_op jit(solution)/shard_map/all_to_all | solution.py:492
  86.3 0.0 copy-start.1
  86.3 0.0 copy-start.4
  86.3 0.0 copy-start.5
  86.3 1.6 %shard_map.124 = (f32[128,512]{1,0:T(8,128)S(1)}, bf16[128,128]{1,0:T(8,128)(2,1)S(1)}, f32[8,512]{1,0:T(8,128)S(1)}) custom-call(bf16[4,128,128]{2,1,0:T(8,128)(2,1)S(1)} %all_to_all.22.states_ref, f32[128,512]{1,0:T(8,128)S(1)} %get-tuple-element.36.pre_ref, f32[2,128,128]{2,1,0:T(8,128)S(1)} %get-tuple-element.37.unit_ref, ...), custom_call_target="tpu_custom_call" | custom-call | tf_op jit(solution)/shard_map/pallas_call | solution.py:462
  87.9 1.3 %collective-permute-start.4 = (f32[8,512]{1,0:T(8,128)S(1)}, f32[8,512]{1,0:T(8,128)S(1)}, u32[]{:S(2)}, u32[]{:S(2)}) collective-permute-start(f32[8,512]{1,0:T(8,128)S(1)} %get-tuple-element.45), channel_id=1, source_target_pairs={{8,0},{16,8},{24,16},{32,24},{40,32},{48,40},{56,48},{64,56},{72,6... | collective-permute-start | bytes 49160 | tf_op jit(solution)/shard_map/ppermute | solution.py:515
  89.2 3.6 %collective-permute-done.4.halo_ref = f32[8,512]{1,0:T(8,128)S(1)} collective-permute-done((f32[8,512]{1,0:T(8,128)S(1)}, f32[8,512]{1,0:T(8,128)S(1)}, u32[]{:S(2)}, u32[]{:S(2)}) %collective-permute-start.4) | collective-permute-done | bytes 16416 | tf_op jit(solution)/shard_map/ppermute | solution.py:515
  92.7 0.0 copy-done.2
  92.7 0.0 copy-done
  92.7 0.0 copy-done.1
  92.7 0.0 copy-done.4
  92.7 0.0 copy-done.5
  92.8 1.1 shard_map.125
  93.8 21.0 %all_to_all.23 = bf16[8,128,256]{2,1,0:T(8,128)(2,1)S(1)} all-to-all(bf16[8,128,256]{2,1,0:T(8,128)(2,1)S(1)} %shard_map.125), channel_id=1, replica_groups=mesh['ctx'=64,'tp'=8] {'tp'}, dimensions={0} | all-to-all | bytes 1048576 | tf_op jit(solution)/shard_map/all_to_all | solution.py:517
  114.8 0.7 reduce_sum.12
Async XLA Ops:
  22.6 2.1 %collective-permute-start = (bf16[16,512]{1,0:T(8,128)(2,1)S(1)}, bf16[16,512]{1,0:T(8,128)(2,1)S(1)}, u32[]{:S(2)}, u32[]{:S(2)}) collective-permute-start(bf16[16,512]{1,0:T(8,128)(2,1)S(1)} %get-tuple-element.27), channel_id=1, source_target_pairs={{0,8},{8,16},{16,24},{24,32},{32,40},{40,48},{48,56},{56,64},{64,7... | collective-permute-start | bytes 49160 | tf_op jit(solution)/shard_map/ppermute | solution.py:500
  23.9 0.9 copy-start.3
  39.5 22.7 %collective-permute-start.3 = (bf16[272,128]{1,0:T(8,128)(2,1)S(1)}, bf16[272,128]{1,0:T(8,128)(2,1)S(1)}, u32[]{:S(2)}, u32[]{:S(2)}) collective-permute-start(bf16[272,128]{1,0:T(8,128)(2,1)S(1)} %shard_map.121.total_ref), channel_id=1, source_target_pairs={{0,96},{16,112},{32,128},{48,144},{64,160},{80,176},{96,192},{104,... | collective-permute-start | bytes 208904 | tf_op jit(solution)/shard_map/ppermute | solution.py:496
  49.0 13.2 %collective-permute-start.2 = (bf16[272,128]{1,0:T(8,128)(2,1)S(1)}, bf16[272,128]{1,0:T(8,128)(2,1)S(1)}, u32[]{:S(2)}, u32[]{:S(2)}) collective-permute-start(bf16[272,128]{1,0:T(8,128)(2,1)S(1)} %shard_map.121.total_ref), channel_id=1, source_target_pairs={{0,64},{16,80},{32,96},{48,112},{64,128},{72,8},{80,144},{88,24},{... | collective-permute-start | bytes 208904 | tf_op jit(solution)/shard_map/ppermute | solution.py:496
  56.4 7.2 %collective-permute-start.1 = (bf16[272,128]{1,0:T(8,128)(2,1)S(1)}, bf16[272,128]{1,0:T(8,128)(2,1)S(1)}, u32[]{:S(2)}, u32[]{:S(2)}) collective-permute-start(bf16[272,128]{1,0:T(8,128)(2,1)S(1)} %shard_map.121.total_ref), channel_id=1, source_target_pairs={{0,32},{16,48},{32,64},{40,8},{48,80},{56,24},{64,96},{72,40},{80,... | collective-permute-start | bytes 208904 | tf_op jit(solution)/shard_map/ppermute | solution.py:496
  77.1 15.6 %copy-start.2 = (bf16[2048,128]{1,0:T(8,128)(2,1)S(1)}, bf16[2048,128]{1,0:T(8,128)(2,1)}, u32[]{:S(2)}) copy-start(bf16[2048,128]{1,0:T(8,128)(2,1)} %wk_ref.3) | copy-start | bytes 1572868
  78.1 14.7 %copy-start = (bf16[2048,256]{1,0:T(8,128)(2,1)S(1)}, bf16[2048,256]{1,0:T(8,128)(2,1)}, u32[]{:S(2)}) copy-start(bf16[2048,256]{1,0:T(8,128)(2,1)} %wv_ref.3) | copy-start | bytes 3145732
  86.3 6.5 %copy-start.1 = (bf16[2048,128]{1,0:T(8,128)(2,1)S(1)}, bf16[2048,128]{1,0:T(8,128)(2,1)}, u32[]{:S(2)}) copy-start(bf16[2048,128]{1,0:T(8,128)(2,1)} %wq_ref.3) | copy-start | bytes 1572868
  86.3 6.5 %copy-start.4 = (bf16[2048,2]{0,1:T(2,128)(2,1)S(1)}, bf16[2048,2]{0,1:T(2,128)(2,1)}, u32[]{:S(2)}) copy-start(bf16[2048,2]{0,1:T(2,128)(2,1)} %param.16) | copy-start | bytes 24580
  86.3 6.5 %copy-start.5 = (bf16[2048,2]{0,1:T(2,128)(2,1)S(1)}, bf16[2048,2]{0,1:T(2,128)(2,1)}, u32[]{:S(2)}) copy-start(bf16[2048,2]{0,1:T(2,128)(2,1)} %param.17) | copy-start | bytes 24580
  87.9 4.9 %collective-permute-start.4 = (f32[8,512]{1,0:T(8,128)S(1)}, f32[8,512]{1,0:T(8,128)S(1)}, u32[]{:S(2)}, u32[]{:S(2)}) collective-permute-start(f32[8,512]{1,0:T(8,128)S(1)} %get-tuple-element.45), channel_id=1, source_target_pairs={{8,0},{16,8},{24,16},{32,24},{40,32},{48,40},{56,48},{64,56},{72,6... | collective-permute-start | bytes 49160 | tf_op jit(solution)/shard_map/ppermute | solution.py:515

commit v5 on v4

--- a/solution.py
+++ b/solution.py
@@ -88,12 +88,31 @@
     return results
 
 
-def project_kernel(
+def core_place():
+    return lax.axis_index("tp") % 2
+
+
+def part_span(part, core, width):
+    return pl.ds(pl.multiple_of((2 * part + core) * width, width), width)
+
+
+def narrow_sums(x_ref, narrow_ref, core):
+    parts, _, width = x_ref.shape
+    beta = jnp.zeros((DH, 2), F32)
+    alpha = jnp.zeros((DH, 2), F32)
+    for part in range(parts):
+        span = part_span(part, core, width)
+        beta = beta + dot(x_ref[part], narrow_ref[0, :, span], (1, 1))
+        alpha = alpha + dot(x_ref[part], narrow_ref[1, :, span], (1, 1))
+    return lanes_of([beta[:, 0:1], beta[:, 1:2], alpha[:, 0:1], alpha[:, 1:2]])
+
+
+def first_project_kernel(
     x_ref, wq_ref, wk_ref, wv_ref, wb_ref, wa_ref, fq_ref, fk_ref, fv_ref, decay_ref, bias_ref,
-    proj_ref, ba_ref, tail_ref, taps_ref, scales_ref, held_ref, narrow_ref, filter_ref, pair_ref,
-    sems,
+    total_ref, gates_ref, taps_ref, scales_ref, rest_ref, narrow_ref,
+    held_ref, filter_ref, pair_ref, sems,
 ):
-    parts, _, width = x_ref.shape
+    core = core_place()
     places = (slice(0, DH), slice(DH, 2 * DH), slice(2 * DH, 4 * DH))
     copies = []
 
@@ -101,39 +120,43 @@
         copies.append(pltpu.make_async_copy(source, target, sems.at[len(copies)]))
         copies[-1].start()
 
-    for part in range(parts):
-        span = slice(part * width, (part + 1) * width)
-        for place, weight in zip(places, (wq_ref, wk_ref, wv_ref)):
-            fetch(weight.at[span, :], held_ref.at[span, place])
+    for place, weight in zip(places, (wq_ref, wk_ref, wv_ref)):
+        fetch(weight.at[:, core], held_ref.at[:, :, place])
     fetch(wb_ref, narrow_ref.at[0])
     fetch(wa_ref, narrow_ref.at[1])
     for place, taps in zip(places, (fq_ref, fk_ref, fv_ref)):
         fetch(taps, filter_ref.at[:, place])
     fetch(decay_ref, pair_ref.at[0])
     fetch(bias_ref, pair_ref.at[1])
+    ready = len(copies)
+    for place, weight in zip(places, (wq_ref, wk_ref, wv_ref)):
+        fetch(weight.at[:, 1 - core], rest_ref.at[:, :, place])
+    for copy in copies[:ready]:
+        copy.wait()
     total = jnp.zeros((DH, 4 * DH), F32)
-    for part in range(parts):
-        span = slice(part * width, (part + 1) * width)
-        for copy in copies[3 * part : 3 * part + 3]:
-            copy.wait()
-        total = total + dot(x_ref[part], held_ref[span, :])
-    for copy in copies[3 * parts :]:
-        copy.wait()
-    beta = jnp.zeros((DH, 2), F32)
-    alpha = jnp.zeros((DH, 2), F32)
-    for part in range(parts):
-        span = slice(part * width, (part + 1) * width)
-        beta = beta + dot(x_ref[part], narrow_ref[0, :, span], (1, 1))
-        alpha = alpha + dot(x_ref[part], narrow_ref[1, :, span], (1, 1))
-    proj_ref[...] = bf(total)
-    tail_ref[...] = bf(total[DH - 16 :])
-    ba_ref[...] = bf(lanes_of([beta[:, 0:1], beta[:, 1:2], alpha[:, 0:1], alpha[:, 1:2]]))
+    for part in range(x_ref.shape[0]):
+        total = total + dot(x_ref[part], held_ref[part])
+    total_ref[...] = total
+    gates_ref[...] = narrow_sums(x_ref, narrow_ref, core)
     taps_ref[0:CONV] = filter_ref[...].astype(F32)
     taps_ref[CONV:] = jnp.zeros((8 - CONV, 4 * DH), F32)
     decay = pair_ref[0]
     bias = pair_ref[1]
     scales_ref[0] = lanes_of([0.0, 0.0, -jnp.exp(decay[:, 0:1]), -jnp.exp(decay[:, 1:2])])
     scales_ref[1] = lanes_of([0.0, 0.0, bias[:, 0:1], bias[:, 1:2]])
+    for copy in copies[ready:]:
+        copy.wait()
+
+
+def second_project_kernel(
+    x_ref, total_ref, part_ref, rest_ref, narrow_ref, proj_ref, ba_ref, tail_ref
+):
+    total = total_ref[...]
+    for part in range(x_ref.shape[0]):
+        total = total + dot(x_ref[part], rest_ref[part])
+    proj_ref[...] = bf(total)
+    tail_ref[...] = bf(total[DH - 16 :])
+    ba_ref[...] = bf(part_ref[...] + narrow_sums(x_ref, narrow_ref, 1 - core_place()))
 
 
 def split_decay(value):
@@ -391,20 +414,28 @@
     full_ref[...] = total[8:]
 
 
-def spread_kernel(full_ref, halo_ref, gates_ref, wq_ref, wk_ref, wv_ref, wb_ref, wa_ref, out_ref):
+def spread_kernel(
+    other, full_ref, halo_ref, gates_ref, wq_ref, wk_ref, wv_ref, wb_ref, wa_ref, out_ref
+):
+    core = core_place()
+    core = 1 - core if other else core
     full = full_ref[...]
     end = full[DH - 8 :] + halo_ref[...]
     grads = bf(jnp.concatenate([full[: DH - 8], end], axis=0))
     gates = gates_ref[...]
-    width = out_ref.shape[2]
-    for part in range(out_ref.shape[0]):
-        span = slice(part * width, (part + 1) * width)
+    parts, _, width = out_ref.shape
+    for part in range(parts):
+        span = part_span(part, core, width)
         total = dot(grads[:, :DH], wq_ref[span, :], (1, 1))
         total = total + dot(grads[:, DH : 2 * DH], wk_ref[span, :], (1, 1))
         total = total + dot(grads[:, 2 * DH :], wv_ref[span, :], (1, 1))
         total = total + dot(gates[:, 0:2], wb_ref[:, span])
         total = total + dot(gates[:, 2:4], wa_ref[:, span])
-        out_ref[part] = bf(total)
+        out_ref[part] = total.astype(out_ref.dtype)
+
+
+def merge_kernel(kept_ref, got_ref, out_ref):
+    out_ref[...] = bf(kept_ref[...] + got_ref[...].astype(F32))
 
 
 def call(kernel, outs, scratch=(), specs=None):
@@ -422,26 +453,33 @@
     return pltpu.with_memory_space_constraint(array, pltpu.HBM)
 
 
-def project(gathered, weights, filters, decay, bias):
-    parts = gathered.shape[0]
+def first_project(mine, weights, filters, decay, bias):
+    parts, rows, width = mine.shape
     inside = pl.BlockSpec(memory_space=pltpu.VMEM)
     outside = pl.BlockSpec(memory_space=pltpu.HBM)
-    model = weights[0].shape[0]
+    model = 2 * parts * width
+    wide = [weight.reshape(parts, 2, width, weight.shape[1]) for weight in weights[:3]]
     return call(
-        project_kernel,
+        first_project_kernel,
         [
-            ((DH, 4 * DH), BF16), ((DH, DH), BF16), ((16, 4 * DH), BF16), ((8, 4 * DH), F32),
-            ((2, DH, DH), F32),
+            ((rows, 4 * DH), F32), ((DH, DH), F32), ((8, 4 * DH), F32), ((2, DH, DH), F32),
+            ((parts, width, 4 * DH), BF16), ((2, 2, model), BF16),
         ],
         [
-            pltpu.VMEM((model, 4 * DH), BF16),
-            pltpu.VMEM((2, 2, model), BF16),
+            pltpu.VMEM((parts, width, 4 * DH), BF16),
             pltpu.VMEM((CONV, 4 * DH), BF16),
             pltpu.VMEM((2, 1, 2), F32),
-            pltpu.SemaphoreType.DMA((3 * parts + 7,)),
+            pltpu.SemaphoreType.DMA((13,)),
         ],
         [inside] + [outside] * 10,
-    )(gathered, *[stay(array) for array in (*weights, *filters, decay, bias)])
+    )(mine, *[stay(array) for array in (*wide, *weights[3:], *filters, decay, bias)])
+
+
+def second_project(other, total, part, rest, narrow):
+    return call(
+        second_project_kernel,
+        [((DH, 4 * DH), BF16), ((DH, DH), BF16), ((16, 4 * DH), BF16)],
+    )(other, total, part, rest, narrow)
 
 
 def slab(proj, tail, taps, cols, gap, grad):
@@ -469,9 +507,12 @@
     )
 
 
-def spread(full, halo, gates, weights, parts):
-    width = weights[0].shape[0] // parts
-    return call(spread_kernel, [((parts, DH, width), BF16)])(full, halo, gates, *weights)[0]
+def spread(full, halo, gates, weights, parts, other):
+    width = weights[0].shape[0] // (2 * parts)
+    return call(
+        functools.partial(spread_kernel, other),
+        [((parts, DH, width), BF16 if other else F32)],
+    )(full, halo, gates, *weights)[0]
 
 
 def local(
@@ -495,8 +536,18 @@
         steps = [(s, s - distance if s % 2 else s + distance) for s in slabs]
         return lax.ppermute(value, "ctx", [(s, t) for s, t in steps if 0 <= t < count])
 
-    gathered = lax.all_gather(inputs, "tp", axis=0)
-    proj, gates, tail, taps, scales = project(gathered, weights, filters, decay, bias)
+    chips = [[2 * chip + core for chip in range(parts // 2)] for core in range(2)]
+
+    def across(value):
+        return lax.all_to_all(value, "tp", 0, 0, axis_index_groups=chips)
+
+    def between(value):
+        return lax.ppermute(value, "tp", [(t, t ^ 1) for t in range(parts)])
+
+    mine = across(jnp.broadcast_to(inputs[None], (parts // 2,) + inputs.shape))
+    other = between(mine)
+    total, part, taps, scales, rest, narrow = first_project(mine, weights, filters, decay, bias)
+    proj, gates, tail = second_project(other, total, part, rest, narrow)
     tail = lax.ppermute(tail, "ctx", [(s, s + 1) for s in range(count - 1)])
     square = (DH, DH)
     cols, gap = call(gate_kernel, [(square, F32), ((2,) + square, F32)])(gates, scales)
@@ -513,9 +564,10 @@
         states, kept, cols, gap, gates, taps, scales, grad_core
     )
     halo = lax.ppermute(halo, "ctx", [(s + 1, s) for s in range(count - 1)])
-    shares = spread(full, halo, grad_gates, weights, parts)
-    shares = lax.all_to_all(shares, "tp", 0, 0)
-    return jnp.sum(shares.astype(F32), axis=0).astype(BF16)
+    given = between(spread(full, halo, grad_gates, weights, parts // 2, True))
+    kept = spread(full, halo, grad_gates, weights, parts // 2, False)
+    shares = call(merge_kernel, [(given.shape, BF16)])(kept, given)[0]
+    return jnp.sum(across(shares).astype(F32), axis=0).astype(BF16)
 
 
 def solution(mesh):

time: 116 us -> 114 us (0.983)
  blocking collectives: 73.4 us -> 51.2 us
  starting transfers between devices: 25.3 us -> 42.4 us
  waiting for transfers between devices: 5.36 us -> 7.74 us
    all_gather x1 -> x0, blocking collectives: 20 us -> none  [local(): gathered = lax.all_gather(inputs, 'tp', axis=0)]
    ppermute x0 -> x2, starting transfers between devices: none -> 17.1 us  [between(): return lax.ppermute(value, 'tp', [(t, t ^ 1) for t in range(parts)])]
    ppermute x3, waiting for transfers between devices: 1.33 us -> 3.58 us  [onward(): lax.ppermute(value, 'ctx', [(s, t) for s, t in steps if 0 <= t < count])]
    all_to_all x1 -> x2, blocking collectives: 21 us -> 19 us  [across(): return lax.all_to_all(value, 'tp', 0, 0, axis_index_groups=chips)]
    pallas_call x2 -> x5, Pallas kernels: 3.66 us -> 3.75 us  [the longest x1 1.93 us: first_project(): call(first_project_kernel, [((rows, 4 * DH), F32), ((DH, DH), F32), ((8,...]
  transfers between devices with their start and end apart: 5 -> 7, of which waited for: 3 -> 4; matrix products, arithmetic and copies ran while one was open for 0% -> 0% of each run, Pallas kernels for 0% -> 3%
where the time goes in v5:
time: 114 us
  blocking collectives  51.2 us (45%)
  starting transfers between devices  42.4 us (37%)
  Pallas kernels  10.7 us (9%)
  waiting for transfers between devices  7.74 us (7%)
    all_to_all x3, blocking collectives, exchange(): return lax.all_to_all(value, 'ctx', 0, 0, axis_index_groups=groups)  32.3 us
    ppermute x3, starting transfers between devices, onward(): lax.ppermute(value, 'ctx', [(s, t) for s, t in steps if 0 <= t < count])  22.7 us
    all_to_all x2, blocking collectives, across(): return lax.all_to_all(value, 'tp', 0, 0, axis_index_groups=chips)  19 us
    ppermute x2, starting transfers between devices, between(): return lax.ppermute(value, 'tp', [(t, t ^ 1) for t in range(parts)])  17.1 us
    ppermute x3, waiting for transfers between devices, onward(): lax.ppermute(value, 'ctx', [(s, t) for s, t in steps if 0 <= t < count])  3.58 us
    pallas_call x1, Pallas kernels, slab(): call(slab_kernel, [((4, PACK, DH), BF16), ((DH, 4 * DH), F32), ((2,) + sq...  3.19 us
    ppermute x1, waiting for transfers between devices, local(): halo = lax.ppermute(halo, 'ctx', [(s + 1, s) for s in range(count - 1)])  3.18 us
  transfers between devices with their start and end apart: 7, of which 4 were waited for; matrix products, arithmetic and copies ran while one was open for 0% of the time, Pallas kernels for 3%

profile of v5, /device:TPU:1, one launch (start us, length us, event | category | flops | bytes accessed | tf_op | source)
XLA Modules:
  0.0 113.8 jit_solution(17243592461194021639)
XLA Ops:
  0.0 0.9 broadcast_in_dim.2
  0.9 10.2 %all_to_all.25.x_ref = bf16[4,128,256]{2,1,0:T(8,128)(2,1)S(1)} all-to-all(bf16[4,128,256]{2,1,0:T(8,128)(2,1)S(1)} %broadcast_in_dim.2), channel_id=1, replica_groups={{0,2,4,6},{1,3,5,7},{8,10,12,14},{9,11,13,15},{16,18,20,22},{17,19,21,2..., dimensions={0} | all-to-all | bytes 524288 | tf_op jit(solution)/shard_map/all_to_all | solution.py:542
  11.0 7.7 %collective-permute-start = (bf16[4,128,256]{2,1,0:T(8,128)(2,1)S(1)}, bf16[4,128,256]{2,1,0:T(8,128)(2,1)S(1)}, u32[]{:S(2)}, u32[]{:S(2)}) collective-permute-start(bf16[4,128,256]{2,1,0:T(8,128)(2,1)S(1)} %all_to_all.25.x_ref), channel_id=1, source_target_pairs={{0,1},{1,0},{2,3},{3,2},{4,5},{5,4},{6,7},{7,6},{8,9},{9,8},{10,11... | collective-permute-start | bytes 786440 | tf_op jit(solution)/shard_map/ppermute | solution.py:545
  18.7 1.9 %shard_map.118 = (f32[128,512]{1,0:T(8,128)S(1)}, f32[128,128]{1,0:T(8,128)S(1)}, f32[8,512]{1,0:T(8,128)S(1)}, f32[2,128,128]{2,1,0:T(8,128)S(1)}, bf16[4,256,5...) custom-call(bf16[4,128,256]{2,1,0:T(8,128)(2,1)S(1)} %all_to_all.25.x_ref, bf16[4,2,256,128]{3,2,1,0:T(8,128)(2,1)} %bitcast.8, ...), custom_call_target="tpu_custom_call" | custom-call | tf_op jit(solution)/shard_map/pallas_call | solution.py:462
  20.6 0.0 collective-permute-done.x_ref
  20.7 0.6 shard_map.119
  21.2 1.3 %collective-permute-start.1 = (bf16[16,512]{1,0:T(8,128)(2,1)S(1)}, bf16[16,512]{1,0:T(8,128)(2,1)S(1)}, u32[]{:S(2)}, u32[]{:S(2)}) collective-permute-start(bf16[16,512]{1,0:T(8,128)(2,1)S(1)} %get-tuple-element.35), channel_id=1, source_target_pairs={{0,8},{8,16},{16,24},{24,32},{32,40},{40,48},{48,56},{56,64},{64,7... | collective-permute-start | bytes 49160 | tf_op jit(solution)/shard_map/ppermute | solution.py:551
  22.5 0.0 copy-start.3
  22.5 0.4 shard_map.120
  22.9 0.5 collective-permute-done.1.tail_ref
  23.4 0.0 copy-done.3
  23.4 3.2 %shard_map.121 = (bf16[4,272,128]{2,1,0:T(8,128)(2,1)S(1)}, f32[128,512]{1,0:T(8,128)S(1)}, f32[2,128,128]{2,1,0:T(8,128)S(1)}, bf16[2,128,128]{2,1,0:T(8,128)(2...) custom-call(bf16[128,512]{1,0:T(8,128)(2,1)S(1)} %get-tuple-element., ...), custom_call_target="tpu_custom_call" | custom-call | tf_op jit(solution)/shard_map/pallas_call | solution.py:487
  26.6 12.3 %all_to_all.26.got_ref.group_ref = bf16[4,272,128]{2,1,0:T(8,128)(2,1)S(1)} all-to-all(bf16[4,272,128]{2,1,0:T(8,128)(2,1)S(1)} %get-tuple-element.41), channel_id=1, replica_groups={{0,8,16,24},{32,40,48,56},{64,72,80,88},{96,104,112,120},{128,136,144,1..., dimensions={0} | all-to-all | bytes 557056 | tf_op jit(solution)/shard_map/all_to_all | solution.py:533
  38.8 0.4 shard_map.122.total_ref
  39.3 9.5 %collective-permute-start.4 = (bf16[272,128]{1,0:T(8,128)(2,1)S(1)}, bf16[272,128]{1,0:T(8,128)(2,1)S(1)}, u32[]{:S(2)}, u32[]{:S(2)}) collective-permute-start(bf16[272,128]{1,0:T(8,128)(2,1)S(1)} %shard_map.122.total_ref), channel_id=1, source_target_pairs={{0,96},{16,112},{32,128},{48,144},{64,160},{80,176},{96,192},{104,... | collective-permute-start | bytes 208904 | tf_op jit(solution)/shard_map/ppermute | solution.py:537
  48.8 7.3 %collective-permute-start.3 = (bf16[272,128]{1,0:T(8,128)(2,1)S(1)}, bf16[272,128]{1,0:T(8,128)(2,1)S(1)}, u32[]{:S(2)}, u32[]{:S(2)}) collective-permute-start(bf16[272,128]{1,0:T(8,128)(2,1)S(1)} %shard_map.122.total_ref), channel_id=1, source_target_pairs={{0,64},{16,80},{32,96},{48,112},{64,128},{72,8},{80,144},{88,24},{... | collective-permute-start | bytes 208904 | tf_op jit(solution)/shard_map/ppermute | solution.py:537
  56.1 5.9 %collective-permute-start.2 = (bf16[272,128]{1,0:T(8,128)(2,1)S(1)}, bf16[272,128]{1,0:T(8,128)(2,1)S(1)}, u32[]{:S(2)}, u32[]{:S(2)}) collective-permute-start(bf16[272,128]{1,0:T(8,128)(2,1)S(1)} %shard_map.122.total_ref), channel_id=1, source_target_pairs={{0,32},{16,48},{32,64},{40,8},{48,80},{56,24},{64,96},{72,40},{80,... | collective-permute-start | bytes 208904 | tf_op jit(solution)/shard_map/ppermute | solution.py:537
  62.0 0.0 collective-permute-done.4.first_ref
  62.0 0.0 collective-permute-done.3.middle_ref
  62.0 3.6 %collective-permute-done.2.last_ref = bf16[272,128]{1,0:T(8,128)(2,1)S(1)} collective-permute-done((bf16[272,128]{1,0:T(8,128)(2,1)S(1)}, bf16[272,128]{1,0:T(8,128)(2,1)S(1)}, u32[]{:S(2)}, u32[]{:S(2)}) %collective-permute-start.2) | collective-permute-done | bytes 69664 | tf_op jit(solution)/shard_map/ppermute | solution.py:537
  65.6 0.4 shard_map.123
  66.1 10.6 %all_to_all.27.rows_ref = bf16[4,272,128]{2,1,0:T(8,128)(2,1)S(1)} all-to-all(bf16[4,272,128]{2,1,0:T(8,128)(2,1)S(1)} %get-tuple-element.42), channel_id=1, replica_groups={{0,128,256,384},{8,136,264,392},{16,144,272,400},{24,152,280,408},{32,1..., dimensions={0} | all-to-all | bytes 557056 | tf_op jit(solution)/shard_map/all_to_all | solution.py:533
  76.6 0.0 copy-start.2
  76.6 0.9 shard_map.124
  77.6 0.0 copy-start
  77.6 9.4 %all_to_all.28.states_ref = bf16[4,128,128]{2,1,0:T(8,128)(2,1)S(1)} all-to-all(bf16[4,128,128]{2,1,0:T(8,128)(2,1)S(1)} %shard_map.124), channel_id=1, replica_groups={{0,8,16,24},{32,40,48,56},{64,72,80,88},{96,104,112,120},{128,136,144,1..., dimensions={0} | all-to-all | bytes 262144 | tf_op jit(solution)/shard_map/all_to_all | solution.py:533
  87.0 0.0 copy-start.1
  87.0 0.0 copy-start.4
  87.0 0.0 copy-start.5
  87.0 1.6 %shard_map.125 = (f32[128,512]{1,0:T(8,128)S(1)}, bf16[128,128]{1,0:T(8,128)(2,1)S(1)}, f32[8,512]{1,0:T(8,128)S(1)}) custom-call(bf16[4,128,128]{2,1,0:T(8,128)(2,1)S(1)} %all_to_all.28.states_ref, f32[128,512]{1,0:T(8,128)S(1)} %get-tuple-element.44.pre_ref, f32[2,128,128]{2,1,0:T(8,128)S(1)} %get-tuple-element.45.unit_ref, ...), custom_call_target="tpu_custom_call" | custom-call | tf_op jit(solution)/shard_map/pallas_call | solution.py:500
  88.6 1.3 %collective-permute-start.5 = (f32[8,512]{1,0:T(8,128)S(1)}, f32[8,512]{1,0:T(8,128)S(1)}, u32[]{:S(2)}, u32[]{:S(2)}) collective-permute-start(f32[8,512]{1,0:T(8,128)S(1)} %get-tuple-element.53), channel_id=1, source_target_pairs={{8,0},{16,8},{24,16},{32,24},{40,32},{48,40},{56,48},{64,56},{72,6... | collective-permute-start | bytes 49160 | tf_op jit(solution)/shard_map/ppermute | solution.py:566
  89.9 3.2 %collective-permute-done.5.halo_ref = f32[8,512]{1,0:T(8,128)S(1)} collective-permute-done((f32[8,512]{1,0:T(8,128)S(1)}, f32[8,512]{1,0:T(8,128)S(1)}, u32[]{:S(2)}, u32[]{:S(2)}) %collective-permute-start.5) | collective-permute-done | bytes 16416 | tf_op jit(solution)/shard_map/ppermute | solution.py:566
  93.1 0.0 copy-done.2
  93.1 0.0 copy-done
  93.1 0.0 copy-done.1
  93.1 0.0 copy-done.4
  93.1 0.0 copy-done.5
  93.1 0.6 shard_map.127
  93.7 9.5 %collective-permute-start.6 = (bf16[4,128,256]{2,1,0:T(8,128)(2,1)S(1)}, bf16[4,128,256]{2,1,0:T(8,128)(2,1)S(1)}, u32[]{:S(2)}, u32[]{:S(2)}) collective-permute-start(bf16[4,128,256]{2,1,0:T(8,128)(2,1)S(1)} %shard_map.127), channel_id=1, source_target_pairs={{0,1},{1,0},{2,3},{3,2},{4,5},{5,4},{6,7},{7,6},{8,9},{9,8},{10,11... | collective-permute-start | bytes 786440 | tf_op jit(solution)/shard_map/ppermute | solution.py:545
  103.2 0.6 shard_map.126.kept_ref
  103.8 0.5 collective-permute-done.6.got_ref
  104.4 8.8 %all_to_all.29 = bf16[4,128,256]{2,1,0:T(8,128)(2,1)S(1)} all-to-all(bf16[4,128,256]{2,1,0:T(8,128)(2,1)S(1)} %shard_map.128), channel_id=1, replica_groups={{0,2,4,6},{1,3,5,7},{8,10,12,14},{9,11,13,15},{16,18,20,22},{17,19,21,2..., dimensions={0} | all-to-all | bytes 524288 | tf_op jit(solution)/shard_map/all_to_all | solution.py:542
  113.2 0.7 reduce_sum.12
  (1 shorter events, 0.0 us)
Async XLA Ops:
  11.0 9.6 %collective-permute-start = (bf16[4,128,256]{2,1,0:T(8,128)(2,1)S(1)}, bf16[4,128,256]{2,1,0:T(8,128)(2,1)S(1)}, u32[]{:S(2)}, u32[]{:S(2)}) collective-permute-start(bf16[4,128,256]{2,1,0:T(8,128)(2,1)S(1)} %all_to_all.25.x_ref), channel_id=1, source_target_pairs={{0,1},{1,0},{2,3},{3,2},{4,5},{5,4},{6,7},{7,6},{8,9},{9,8},{10,11... | collective-permute-start | bytes 786440 | tf_op jit(solution)/shard_map/ppermute | solution.py:545
  21.2 2.1 %collective-permute-start.1 = (bf16[16,512]{1,0:T(8,128)(2,1)S(1)}, bf16[16,512]{1,0:T(8,128)(2,1)S(1)}, u32[]{:S(2)}, u32[]{:S(2)}) collective-permute-start(bf16[16,512]{1,0:T(8,128)(2,1)S(1)} %get-tuple-element.35), channel_id=1, source_target_pairs={{0,8},{8,16},{16,24},{24,32},{32,40},{40,48},{48,56},{56,64},{64,7... | collective-permute-start | bytes 49160 | tf_op jit(solution)/shard_map/ppermute | solution.py:551
  22.5 0.9 copy-start.3
  39.3 22.7 %collective-permute-start.4 = (bf16[272,128]{1,0:T(8,128)(2,1)S(1)}, bf16[272,128]{1,0:T(8,128)(2,1)S(1)}, u32[]{:S(2)}, u32[]{:S(2)}) collective-permute-start(bf16[272,128]{1,0:T(8,128)(2,1)S(1)} %shard_map.122.total_ref), channel_id=1, source_target_pairs={{0,96},{16,112},{32,128},{48,144},{64,160},{80,176},{96,192},{104,... | collective-permute-start | bytes 208904 | tf_op jit(solution)/shard_map/ppermute | solution.py:537
  48.8 13.2 %collective-permute-start.3 = (bf16[272,128]{1,0:T(8,128)(2,1)S(1)}, bf16[272,128]{1,0:T(8,128)(2,1)S(1)}, u32[]{:S(2)}, u32[]{:S(2)}) collective-permute-start(bf16[272,128]{1,0:T(8,128)(2,1)S(1)} %shard_map.122.total_ref), channel_id=1, source_target_pairs={{0,64},{16,80},{32,96},{48,112},{64,128},{72,8},{80,144},{88,24},{... | collective-permute-start | bytes 208904 | tf_op jit(solution)/shard_map/ppermute | solution.py:537
  56.1 9.5 %collective-permute-start.2 = (bf16[272,128]{1,0:T(8,128)(2,1)S(1)}, bf16[272,128]{1,0:T(8,128)(2,1)S(1)}, u32[]{:S(2)}, u32[]{:S(2)}) collective-permute-start(bf16[272,128]{1,0:T(8,128)(2,1)S(1)} %shard_map.122.total_ref), channel_id=1, source_target_pairs={{0,32},{16,48},{32,64},{40,8},{48,80},{56,24},{64,96},{72,40},{80,... | collective-permute-start | bytes 208904 | tf_op jit(solution)/shard_map/ppermute | solution.py:537
  76.6 16.4 %copy-start.2 = (bf16[2048,128]{1,0:T(8,128)(2,1)S(1)}, bf16[2048,128]{1,0:T(8,128)(2,1)}, u32[]{:S(2)}) copy-start(bf16[2048,128]{1,0:T(8,128)(2,1)} %wk_ref.3) | copy-start | bytes 1572868
  77.6 15.5 %copy-start = (bf16[2048,256]{1,0:T(8,128)(2,1)S(1)}, bf16[2048,256]{1,0:T(8,128)(2,1)}, u32[]{:S(2)}) copy-start(bf16[2048,256]{1,0:T(8,128)(2,1)} %wv_ref.3) | copy-start | bytes 3145732
  87.0 6.1 %copy-start.1 = (bf16[2048,128]{1,0:T(8,128)(2,1)S(1)}, bf16[2048,128]{1,0:T(8,128)(2,1)}, u32[]{:S(2)}) copy-start(bf16[2048,128]{1,0:T(8,128)(2,1)} %wq_ref.3) | copy-start | bytes 1572868
  87.0 6.1 %copy-start.4 = (bf16[2048,2]{0,1:T(2,128)(2,1)S(1)}, bf16[2048,2]{0,1:T(2,128)(2,1)}, u32[]{:S(2)}) copy-start(bf16[2048,2]{0,1:T(2,128)(2,1)} %param.16) | copy-start | bytes 24580
  87.0 6.1 %copy-start.5 = (bf16[2048,2]{0,1:T(2,128)(2,1)S(1)}, bf16[2048,2]{0,1:T(2,128)(2,1)}, u32[]{:S(2)}) copy-start(bf16[2048,2]{0,1:T(2,128)(2,1)} %param.17) | copy-start | bytes 24580
  88.6 4.5 %collective-permute-start.5 = (f32[8,512]{1,0:T(8,128)S(1)}, f32[8,512]{1,0:T(8,128)S(1)}, u32[]{:S(2)}, u32[]{:S(2)}) collective-permute-start(f32[8,512]{1,0:T(8,128)S(1)} %get-tuple-element.53), channel_id=1, source_target_pairs={{8,0},{16,8},{24,16},{32,24},{40,32},{48,40},{56,48},{64,56},{72,6... | collective-permute-start | bytes 49160 | tf_op jit(solution)/shard_map/ppermute | solution.py:566
  93.7 10.6 %collective-permute-start.6 = (bf16[4,128,256]{2,1,0:T(8,128)(2,1)S(1)}, bf16[4,128,256]{2,1,0:T(8,128)(2,1)S(1)}, u32[]{:S(2)}, u32[]{:S(2)}) collective-permute-start(bf16[4,128,256]{2,1,0:T(8,128)(2,1)S(1)} %shard_map.127), channel_id=1, source_target_pairs={{0,1},{1,0},{2,3},{3,2},{4,5},{5,4},{6,7},{7,6},{8,9},{9,8},{10,11... | collective-permute-start | bytes 786440 | tf_op jit(solution)/shard_map/ppermute | solution.py:545

commit v6 on v5

--- a/solution.py
+++ b/solution.py
@@ -12,7 +12,7 @@
 EPS = 1e-06
 SCALE = DH ** (-0.5)
 RADIX = 4
-PACK = 2 * DH + 16
+PACK = 2 * DH
 F32 = jnp.float32
 BF16 = jnp.bfloat16
 
@@ -148,6 +148,17 @@
         copy.wait()
 
 
+def copies_kernel(x_ref, out_ref, sems):
+    copies = [
+        pltpu.make_async_copy(x_ref, out_ref.at[part], sems.at[part])
+        for part in range(out_ref.shape[0])
+    ]
+    for copy in copies:
+        copy.start()
+    for copy in copies:
+        copy.wait()
+
+
 def second_project_kernel(
     x_ref, total_ref, part_ref, rest_ref, narrow_ref, proj_ref, ba_ref, tail_ref
 ):
@@ -157,14 +168,6 @@
     proj_ref[...] = bf(total)
     tail_ref[...] = bf(total[DH - 16 :])
     ba_ref[...] = bf(part_ref[...] + narrow_sums(x_ref, narrow_ref, 1 - core_place()))
-
-
-def split_decay(value):
-    high = bf(value).astype(F32)
-    middle = bf(value - high).astype(F32)
-    low = value - high - middle
-    row = lax.broadcasted_iota(jnp.int32, (16, DH), 0)
-    return bf(jnp.where(row == 0, high, jnp.where(row == 1, middle, jnp.where(row == 2, low, 0.0))))
 
 
 def gate_kernel(ba_ref, scales_ref, cols_ref, gap_ref):
@@ -201,7 +204,7 @@
     unit_ref[1] = key
     cols = cols_ref[...]
     gram = dot3(key, key, (1, 1))
-    cross = dot3(query, key, (1, 1))
+    cross = dot(query, key, (1, 1))
     gram_ref[...] = gram
     cross_ref[...] = cross
     betas = [cols[:, head : head + 1] for head in range(2)]
@@ -229,44 +232,40 @@
         weighted_ref[head] = bf(weighted)
         back_ref[head] = back
         ahead = dot(key_tail, both, (0, 0))
-        moved = ahead[:, DH:]
-        decay_rows = split_decay(jnp.exp(last))
-        send_ref[2 * head, 0:DH] = bf(moved)
-        send_ref[2 * head, DH : 2 * DH] = bf(ahead[:, :DH])
-        send_ref[2 * head, 2 * DH :] = decay_rows
-        send_ref[2 * head + 1, 0:DH] = bf(moved.T)
-        send_ref[2 * head + 1, DH : 2 * DH] = bf(
+        lost = jnp.where(row == col, 1.0 - jnp.exp(last), 0.0) + ahead[:, DH:]
+        send_ref[2 * head, 0:DH] = bf(lost)
+        send_ref[2 * head, DH:] = bf(ahead[:, :DH])
+        send_ref[2 * head + 1, 0:DH] = bf(lost.T)
+        send_ref[2 * head + 1, DH:] = bf(
             dot(gamma * query, grad, (0, 0)) - dot(weighted, back, (0, 0))
         )
-        send_ref[2 * head + 1, 2 * DH :] = decay_rows
 
 
 def unpack(ref):
-    decay = ref[2 * DH :].astype(F32)
+    return ref[0:DH], ref[DH:].astype(F32)
+
+
+def dot_wide(matrix, value):
+    high, low = halves(value)
+    return dot(matrix, high) + dot(matrix, low)
+
+
+def apply_map(later, state):
+    matrix, offset = later
+    return state - dot_wide(matrix, state) + offset
+
+
+def compose(later, earlier):
+    matrix, offset = later
+    before = earlier[0].astype(F32)
     return (
-        decay[0:1, 0:1] + decay[1:2, 0:1] + decay[2:3, 0:1],
-        ref[0:DH].astype(F32),
-        ref[DH : 2 * DH].astype(F32),
-    )
-
-
-def apply_map(later, state):
-    decay, matrix, offset = later
-    return decay * state - dot(matrix, state) + offset
-
-
-def compose(later, earlier):
-    decay, matrix, offset = later
-    return (
-        decay * earlier[0],
-        decay * earlier[1] + earlier[0] * matrix - dot(matrix, earlier[1]),
-        apply_map(later, earlier[2]),
+        before + matrix.astype(F32) - dot_wide(matrix, before),
+        apply_map(later, earlier[1]),
     )
 
 
 def pack(total):
-    decay, matrix, offset = total
-    return jnp.concatenate([bf(matrix), bf(offset), split_decay(decay)], axis=0)
+    return jnp.concatenate([bf(total[0]), bf(total[1])], axis=0)
 
 
 def is_backward():
@@ -287,9 +286,8 @@
 
 def window_kernel(total_ref, last_ref, middle_ref, first_ref, wider_ref, before_ref):
     before = compose(unpack(last_ref), compose(unpack(middle_ref), unpack(first_ref)))
-    before_ref[0:DH] = before[1]
-    before_ref[DH : 2 * DH] = before[2]
-    before_ref[2 * DH :] = jnp.broadcast_to(before[0], (8, DH))
+    before_ref[0:DH] = before[0]
+    before_ref[DH:] = before[1]
     wider = pack(compose(unpack(total_ref), before))
     for place in range(RADIX):
         wider_ref[place] = wider
@@ -302,8 +300,7 @@
     for step in range(RADIX - 1):
         later = apply_map(unpack(rows_ref.at[in_order(step, backward)]), state)
         state = jnp.where(step < place, later, state)
-    before = (before_ref[2 * DH : 2 * DH + 1, 0:1], before_ref[0:DH], before_ref[DH : 2 * DH])
-    state = apply_map(before, state)
+    state = apply_map((before_ref[0:DH], before_ref[DH:]), state)
     for step in range(RADIX):
         spot = in_order(step, backward)
         out_ref[spot] = bf(state)
@@ -544,7 +541,13 @@
     def between(value):
         return lax.ppermute(value, "tp", [(t, t ^ 1) for t in range(parts)])
 
-    mine = across(jnp.broadcast_to(inputs[None], (parts // 2,) + inputs.shape))
+    copies = call(
+        copies_kernel,
+        [((parts // 2,) + inputs.shape, BF16)],
+        [pltpu.SemaphoreType.DMA((parts // 2,))],
+        [pl.BlockSpec(memory_space=pltpu.HBM)],
+    )(stay(inputs))[0]
+    mine = across(copies)
     other = between(mine)
     total, part, taps, scales, rest, narrow = first_project(mine, weights, filters, decay, bias)
     proj, gates, tail = second_project(other, total, part, rest, narrow)
@@ -556,7 +559,7 @@
     total = call(group_kernel, [((PACK, DH), BF16)])(got)[0]
     earlier = [onward(total, RADIX * step) for step in range(1, RADIX)]
     total, before = call(
-        window_kernel, [((RADIX, PACK, DH), BF16), ((2 * DH + 8, DH), F32)]
+        window_kernel, [((RADIX, PACK, DH), BF16), ((PACK, DH), F32)]
     )(total, *earlier)
     states = call(states_kernel, [((RADIX, DH, DH), BF16)])(exchange(total, rank), before, got)[0]
     states = exchange(states, group)

time: 114 us -> 114 us (level)
  blocking collectives: 51.2 us -> 49.8 us
  Pallas kernels: 10.7 us -> 11.9 us
    all_to_all x3, blocking collectives: 32.3 us -> 30.8 us  [exchange(): return lax.all_to_all(value, 'ctx', 0, 0, axis_index_groups=groups)]
where the time goes in v6:
time: 114 us; the launch traced here: 113 us
  blocking collectives  49.8 us (44%)
  starting transfers between devices  42.5 us (37%)
  Pallas kernels  11.9 us (10%)
  waiting for transfers between devices  8.01 us (7%)
    all_to_all x3, blocking collectives, exchange(): return lax.all_to_all(value, 'ctx', 0, 0, axis_index_groups=groups)  30.8 us
    ppermute x3, starting transfers between devices, onward(): lax.ppermute(value, 'ctx', [(s, t) for s, t in steps if 0 <= t < count])  22.7 us
    all_to_all x2, blocking collectives, across(): return lax.all_to_all(value, 'tp', 0, 0, axis_index_groups=chips)  19 us
    ppermute x2, starting transfers between devices, between(): return lax.ppermute(value, 'tp', [(t, t ^ 1) for t in range(parts)])  17.2 us
    ppermute x1, waiting for transfers between devices, local(): halo = lax.ppermute(halo, 'ctx', [(s + 1, s) for s in range(count - 1)])  3.78 us
    ppermute x3, waiting for transfers between devices, onward(): lax.ppermute(value, 'ctx', [(s, t) for s, t in steps if 0 <= t < count])  3.26 us
    pallas_call x1, Pallas kernels, slab(): call(slab_kernel, [((4, PACK, DH), BF16), ((DH, 4 * DH), F32), ((2,) + sq...  3.04 us
  transfers between devices with their start and end apart: 7, of which 4 were waited for; matrix products, arithmetic and copies ran while one was open for 0% of the time, Pallas kernels for 3%

profile of v6, /device:TPU:1, one launch (start us, length us, event | category | flops | bytes accessed | tf_op | source)
XLA Modules:
  0.0 113.0 jit_solution(14363573302442281765)
XLA Ops:
  0.0 1.0 shard_map.118
  1.0 10.2 %all_to_all.25.x_ref = bf16[4,128,256]{2,1,0:T(8,128)(2,1)S(1)} all-to-all(bf16[4,128,256]{2,1,0:T(8,128)(2,1)S(1)} %shard_map.118), channel_id=1, replica_groups={{0,2,4,6},{1,3,5,7},{8,10,12,14},{9,11,13,15},{16,18,20,22},{17,19,21,2..., dimensions={0} | all-to-all | bytes 524288 | tf_op jit(solution)/shard_map/all_to_all | solution.py:539
  11.2 7.7 %collective-permute-start = (bf16[4,128,256]{2,1,0:T(8,128)(2,1)S(1)}, bf16[4,128,256]{2,1,0:T(8,128)(2,1)S(1)}, u32[]{:S(2)}, u32[]{:S(2)}) collective-permute-start(bf16[4,128,256]{2,1,0:T(8,128)(2,1)S(1)} %all_to_all.25.x_ref), channel_id=1, source_target_pairs={{0,1},{1,0},{2,3},{3,2},{4,5},{5,4},{6,7},{7,6},{8,9},{9,8},{10,11... | collective-permute-start | bytes 786440 | tf_op jit(solution)/shard_map/ppermute | solution.py:542
  18.9 1.9 %shard_map.119 = (f32[128,512]{1,0:T(8,128)S(1)}, f32[128,128]{1,0:T(8,128)S(1)}, f32[8,512]{1,0:T(8,128)S(1)}, f32[2,128,128]{2,1,0:T(8,128)S(1)}, bf16[4,256,5...) custom-call(bf16[4,128,256]{2,1,0:T(8,128)(2,1)S(1)} %all_to_all.25.x_ref, bf16[4,2,256,128]{3,2,1,0:T(8,128)(2,1)} %bitcast.8, ...), custom_call_target="tpu_custom_call" | custom-call | tf_op jit(solution)/shard_map/pallas_call | solution.py:459
  20.8 0.0 collective-permute-done.x_ref
  20.8 0.6 shard_map.120
  21.4 1.3 %collective-permute-start.1 = (bf16[16,512]{1,0:T(8,128)(2,1)S(1)}, bf16[16,512]{1,0:T(8,128)(2,1)S(1)}, u32[]{:S(2)}, u32[]{:S(2)}) collective-permute-start(bf16[16,512]{1,0:T(8,128)(2,1)S(1)} %get-tuple-element.35), channel_id=1, source_target_pairs={{0,8},{8,16},{16,24},{24,32},{32,40},{40,48},{48,56},{56,64},{64,7... | collective-permute-start | bytes 49160 | tf_op jit(solution)/shard_map/ppermute | solution.py:554
  22.7 0.0 copy-start.3
  22.7 0.4 shard_map.121
  23.1 0.5 collective-permute-done.1.tail_ref
  23.5 0.0 copy-done.3
  23.5 3.0 %shard_map.122 = (bf16[4,256,128]{2,1,0:T(8,128)(2,1)S(1)}, f32[128,512]{1,0:T(8,128)S(1)}, f32[2,128,128]{2,1,0:T(8,128)S(1)}, bf16[2,128,128]{2,1,0:T(8,128)(2...) custom-call(bf16[128,512]{1,0:T(8,128)(2,1)S(1)} %get-tuple-element., ...), custom_call_target="tpu_custom_call" | custom-call | tf_op jit(solution)/shard_map/pallas_call | solution.py:484
  26.6 11.3 %all_to_all.26.got_ref.group_ref = bf16[4,256,128]{2,1,0:T(8,128)(2,1)S(1)} all-to-all(bf16[4,256,128]{2,1,0:T(8,128)(2,1)S(1)} %get-tuple-element.41), channel_id=1, replica_groups={{0,8,16,24},{32,40,48,56},{64,72,80,88},{96,104,112,120},{128,136,144,1..., dimensions={0} | all-to-all | bytes 524288 | tf_op jit(solution)/shard_map/all_to_all | solution.py:530
  37.9 0.5 shard_map.123.total_ref
  38.4 9.5 %collective-permute-start.4 = (bf16[256,128]{1,0:T(8,128)(2,1)S(1)}, bf16[256,128]{1,0:T(8,128)(2,1)S(1)}, u32[]{:S(2)}, u32[]{:S(2)}) collective-permute-start(bf16[256,128]{1,0:T(8,128)(2,1)S(1)} %shard_map.123.total_ref), channel_id=1, source_target_pairs={{0,96},{16,112},{32,128},{48,144},{64,160},{80,176},{96,192},{104,... | collective-permute-start | bytes 196616 | tf_op jit(solution)/shard_map/ppermute | solution.py:534
  47.9 7.3 %collective-permute-start.3 = (bf16[256,128]{1,0:T(8,128)(2,1)S(1)}, bf16[256,128]{1,0:T(8,128)(2,1)S(1)}, u32[]{:S(2)}, u32[]{:S(2)}) collective-permute-start(bf16[256,128]{1,0:T(8,128)(2,1)S(1)} %shard_map.123.total_ref), channel_id=1, source_target_pairs={{0,64},{16,80},{32,96},{48,112},{64,128},{72,8},{80,144},{88,24},{... | collective-permute-start | bytes 196616 | tf_op jit(solution)/shard_map/ppermute | solution.py:534
  55.2 5.9 %collective-permute-start.2 = (bf16[256,128]{1,0:T(8,128)(2,1)S(1)}, bf16[256,128]{1,0:T(8,128)(2,1)S(1)}, u32[]{:S(2)}, u32[]{:S(2)}) collective-permute-start(bf16[256,128]{1,0:T(8,128)(2,1)S(1)} %shard_map.123.total_ref), channel_id=1, source_target_pairs={{0,32},{16,48},{32,64},{40,8},{48,80},{56,24},{64,96},{72,40},{80,... | collective-permute-start | bytes 196616 | tf_op jit(solution)/shard_map/ppermute | solution.py:534
  61.1 0.0 collective-permute-done.4.first_ref
  61.1 0.0 collective-permute-done.3.middle_ref
  61.1 3.3 %collective-permute-done.2.last_ref = bf16[256,128]{1,0:T(8,128)(2,1)S(1)} collective-permute-done((bf16[256,128]{1,0:T(8,128)(2,1)S(1)}, bf16[256,128]{1,0:T(8,128)(2,1)S(1)}, u32[]{:S(2)}, u32[]{:S(2)}) %collective-permute-start.2) | collective-permute-done | bytes 65568 | tf_op jit(solution)/shard_map/ppermute | solution.py:534
  64.4 0.5 shard_map.124
  64.9 11.2 %all_to_all.27.rows_ref = bf16[4,256,128]{2,1,0:T(8,128)(2,1)S(1)} all-to-all(bf16[4,256,128]{2,1,0:T(8,128)(2,1)S(1)} %get-tuple-element.42), channel_id=1, replica_groups={{0,128,256,384},{8,136,264,392},{16,144,272,400},{24,152,280,408},{32,1..., dimensions={0} | all-to-all | bytes 524288 | tf_op jit(solution)/shard_map/all_to_all | solution.py:530
  76.1 0.0 copy-start.2
  76.1 1.1 shard_map.125
  77.2 0.0 copy-start
  77.2 8.3 %all_to_all.28.states_ref = bf16[4,128,128]{2,1,0:T(8,128)(2,1)S(1)} all-to-all(bf16[4,128,128]{2,1,0:T(8,128)(2,1)S(1)} %shard_map.125), channel_id=1, replica_groups={{0,8,16,24},{32,40,48,56},{64,72,80,88},{96,104,112,120},{128,136,144,1..., dimensions={0} | all-to-all | bytes 262144 | tf_op jit(solution)/shard_map/all_to_all | solution.py:530
  85.5 0.0 copy-start.1
  85.5 0.0 copy-start.4
  85.5 0.0 copy-start.5
  85.5 1.6 %shard_map.126 = (f32[128,512]{1,0:T(8,128)S(1)}, bf16[128,128]{1,0:T(8,128)(2,1)S(1)}, f32[8,512]{1,0:T(8,128)S(1)}) custom-call(bf16[4,128,128]{2,1,0:T(8,128)(2,1)S(1)} %all_to_all.28.states_ref, f32[128,512]{1,0:T(8,128)S(1)} %get-tuple-element.44.pre_ref, f32[2,128,128]{2,1,0:T(8,128)S(1)} %get-tuple-element.45.unit_ref, ...), custom_call_target="tpu_custom_call" | custom-call | tf_op jit(solution)/shard_map/pallas_call | solution.py:497
  87.1 1.3 %collective-permute-start.5 = (f32[8,512]{1,0:T(8,128)S(1)}, f32[8,512]{1,0:T(8,128)S(1)}, u32[]{:S(2)}, u32[]{:S(2)}) collective-permute-start(f32[8,512]{1,0:T(8,128)S(1)} %get-tuple-element.53), channel_id=1, source_target_pairs={{8,0},{16,8},{24,16},{32,24},{40,32},{48,40},{56,48},{64,56},{72,6... | collective-permute-start | bytes 49160 | tf_op jit(solution)/shard_map/ppermute | solution.py:569
  88.4 3.8 %collective-permute-done.5.halo_ref = f32[8,512]{1,0:T(8,128)S(1)} collective-permute-done((f32[8,512]{1,0:T(8,128)S(1)}, f32[8,512]{1,0:T(8,128)S(1)}, u32[]{:S(2)}, u32[]{:S(2)}) %collective-permute-start.5) | collective-permute-done | bytes 16416 | tf_op jit(solution)/shard_map/ppermute | solution.py:569
  92.2 0.0 copy-done.2
  92.2 0.0 copy-done
  92.2 0.0 copy-done.1
  92.2 0.0 copy-done.4
  92.2 0.0 copy-done.5
  92.2 0.6 shard_map.128
  92.8 9.6 %collective-permute-start.6 = (bf16[4,128,256]{2,1,0:T(8,128)(2,1)S(1)}, bf16[4,128,256]{2,1,0:T(8,128)(2,1)S(1)}, u32[]{:S(2)}, u32[]{:S(2)}) collective-permute-start(bf16[4,128,256]{2,1,0:T(8,128)(2,1)S(1)} %shard_map.128), channel_id=1, source_target_pairs={{0,1},{1,0},{2,3},{3,2},{4,5},{5,4},{6,7},{7,6},{8,9},{9,8},{10,11... | collective-permute-start | bytes 786440 | tf_op jit(solution)/shard_map/ppermute | solution.py:542
  102.4 0.6 shard_map.127.kept_ref
  103.0 0.5 collective-permute-done.6.got_ref
  103.6 8.8 %all_to_all.29 = bf16[4,128,256]{2,1,0:T(8,128)(2,1)S(1)} all-to-all(bf16[4,128,256]{2,1,0:T(8,128)(2,1)S(1)} %shard_map.129), channel_id=1, replica_groups={{0,2,4,6},{1,3,5,7},{8,10,12,14},{9,11,13,15},{16,18,20,22},{17,19,21,2..., dimensions={0} | all-to-all | bytes 524288 | tf_op jit(solution)/shard_map/all_to_all | solution.py:539
  112.4 0.7 reduce_sum.12
  (1 shorter events, 0.0 us)
Async XLA Ops:
  11.2 9.6 %collective-permute-start = (bf16[4,128,256]{2,1,0:T(8,128)(2,1)S(1)}, bf16[4,128,256]{2,1,0:T(8,128)(2,1)S(1)}, u32[]{:S(2)}, u32[]{:S(2)}) collective-permute-start(bf16[4,128,256]{2,1,0:T(8,128)(2,1)S(1)} %all_to_all.25.x_ref), channel_id=1, source_target_pairs={{0,1},{1,0},{2,3},{3,2},{4,5},{5,4},{6,7},{7,6},{8,9},{9,8},{10,11... | collective-permute-start | bytes 786440 | tf_op jit(solution)/shard_map/ppermute | solution.py:542
  21.4 2.1 %collective-permute-start.1 = (bf16[16,512]{1,0:T(8,128)(2,1)S(1)}, bf16[16,512]{1,0:T(8,128)(2,1)S(1)}, u32[]{:S(2)}, u32[]{:S(2)}) collective-permute-start(bf16[16,512]{1,0:T(8,128)(2,1)S(1)} %get-tuple-element.35), channel_id=1, source_target_pairs={{0,8},{8,16},{16,24},{24,32},{32,40},{40,48},{48,56},{56,64},{64,7... | collective-permute-start | bytes 49160 | tf_op jit(solution)/shard_map/ppermute | solution.py:554
  22.7 0.9 copy-start.3
  38.4 22.7 %collective-permute-start.4 = (bf16[256,128]{1,0:T(8,128)(2,1)S(1)}, bf16[256,128]{1,0:T(8,128)(2,1)S(1)}, u32[]{:S(2)}, u32[]{:S(2)}) collective-permute-start(bf16[256,128]{1,0:T(8,128)(2,1)S(1)} %shard_map.123.total_ref), channel_id=1, source_target_pairs={{0,96},{16,112},{32,128},{48,144},{64,160},{80,176},{96,192},{104,... | collective-permute-start | bytes 196616 | tf_op jit(solution)/shard_map/ppermute | solution.py:534
  47.9 13.2 %collective-permute-start.3 = (bf16[256,128]{1,0:T(8,128)(2,1)S(1)}, bf16[256,128]{1,0:T(8,128)(2,1)S(1)}, u32[]{:S(2)}, u32[]{:S(2)}) collective-permute-start(bf16[256,128]{1,0:T(8,128)(2,1)S(1)} %shard_map.123.total_ref), channel_id=1, source_target_pairs={{0,64},{16,80},{32,96},{48,112},{64,128},{72,8},{80,144},{88,24},{... | collective-permute-start | bytes 196616 | tf_op jit(solution)/shard_map/ppermute | solution.py:534
  55.2 9.1 %collective-permute-start.2 = (bf16[256,128]{1,0:T(8,128)(2,1)S(1)}, bf16[256,128]{1,0:T(8,128)(2,1)S(1)}, u32[]{:S(2)}, u32[]{:S(2)}) collective-permute-start(bf16[256,128]{1,0:T(8,128)(2,1)S(1)} %shard_map.123.total_ref), channel_id=1, source_target_pairs={{0,32},{16,48},{32,64},{40,8},{48,80},{56,24},{64,96},{72,40},{80,... | collective-permute-start | bytes 196616 | tf_op jit(solution)/shard_map/ppermute | solution.py:534
  76.1 16.1 %copy-start.2 = (bf16[2048,128]{1,0:T(8,128)(2,1)S(1)}, bf16[2048,128]{1,0:T(8,128)(2,1)}, u32[]{:S(2)}) copy-start(bf16[2048,128]{1,0:T(8,128)(2,1)} %wk_ref.3) | copy-start | bytes 1572868
  77.2 15.0 %copy-start = (bf16[2048,256]{1,0:T(8,128)(2,1)S(1)}, bf16[2048,256]{1,0:T(8,128)(2,1)}, u32[]{:S(2)}) copy-start(bf16[2048,256]{1,0:T(8,128)(2,1)} %wv_ref.3) | copy-start | bytes 3145732
  85.5 6.7 %copy-start.1 = (bf16[2048,128]{1,0:T(8,128)(2,1)S(1)}, bf16[2048,128]{1,0:T(8,128)(2,1)}, u32[]{:S(2)}) copy-start(bf16[2048,128]{1,0:T(8,128)(2,1)} %wq_ref.3) | copy-start | bytes 1572868
  85.5 6.7 %copy-start.4 = (bf16[2048,2]{0,1:T(2,128)(2,1)S(1)}, bf16[2048,2]{0,1:T(2,128)(2,1)}, u32[]{:S(2)}) copy-start(bf16[2048,2]{0,1:T(2,128)(2,1)} %param.16) | copy-start | bytes 24580
  85.5 6.7 %copy-start.5 = (bf16[2048,2]{0,1:T(2,128)(2,1)S(1)}, bf16[2048,2]{0,1:T(2,128)(2,1)}, u32[]{:S(2)}) copy-start(bf16[2048,2]{0,1:T(2,128)(2,1)} %param.17) | copy-start | bytes 24580
  87.1 5.1 %collective-permute-start.5 = (f32[8,512]{1,0:T(8,128)S(1)}, f32[8,512]{1,0:T(8,128)S(1)}, u32[]{:S(2)}, u32[]{:S(2)}) collective-permute-start(f32[8,512]{1,0:T(8,128)S(1)} %get-tuple-element.53), channel_id=1, source_target_pairs={{8,0},{16,8},{24,16},{32,24},{40,32},{48,40},{56,48},{64,56},{72,6... | collective-permute-start | bytes 49160 | tf_op jit(solution)/shard_map/ppermute | solution.py:569
  92.8 10.7 %collective-permute-start.6 = (bf16[4,128,256]{2,1,0:T(8,128)(2,1)S(1)}, bf16[4,128,256]{2,1,0:T(8,128)(2,1)S(1)}, u32[]{:S(2)}, u32[]{:S(2)}) collective-permute-start(bf16[4,128,256]{2,1,0:T(8,128)(2,1)S(1)} %shard_map.128), channel_id=1, source_target_pairs={{0,1},{1,0},{2,3},{3,2},{4,5},{5,4},{6,7},{7,6},{8,9},{9,8},{10,11... | collective-permute-start | bytes 786440 | tf_op jit(solution)/shard_map/ppermute | solution.py:542

commit v7 on v6

--- a/solution.py
+++ b/solution.py
@@ -145,17 +145,6 @@
     scales_ref[0] = lanes_of([0.0, 0.0, -jnp.exp(decay[:, 0:1]), -jnp.exp(decay[:, 1:2])])
     scales_ref[1] = lanes_of([0.0, 0.0, bias[:, 0:1], bias[:, 1:2]])
     for copy in copies[ready:]:
-        copy.wait()
-
-
-def copies_kernel(x_ref, out_ref, sems):
-    copies = [
-        pltpu.make_async_copy(x_ref, out_ref.at[part], sems.at[part])
-        for part in range(out_ref.shape[0])
-    ]
-    for copy in copies:
-        copy.start()
-    for copy in copies:
         copy.wait()
 
 
@@ -245,21 +234,16 @@
     return ref[0:DH], ref[DH:].astype(F32)
 
 
-def dot_wide(matrix, value):
-    high, low = halves(value)
-    return dot(matrix, high) + dot(matrix, low)
-
-
 def apply_map(later, state):
     matrix, offset = later
-    return state - dot_wide(matrix, state) + offset
+    return state - dot(matrix, state) + offset
 
 
 def compose(later, earlier):
     matrix, offset = later
     before = earlier[0].astype(F32)
     return (
-        before + matrix.astype(F32) - dot_wide(matrix, before),
+        before + matrix.astype(F32) - dot(matrix, before),
         apply_map(later, earlier[1]),
     )
 
@@ -541,13 +525,7 @@
     def between(value):
         return lax.ppermute(value, "tp", [(t, t ^ 1) for t in range(parts)])
 
-    copies = call(
-        copies_kernel,
-        [((parts // 2,) + inputs.shape, BF16)],
-        [pltpu.SemaphoreType.DMA((parts // 2,))],
-        [pl.BlockSpec(memory_space=pltpu.HBM)],
-    )(stay(inputs))[0]
-    mine = across(copies)
+    mine = across(jnp.broadcast_to(inputs[None], (parts // 2,) + inputs.shape))
     other = between(mine)
     total, part, taps, scales, rest, narrow = first_project(mine, weights, filters, decay, bias)
     proj, gates, tail = second_project(other, total, part, rest, narrow)
@@ -557,7 +535,8 @@
     send, *kept = slab(proj, tail, taps, cols, gap, grad_core)
     got = exchange(send, group)
     total = call(group_kernel, [((PACK, DH), BF16)])(got)[0]
-    earlier = [onward(total, RADIX * step) for step in range(1, RADIX)]
+    last = onward(total, RADIX)
+    earlier = [last, onward(last, RADIX), onward(total, 3 * RADIX)]
     total, before = call(
         window_kernel, [((RADIX, PACK, DH), BF16), ((PACK, DH), F32)]
     )(total, *earlier)

time: 114 us -> 110 us (0.965)
  starting transfers between devices: 42.5 us -> 37.4 us
  blocking collectives: 49.8 us -> 54.3 us
  waiting for transfers between devices: 8.01 us -> 5.47 us
  Pallas kernels: 11.9 us -> 10.6 us
    all_to_all x3, blocking collectives: 30.8 us -> 35.3 us  [exchange(): return lax.all_to_all(value, 'ctx', 0, 0, axis_index_groups=groups)]
    ppermute x3, starting transfers between devices: 22.7 us -> 19 us  [onward(): lax.ppermute(value, 'ctx', [(s, t) for s, t in steps if 0 <= t < count])]
    ppermute x3, waiting for transfers between devices: 3.26 us -> 1.31 us  [onward(): lax.ppermute(value, 'ctx', [(s, t) for s, t in steps if 0 <= t < count])]
    ppermute x2, starting transfers between devices: 17.2 us -> 15.7 us  [between(): return lax.ppermute(value, 'tp', [(t, t ^ 1) for t in range(parts)])]
where the time goes in v7:
time: 110 us; the launch traced here: 109 us
  blocking collectives  54.3 us (49%)
  starting transfers between devices  37.4 us (34%)
  Pallas kernels  10.6 us (10%)
  waiting for transfers between devices  5.47 us (5%)
    all_to_all x3, blocking collectives, exchange(): return lax.all_to_all(value, 'ctx', 0, 0, axis_index_groups=groups)  35.3 us
    ppermute x3, starting transfers between devices, onward(): lax.ppermute(value, 'ctx', [(s, t) for s, t in steps if 0 <= t < count])  19 us
    all_to_all x2, blocking collectives, across(): return lax.all_to_all(value, 'tp', 0, 0, axis_index_groups=chips)  19 us
    ppermute x2, starting transfers between devices, between(): return lax.ppermute(value, 'tp', [(t, t ^ 1) for t in range(parts)])  15.7 us
    ppermute x1, waiting for transfers between devices, local(): halo = lax.ppermute(halo, 'ctx', [(s + 1, s) for s in range(count - 1)])  3.18 us
    pallas_call x1, Pallas kernels, slab(): call(slab_kernel, [((4, PACK, DH), BF16), ((DH, 4 * DH), F32), ((2,) + sq...  3.04 us
  transfers between devices with their start and end apart: 7, of which 4 were waited for; matrix products, arithmetic and copies ran while one was open for 0% of the time, Pallas kernels for 3%

profile of v7, /device:TPU:1, one launch (start us, length us, event | category | flops | bytes accessed | tf_op | source)
XLA Modules:
  0.0 109.4 jit_solution(9423703998995631225)
XLA Ops:
  0.0 0.9 broadcast_in_dim.2
  0.9 10.2 %all_to_all.25.x_ref = bf16[4,128,256]{2,1,0:T(8,128)(2,1)S(1)} all-to-all(bf16[4,128,256]{2,1,0:T(8,128)(2,1)S(1)} %broadcast_in_dim.2), channel_id=1, replica_groups={{0,2,4,6},{1,3,5,7},{8,10,12,14},{9,11,13,15},{16,18,20,22},{17,19,21,2..., dimensions={0} | all-to-all | bytes 524288 | tf_op jit(solution)/shard_map/all_to_all | solution.py:523
  11.0 7.7 %collective-permute-start = (bf16[4,128,256]{2,1,0:T(8,128)(2,1)S(1)}, bf16[4,128,256]{2,1,0:T(8,128)(2,1)S(1)}, u32[]{:S(2)}, u32[]{:S(2)}) collective-permute-start(bf16[4,128,256]{2,1,0:T(8,128)(2,1)S(1)} %all_to_all.25.x_ref), channel_id=1, source_target_pairs={{0,1},{1,0},{2,3},{3,2},{4,5},{5,4},{6,7},{7,6},{8,9},{9,8},{10,11... | collective-permute-start | bytes 786440 | tf_op jit(solution)/shard_map/ppermute | solution.py:526
  18.7 1.9 %shard_map.118 = (f32[128,512]{1,0:T(8,128)S(1)}, f32[128,128]{1,0:T(8,128)S(1)}, f32[8,512]{1,0:T(8,128)S(1)}, f32[2,128,128]{2,1,0:T(8,128)S(1)}, bf16[4,256,5...) custom-call(bf16[4,128,256]{2,1,0:T(8,128)(2,1)S(1)} %all_to_all.25.x_ref, bf16[4,2,256,128]{3,2,1,0:T(8,128)(2,1)} %bitcast.8, ...), custom_call_target="tpu_custom_call" | custom-call | tf_op jit(solution)/shard_map/pallas_call | solution.py:443
  20.6 0.0 collective-permute-done.x_ref
  20.7 0.6 shard_map.119
  21.2 1.3 %collective-permute-start.1 = (bf16[16,512]{1,0:T(8,128)(2,1)S(1)}, bf16[16,512]{1,0:T(8,128)(2,1)S(1)}, u32[]{:S(2)}, u32[]{:S(2)}) collective-permute-start(bf16[16,512]{1,0:T(8,128)(2,1)S(1)} %get-tuple-element.35), channel_id=1, source_target_pairs={{0,8},{8,16},{16,24},{24,32},{32,40},{40,48},{48,56},{56,64},{64,7... | collective-permute-start | bytes 49160 | tf_op jit(solution)/shard_map/ppermute | solution.py:532
  22.5 0.0 copy-start.3
  22.5 0.4 shard_map.120
  22.9 0.5 collective-permute-done.1.tail_ref
  23.4 0.0 copy-done.3
  23.4 3.0 %shard_map.121 = (bf16[4,256,128]{2,1,0:T(8,128)(2,1)S(1)}, f32[128,512]{1,0:T(8,128)S(1)}, f32[2,128,128]{2,1,0:T(8,128)S(1)}, bf16[2,128,128]{2,1,0:T(8,128)(2...) custom-call(bf16[128,512]{1,0:T(8,128)(2,1)S(1)} %get-tuple-element., ...), custom_call_target="tpu_custom_call" | custom-call | tf_op jit(solution)/shard_map/pallas_call | solution.py:468
  26.4 11.3 %all_to_all.26.got_ref.group_ref = bf16[4,256,128]{2,1,0:T(8,128)(2,1)S(1)} all-to-all(bf16[4,256,128]{2,1,0:T(8,128)(2,1)S(1)} %get-tuple-element.41), channel_id=1, replica_groups={{0,8,16,24},{32,40,48,56},{64,72,80,88},{96,104,112,120},{128,136,144,1..., dimensions={0} | all-to-all | bytes 524288 | tf_op jit(solution)/shard_map/all_to_all | solution.py:514
  37.7 0.4 shard_map.122.total_ref
  38.1 8.8 %collective-permute-start.2 = (bf16[256,128]{1,0:T(8,128)(2,1)S(1)}, bf16[256,128]{1,0:T(8,128)(2,1)S(1)}, u32[]{:S(2)}, u32[]{:S(2)}) collective-permute-start(bf16[256,128]{1,0:T(8,128)(2,1)S(1)} %shard_map.122.total_ref), channel_id=1, source_target_pairs={{0,32},{16,48},{32,64},{40,8},{48,80},{56,24},{64,96},{72,40},{80,... | collective-permute-start | bytes 196616 | tf_op jit(solution)/shard_map/ppermute | solution.py:518
  47.0 5.9 %collective-permute-start.4 = (bf16[256,128]{1,0:T(8,128)(2,1)S(1)}, bf16[256,128]{1,0:T(8,128)(2,1)S(1)}, u32[]{:S(2)}, u32[]{:S(2)}) collective-permute-start(bf16[256,128]{1,0:T(8,128)(2,1)S(1)} %shard_map.122.total_ref), channel_id=1, source_target_pairs={{0,96},{16,112},{32,128},{48,144},{64,160},{80,176},{96,192},{104,... | collective-permute-start | bytes 196616 | tf_op jit(solution)/shard_map/ppermute | solution.py:518
  52.9 0.0 collective-permute-done.2.last_ref
  52.9 4.3 %collective-permute-start.3 = (bf16[256,128]{1,0:T(8,128)(2,1)S(1)}, bf16[256,128]{1,0:T(8,128)(2,1)S(1)}, u32[]{:S(2)}, u32[]{:S(2)}) collective-permute-start(bf16[256,128]{1,0:T(8,128)(2,1)S(1)} %collective-permute-done.2.last_ref), channel_id=1, source_target_pairs={{0,32},{16,48},{32,64},{40,8},{48,80},{56,24},{64,96},{72,40},{80,... | collective-permute-start | bytes 196616 | tf_op jit(solution)/shard_map/ppermute | solution.py:518
  57.2 0.0 collective-permute-done.4.first_ref
  57.2 1.3 %collective-permute-done.3.middle_ref = bf16[256,128]{1,0:T(8,128)(2,1)S(1)} collective-permute-done((bf16[256,128]{1,0:T(8,128)(2,1)S(1)}, bf16[256,128]{1,0:T(8,128)(2,1)S(1)}, u32[]{:S(2)}, u32[]{:S(2)}) %collective-permute-start.3) | collective-permute-done | bytes 65568 | tf_op jit(solution)/shard_map/ppermute | solution.py:518
  58.5 0.4 shard_map.123
  58.9 14.5 %all_to_all.27.rows_ref = bf16[4,256,128]{2,1,0:T(8,128)(2,1)S(1)} all-to-all(bf16[4,256,128]{2,1,0:T(8,128)(2,1)S(1)} %get-tuple-element.42), channel_id=1, replica_groups={{0,128,256,384},{8,136,264,392},{16,144,272,400},{24,152,280,408},{32,1..., dimensions={0} | all-to-all | bytes 524288 | tf_op jit(solution)/shard_map/all_to_all | solution.py:514
  73.4 0.0 copy-start.2
  73.4 0.9 shard_map.124
  74.3 0.0 copy-start
  74.4 9.5 %all_to_all.28.states_ref = bf16[4,128,128]{2,1,0:T(8,128)(2,1)S(1)} all-to-all(bf16[4,128,128]{2,1,0:T(8,128)(2,1)S(1)} %shard_map.124), channel_id=1, replica_groups={{0,8,16,24},{32,40,48,56},{64,72,80,88},{96,104,112,120},{128,136,144,1..., dimensions={0} | all-to-all | bytes 262144 | tf_op jit(solution)/shard_map/all_to_all | solution.py:514
  83.9 0.0 copy-start.1
  83.9 0.0 copy-start.4
  83.9 0.0 copy-start.5
  83.9 1.6 %shard_map.125 = (f32[128,512]{1,0:T(8,128)S(1)}, bf16[128,128]{1,0:T(8,128)(2,1)S(1)}, f32[8,512]{1,0:T(8,128)S(1)}) custom-call(bf16[4,128,128]{2,1,0:T(8,128)(2,1)S(1)} %all_to_all.28.states_ref, f32[128,512]{1,0:T(8,128)S(1)} %get-tuple-element.44.pre_ref, f32[2,128,128]{2,1,0:T(8,128)S(1)} %get-tuple-element.45.unit_ref, ...), custom_call_target="tpu_custom_call" | custom-call | tf_op jit(solution)/shard_map/pallas_call | solution.py:481
  85.5 1.3 %collective-permute-start.5 = (f32[8,512]{1,0:T(8,128)S(1)}, f32[8,512]{1,0:T(8,128)S(1)}, u32[]{:S(2)}, u32[]{:S(2)}) collective-permute-start(f32[8,512]{1,0:T(8,128)S(1)} %get-tuple-element.53), channel_id=1, source_target_pairs={{8,0},{16,8},{24,16},{32,24},{40,32},{48,40},{56,48},{64,56},{72,6... | collective-permute-start | bytes 49160 | tf_op jit(solution)/shard_map/ppermute | solution.py:548
  86.8 3.2 %collective-permute-done.5.halo_ref = f32[8,512]{1,0:T(8,128)S(1)} collective-permute-done((f32[8,512]{1,0:T(8,128)S(1)}, f32[8,512]{1,0:T(8,128)S(1)}, u32[]{:S(2)}, u32[]{:S(2)}) %collective-permute-start.5) | collective-permute-done | bytes 16416 | tf_op jit(solution)/shard_map/ppermute | solution.py:548
  90.0 0.0 copy-done.2
  90.0 0.0 copy-done
  90.0 0.0 copy-done.1
  90.0 0.0 copy-done.4
  90.0 0.0 copy-done.5
  90.0 0.6 shard_map.127
  90.6 8.1 %collective-permute-start.6 = (bf16[4,128,256]{2,1,0:T(8,128)(2,1)S(1)}, bf16[4,128,256]{2,1,0:T(8,128)(2,1)S(1)}, u32[]{:S(2)}, u32[]{:S(2)}) collective-permute-start(bf16[4,128,256]{2,1,0:T(8,128)(2,1)S(1)} %shard_map.127), channel_id=1, source_target_pairs={{0,1},{1,0},{2,3},{3,2},{4,5},{5,4},{6,7},{7,6},{8,9},{9,8},{10,11... | collective-permute-start | bytes 786440 | tf_op jit(solution)/shard_map/ppermute | solution.py:526
  98.7 0.6 shard_map.126.kept_ref
  99.3 0.5 collective-permute-done.6.got_ref
  99.9 8.8 %all_to_all.29 = bf16[4,128,256]{2,1,0:T(8,128)(2,1)S(1)} all-to-all(bf16[4,128,256]{2,1,0:T(8,128)(2,1)S(1)} %shard_map.128), channel_id=1, replica_groups={{0,2,4,6},{1,3,5,7},{8,10,12,14},{9,11,13,15},{16,18,20,22},{17,19,21,2..., dimensions={0} | all-to-all | bytes 524288 | tf_op jit(solution)/shard_map/all_to_all | solution.py:523
  108.7 0.7 reduce_sum.12
  (1 shorter events, 0.0 us)
Async XLA Ops:
  11.0 9.6 %collective-permute-start = (bf16[4,128,256]{2,1,0:T(8,128)(2,1)S(1)}, bf16[4,128,256]{2,1,0:T(8,128)(2,1)S(1)}, u32[]{:S(2)}, u32[]{:S(2)}) collective-permute-start(bf16[4,128,256]{2,1,0:T(8,128)(2,1)S(1)} %all_to_all.25.x_ref), channel_id=1, source_target_pairs={{0,1},{1,0},{2,3},{3,2},{4,5},{5,4},{6,7},{7,6},{8,9},{9,8},{10,11... | collective-permute-start | bytes 786440 | tf_op jit(solution)/shard_map/ppermute | solution.py:526
  21.2 2.1 %collective-permute-start.1 = (bf16[16,512]{1,0:T(8,128)(2,1)S(1)}, bf16[16,512]{1,0:T(8,128)(2,1)S(1)}, u32[]{:S(2)}, u32[]{:S(2)}) collective-permute-start(bf16[16,512]{1,0:T(8,128)(2,1)S(1)} %get-tuple-element.35), channel_id=1, source_target_pairs={{0,8},{8,16},{16,24},{24,32},{32,40},{40,48},{48,56},{56,64},{64,7... | collective-permute-start | bytes 49160 | tf_op jit(solution)/shard_map/ppermute | solution.py:532
  22.5 0.9 copy-start.3
  38.1 14.8 %collective-permute-start.2 = (bf16[256,128]{1,0:T(8,128)(2,1)S(1)}, bf16[256,128]{1,0:T(8,128)(2,1)S(1)}, u32[]{:S(2)}, u32[]{:S(2)}) collective-permute-start(bf16[256,128]{1,0:T(8,128)(2,1)S(1)} %shard_map.122.total_ref), channel_id=1, source_target_pairs={{0,32},{16,48},{32,64},{40,8},{48,80},{56,24},{64,96},{72,40},{80,... | collective-permute-start | bytes 196616 | tf_op jit(solution)/shard_map/ppermute | solution.py:518
  47.0 10.2 %collective-permute-start.4 = (bf16[256,128]{1,0:T(8,128)(2,1)S(1)}, bf16[256,128]{1,0:T(8,128)(2,1)S(1)}, u32[]{:S(2)}, u32[]{:S(2)}) collective-permute-start(bf16[256,128]{1,0:T(8,128)(2,1)S(1)} %shard_map.122.total_ref), channel_id=1, source_target_pairs={{0,96},{16,112},{32,128},{48,144},{64,160},{80,176},{96,192},{104,... | collective-permute-start | bytes 196616 | tf_op jit(solution)/shard_map/ppermute | solution.py:518
  52.9 5.6 %collective-permute-start.3 = (bf16[256,128]{1,0:T(8,128)(2,1)S(1)}, bf16[256,128]{1,0:T(8,128)(2,1)S(1)}, u32[]{:S(2)}, u32[]{:S(2)}) collective-permute-start(bf16[256,128]{1,0:T(8,128)(2,1)S(1)} %collective-permute-done.2.last_ref), channel_id=1, source_target_pairs={{0,32},{16,48},{32,64},{40,8},{48,80},{56,24},{64,96},{72,40},{80,... | collective-permute-start | bytes 196616 | tf_op jit(solution)/shard_map/ppermute | solution.py:518
  73.4 16.6 %copy-start.2 = (bf16[2048,128]{1,0:T(8,128)(2,1)S(1)}, bf16[2048,128]{1,0:T(8,128)(2,1)}, u32[]{:S(2)}) copy-start(bf16[2048,128]{1,0:T(8,128)(2,1)} %wk_ref.3) | copy-start | bytes 1572868
  74.3 15.6 %copy-start = (bf16[2048,256]{1,0:T(8,128)(2,1)S(1)}, bf16[2048,256]{1,0:T(8,128)(2,1)}, u32[]{:S(2)}) copy-start(bf16[2048,256]{1,0:T(8,128)(2,1)} %wv_ref.3) | copy-start | bytes 3145732
  83.9 6.1 %copy-start.1 = (bf16[2048,128]{1,0:T(8,128)(2,1)S(1)}, bf16[2048,128]{1,0:T(8,128)(2,1)}, u32[]{:S(2)}) copy-start(bf16[2048,128]{1,0:T(8,128)(2,1)} %wq_ref.3) | copy-start | bytes 1572868
  83.9 6.1 %copy-start.4 = (bf16[2048,2]{0,1:T(2,128)(2,1)S(1)}, bf16[2048,2]{0,1:T(2,128)(2,1)}, u32[]{:S(2)}) copy-start(bf16[2048,2]{0,1:T(2,128)(2,1)} %param.16) | copy-start | bytes 24580
  83.9 6.1 %copy-start.5 = (bf16[2048,2]{0,1:T(2,128)(2,1)S(1)}, bf16[2048,2]{0,1:T(2,128)(2,1)}, u32[]{:S(2)}) copy-start(bf16[2048,2]{0,1:T(2,128)(2,1)} %param.17) | copy-start | bytes 24580
  85.5 4.5 %collective-permute-start.5 = (f32[8,512]{1,0:T(8,128)S(1)}, f32[8,512]{1,0:T(8,128)S(1)}, u32[]{:S(2)}, u32[]{:S(2)}) collective-permute-start(f32[8,512]{1,0:T(8,128)S(1)} %get-tuple-element.53), channel_id=1, source_target_pairs={{8,0},{16,8},{24,16},{32,24},{40,32},{48,40},{56,48},{64,56},{72,6... | collective-permute-start | bytes 49160 | tf_op jit(solution)/shard_map/ppermute | solution.py:548
  90.6 9.2 %collective-permute-start.6 = (bf16[4,128,256]{2,1,0:T(8,128)(2,1)S(1)}, bf16[4,128,256]{2,1,0:T(8,128)(2,1)S(1)}, u32[]{:S(2)}, u32[]{:S(2)}) collective-permute-start(bf16[4,128,256]{2,1,0:T(8,128)(2,1)S(1)} %shard_map.127), channel_id=1, source_target_pairs={{0,1},{1,0},{2,3},{3,2},{4,5},{5,4},{6,7},{7,6},{8,9},{9,8},{10,11... | collective-permute-start | bytes 786440 | tf_op jit(solution)/shard_map/ppermute | solution.py:526

commit v8 on v7

--- a/solution.py
+++ b/solution.py
@@ -535,8 +535,8 @@
     send, *kept = slab(proj, tail, taps, cols, gap, grad_core)
     got = exchange(send, group)
     total = call(group_kernel, [((PACK, DH), BF16)])(got)[0]
-    last = onward(total, RADIX)
-    earlier = [last, onward(last, RADIX), onward(total, 3 * RADIX)]
+    last, again = lax.optimization_barrier((onward(total, RADIX), total))
+    earlier = [last, onward(last, RADIX), onward(again, 3 * RADIX)]
     total, before = call(
         window_kernel, [((RADIX, PACK, DH), BF16), ((PACK, DH), F32)]
     )(total, *earlier)

time: 110 us -> 115 us (1.045)
  starting transfers between devices: 37.4 us -> 42.6 us
  blocking collectives: 54.3 us -> 52.4 us
  waiting for transfers between devices: 5.47 us -> 6.78 us
    ppermute x3, starting transfers between devices: 19 us -> 23.2 us  [onward(): lax.ppermute(value, 'ctx', [(s, t) for s, t in steps if 0 <= t < count])]
    all_to_all x3, blocking collectives: 35.3 us -> 33.5 us  [exchange(): return lax.all_to_all(value, 'ctx', 0, 0, axis_index_groups=groups)]
    ppermute x3, waiting for transfers between devices: 1.31 us -> 2.61 us  [onward(): lax.ppermute(value, 'ctx', [(s, t) for s, t in steps if 0 <= t < count])]
  transfers between devices with their start and end apart: 7 -> 7, of which waited for: 4 -> 5; matrix products, arithmetic and copies ran while one was open for 0% -> 0% of each run, Pallas kernels for 3% -> 3%
where the time goes in v8:
time: 115 us; the launch traced here: 114 us
  blocking collectives  52.4 us (46%)
  starting transfers between devices  42.6 us (37%)
  Pallas kernels  10.5 us (9%)
  waiting for transfers between devices  6.78 us (6%)
    all_to_all x3, blocking collectives, exchange(): return lax.all_to_all(value, 'ctx', 0, 0, axis_index_groups=groups)  33.5 us
    ppermute x3, starting transfers between devices, onward(): lax.ppermute(value, 'ctx', [(s, t) for s, t in steps if 0 <= t < count])  23.2 us
    all_to_all x2, blocking collectives, across(): return lax.all_to_all(value, 'tp', 0, 0, axis_index_groups=chips)  19 us
    ppermute x2, starting transfers between devices, between(): return lax.ppermute(value, 'tp', [(t, t ^ 1) for t in range(parts)])  16.8 us
    ppermute x1, waiting for transfers between devices, local(): halo = lax.ppermute(halo, 'ctx', [(s + 1, s) for s in range(count - 1)])  3.18 us
    pallas_call x1, Pallas kernels, slab(): call(slab_kernel, [((4, PACK, DH), BF16), ((DH, 4 * DH), F32), ((2,) + sq...  3.04 us
    ppermute x3, waiting for transfers between devices, onward(): lax.ppermute(value, 'ctx', [(s, t) for s, t in steps if 0 <= t < count])  2.61 us
  transfers between devices with their start and end apart: 7, of which 5 were waited for; matrix products, arithmetic and copies ran while one was open for 0% of the time, Pallas kernels for 3%

profile of v8, /device:TPU:1, one launch (start us, length us, event | category | flops | bytes accessed | tf_op | source)
XLA Modules:
  0.0 114.1 jit_solution(12850518511733153788)
XLA Ops:
  0.0 0.9 broadcast_in_dim.2
  0.9 10.2 %all_to_all.25.x_ref = bf16[4,128,256]{2,1,0:T(8,128)(2,1)S(1)} all-to-all(bf16[4,128,256]{2,1,0:T(8,128)(2,1)S(1)} %broadcast_in_dim.2), channel_id=1, replica_groups={{0,2,4,6},{1,3,5,7},{8,10,12,14},{9,11,13,15},{16,18,20,22},{17,19,21,2..., dimensions={0} | all-to-all | bytes 524288 | tf_op jit(solution)/shard_map/all_to_all | solution.py:523
  11.0 7.7 %collective-permute-start = (bf16[4,128,256]{2,1,0:T(8,128)(2,1)S(1)}, bf16[4,128,256]{2,1,0:T(8,128)(2,1)S(1)}, u32[]{:S(2)}, u32[]{:S(2)}) collective-permute-start(bf16[4,128,256]{2,1,0:T(8,128)(2,1)S(1)} %all_to_all.25.x_ref), channel_id=1, source_target_pairs={{0,1},{1,0},{2,3},{3,2},{4,5},{5,4},{6,7},{7,6},{8,9},{9,8},{10,11... | collective-permute-start | bytes 786440 | tf_op jit(solution)/shard_map/ppermute | solution.py:526
  18.7 1.9 %shard_map.118 = (f32[128,512]{1,0:T(8,128)S(1)}, f32[128,128]{1,0:T(8,128)S(1)}, f32[8,512]{1,0:T(8,128)S(1)}, f32[2,128,128]{2,1,0:T(8,128)S(1)}, bf16[4,256,5...) custom-call(bf16[4,128,256]{2,1,0:T(8,128)(2,1)S(1)} %all_to_all.25.x_ref, bf16[4,2,256,128]{3,2,1,0:T(8,128)(2,1)} %bitcast.8, ...), custom_call_target="tpu_custom_call" | custom-call | tf_op jit(solution)/shard_map/pallas_call | solution.py:443
  20.6 0.0 collective-permute-done.x_ref
  20.7 0.6 shard_map.119
  21.2 1.3 %collective-permute-start.1 = (bf16[16,512]{1,0:T(8,128)(2,1)S(1)}, bf16[16,512]{1,0:T(8,128)(2,1)S(1)}, u32[]{:S(2)}, u32[]{:S(2)}) collective-permute-start(bf16[16,512]{1,0:T(8,128)(2,1)S(1)} %get-tuple-element.37), channel_id=1, source_target_pairs={{0,8},{8,16},{16,24},{24,32},{32,40},{40,48},{48,56},{56,64},{64,7... | collective-permute-start | bytes 49160 | tf_op jit(solution)/shard_map/ppermute | solution.py:532
  22.5 0.0 copy-start.3
  22.5 0.4 shard_map.120
  22.9 0.5 collective-permute-done.1.tail_ref
  23.4 0.0 copy-done.3
  23.4 3.0 %shard_map.121 = (bf16[4,256,128]{2,1,0:T(8,128)(2,1)S(1)}, f32[128,512]{1,0:T(8,128)S(1)}, f32[2,128,128]{2,1,0:T(8,128)S(1)}, bf16[2,128,128]{2,1,0:T(8,128)(2...) custom-call(bf16[128,512]{1,0:T(8,128)(2,1)S(1)} %get-tuple-element., ...), custom_call_target="tpu_custom_call" | custom-call | tf_op jit(solution)/shard_map/pallas_call | solution.py:468
  26.4 11.3 %all_to_all.26.got_ref.group_ref = bf16[4,256,128]{2,1,0:T(8,128)(2,1)S(1)} all-to-all(bf16[4,256,128]{2,1,0:T(8,128)(2,1)S(1)} %get-tuple-element.43), channel_id=1, replica_groups={{0,8,16,24},{32,40,48,56},{64,72,80,88},{96,104,112,120},{128,136,144,1..., dimensions={0} | all-to-all | bytes 524288 | tf_op jit(solution)/shard_map/all_to_all | solution.py:514
  37.7 0.4 shard_map.122.total_ref
  38.1 8.8 %collective-permute-start.2 = (bf16[256,128]{1,0:T(8,128)(2,1)S(1)}, bf16[256,128]{1,0:T(8,128)(2,1)S(1)}, u32[]{:S(2)}, u32[]{:S(2)}) collective-permute-start(bf16[256,128]{1,0:T(8,128)(2,1)S(1)} %shard_map.122.total_ref), channel_id=1, source_target_pairs={{0,32},{16,48},{32,64},{40,8},{48,80},{56,24},{64,96},{72,40},{80,... | collective-permute-start | bytes 196616 | tf_op jit(solution)/shard_map/ppermute | solution.py:518
  47.0 1.3 %collective-permute-done.2.last_ref = bf16[256,128]{1,0:T(8,128)(2,1)S(1)} collective-permute-done((bf16[256,128]{1,0:T(8,128)(2,1)S(1)}, bf16[256,128]{1,0:T(8,128)(2,1)S(1)}, u32[]{:S(2)}, u32[]{:S(2)}) %collective-permute-start.2) | collective-permute-done | bytes 65568 | tf_op jit(solution)/shard_map/ppermute | solution.py:518
  48.3 8.3 %collective-permute-start.4 = (bf16[256,128]{1,0:T(8,128)(2,1)S(1)}, bf16[256,128]{1,0:T(8,128)(2,1)S(1)}, u32[]{:S(2)}, u32[]{:S(2)}) collective-permute-start(bf16[256,128]{1,0:T(8,128)(2,1)S(1)} %shard_map.122.total_ref), channel_id=1, source_target_pairs={{0,96},{16,112},{32,128},{48,144},{64,160},{80,176},{96,192},{104,... | collective-permute-start | bytes 196616 | tf_op jit(solution)/shard_map/ppermute | solution.py:518
  56.6 6.1 %collective-permute-start.3 = (bf16[256,128]{1,0:T(8,128)(2,1)S(1)}, bf16[256,128]{1,0:T(8,128)(2,1)S(1)}, u32[]{:S(2)}, u32[]{:S(2)}) collective-permute-start(bf16[256,128]{1,0:T(8,128)(2,1)S(1)} %collective-permute-done.2.last_ref), channel_id=1, source_target_pairs={{0,32},{16,48},{32,64},{40,8},{48,80},{56,24},{64,96},{72,40},{80,... | collective-permute-start | bytes 196616 | tf_op jit(solution)/shard_map/ppermute | solution.py:518
  62.7 0.0 collective-permute-done.4.first_ref
  62.7 1.3 %collective-permute-done.3.middle_ref = bf16[256,128]{1,0:T(8,128)(2,1)S(1)} collective-permute-done((bf16[256,128]{1,0:T(8,128)(2,1)S(1)}, bf16[256,128]{1,0:T(8,128)(2,1)S(1)}, u32[]{:S(2)}, u32[]{:S(2)}) %collective-permute-start.3) | collective-permute-done | bytes 65568 | tf_op jit(solution)/shard_map/ppermute | solution.py:518
  64.0 0.4 shard_map.123
  64.4 12.2 %all_to_all.27.rows_ref = bf16[4,256,128]{2,1,0:T(8,128)(2,1)S(1)} all-to-all(bf16[4,256,128]{2,1,0:T(8,128)(2,1)S(1)} %get-tuple-element.46), channel_id=1, replica_groups={{0,128,256,384},{8,136,264,392},{16,144,272,400},{24,152,280,408},{32,1..., dimensions={0} | all-to-all | bytes 524288 | tf_op jit(solution)/shard_map/all_to_all | solution.py:514
  76.7 0.0 copy-start.2
  76.7 0.9 shard_map.124
  77.6 0.0 copy-start
  77.6 9.9 %all_to_all.28.states_ref = bf16[4,128,128]{2,1,0:T(8,128)(2,1)S(1)} all-to-all(bf16[4,128,128]{2,1,0:T(8,128)(2,1)S(1)} %shard_map.124), channel_id=1, replica_groups={{0,8,16,24},{32,40,48,56},{64,72,80,88},{96,104,112,120},{128,136,144,1..., dimensions={0} | all-to-all | bytes 262144 | tf_op jit(solution)/shard_map/all_to_all | solution.py:514
  87.6 0.0 copy-start.1
  87.6 0.0 copy-start.4
  87.6 0.0 copy-start.5
  87.6 1.6 %shard_map.125 = (f32[128,512]{1,0:T(8,128)S(1)}, bf16[128,128]{1,0:T(8,128)(2,1)S(1)}, f32[8,512]{1,0:T(8,128)S(1)}) custom-call(bf16[4,128,128]{2,1,0:T(8,128)(2,1)S(1)} %all_to_all.28.states_ref, f32[128,512]{1,0:T(8,128)S(1)} %get-tuple-element.48.pre_ref, f32[2,128,128]{2,1,0:T(8,128)S(1)} %get-tuple-element.49.unit_ref, ...), custom_call_target="tpu_custom_call" | custom-call | tf_op jit(solution)/shard_map/pallas_call | solution.py:481
  89.2 1.3 %collective-permute-start.5 = (f32[8,512]{1,0:T(8,128)S(1)}, f32[8,512]{1,0:T(8,128)S(1)}, u32[]{:S(2)}, u32[]{:S(2)}) collective-permute-start(f32[8,512]{1,0:T(8,128)S(1)} %get-tuple-element.57), channel_id=1, source_target_pairs={{8,0},{16,8},{24,16},{32,24},{40,32},{48,40},{56,48},{64,56},{72,6... | collective-permute-start | bytes 49160 | tf_op jit(solution)/shard_map/ppermute | solution.py:548
  90.5 3.2 %collective-permute-done.5.halo_ref = f32[8,512]{1,0:T(8,128)S(1)} collective-permute-done((f32[8,512]{1,0:T(8,128)S(1)}, f32[8,512]{1,0:T(8,128)S(1)}, u32[]{:S(2)}, u32[]{:S(2)}) %collective-permute-start.5) | collective-permute-done | bytes 16416 | tf_op jit(solution)/shard_map/ppermute | solution.py:548
  93.6 0.0 copy-done.2
  93.6 0.0 copy-done
  93.7 0.0 copy-done.1
  93.7 0.0 copy-done.4
  93.7 0.0 copy-done.5
  93.7 0.6 shard_map.127
  94.3 9.2 %collective-permute-start.6 = (bf16[4,128,256]{2,1,0:T(8,128)(2,1)S(1)}, bf16[4,128,256]{2,1,0:T(8,128)(2,1)S(1)}, u32[]{:S(2)}, u32[]{:S(2)}) collective-permute-start(bf16[4,128,256]{2,1,0:T(8,128)(2,1)S(1)} %shard_map.127), channel_id=1, source_target_pairs={{0,1},{1,0},{2,3},{3,2},{4,5},{5,4},{6,7},{7,6},{8,9},{9,8},{10,11... | collective-permute-start | bytes 786440 | tf_op jit(solution)/shard_map/ppermute | solution.py:526
  103.5 0.6 shard_map.126.kept_ref
  104.1 0.5 collective-permute-done.6.got_ref
  104.7 8.8 %all_to_all.29 = bf16[4,128,256]{2,1,0:T(8,128)(2,1)S(1)} all-to-all(bf16[4,128,256]{2,1,0:T(8,128)(2,1)S(1)} %shard_map.128), channel_id=1, replica_groups={{0,2,4,6},{1,3,5,7},{8,10,12,14},{9,11,13,15},{16,18,20,22},{17,19,21,2..., dimensions={0} | all-to-all | bytes 524288 | tf_op jit(solution)/shard_map/all_to_all | solution.py:523
  113.5 0.7 reduce_sum.12
  (1 shorter events, 0.0 us)
Async XLA Ops:
  11.0 9.6 %collective-permute-start = (bf16[4,128,256]{2,1,0:T(8,128)(2,1)S(1)}, bf16[4,128,256]{2,1,0:T(8,128)(2,1)S(1)}, u32[]{:S(2)}, u32[]{:S(2)}) collective-permute-start(bf16[4,128,256]{2,1,0:T(8,128)(2,1)S(1)} %all_to_all.25.x_ref), channel_id=1, source_target_pairs={{0,1},{1,0},{2,3},{3,2},{4,5},{5,4},{6,7},{7,6},{8,9},{9,8},{10,11... | collective-permute-start | bytes 786440 | tf_op jit(solution)/shard_map/ppermute | solution.py:526
  21.2 2.1 %collective-permute-start.1 = (bf16[16,512]{1,0:T(8,128)(2,1)S(1)}, bf16[16,512]{1,0:T(8,128)(2,1)S(1)}, u32[]{:S(2)}, u32[]{:S(2)}) collective-permute-start(bf16[16,512]{1,0:T(8,128)(2,1)S(1)} %get-tuple-element.37), channel_id=1, source_target_pairs={{0,8},{8,16},{16,24},{24,32},{32,40},{40,48},{48,56},{56,64},{64,7... | collective-permute-start | bytes 49160 | tf_op jit(solution)/shard_map/ppermute | solution.py:532
  22.5 0.9 copy-start.3
  38.1 10.1 %collective-permute-start.2 = (bf16[256,128]{1,0:T(8,128)(2,1)S(1)}, bf16[256,128]{1,0:T(8,128)(2,1)S(1)}, u32[]{:S(2)}, u32[]{:S(2)}) collective-permute-start(bf16[256,128]{1,0:T(8,128)(2,1)S(1)} %shard_map.122.total_ref), channel_id=1, source_target_pairs={{0,32},{16,48},{32,64},{40,8},{48,80},{56,24},{64,96},{72,40},{80,... | collective-permute-start | bytes 196616 | tf_op jit(solution)/shard_map/ppermute | solution.py:518
  48.3 14.4 %collective-permute-start.4 = (bf16[256,128]{1,0:T(8,128)(2,1)S(1)}, bf16[256,128]{1,0:T(8,128)(2,1)S(1)}, u32[]{:S(2)}, u32[]{:S(2)}) collective-permute-start(bf16[256,128]{1,0:T(8,128)(2,1)S(1)} %shard_map.122.total_ref), channel_id=1, source_target_pairs={{0,96},{16,112},{32,128},{48,144},{64,160},{80,176},{96,192},{104,... | collective-permute-start | bytes 196616 | tf_op jit(solution)/shard_map/ppermute | solution.py:518
  56.6 7.4 %collective-permute-start.3 = (bf16[256,128]{1,0:T(8,128)(2,1)S(1)}, bf16[256,128]{1,0:T(8,128)(2,1)S(1)}, u32[]{:S(2)}, u32[]{:S(2)}) collective-permute-start(bf16[256,128]{1,0:T(8,128)(2,1)S(1)} %collective-permute-done.2.last_ref), channel_id=1, source_target_pairs={{0,32},{16,48},{32,64},{40,8},{48,80},{56,24},{64,96},{72,40},{80,... | collective-permute-start | bytes 196616 | tf_op jit(solution)/shard_map/ppermute | solution.py:518
  76.7 17.0 %copy-start.2 = (bf16[2048,128]{1,0:T(8,128)(2,1)S(1)}, bf16[2048,128]{1,0:T(8,128)(2,1)}, u32[]{:S(2)}) copy-start(bf16[2048,128]{1,0:T(8,128)(2,1)} %wk_ref.3) | copy-start | bytes 1572868
  77.6 16.0 %copy-start = (bf16[2048,256]{1,0:T(8,128)(2,1)S(1)}, bf16[2048,256]{1,0:T(8,128)(2,1)}, u32[]{:S(2)}) copy-start(bf16[2048,256]{1,0:T(8,128)(2,1)} %wv_ref.3) | copy-start | bytes 3145732
  87.6 6.1 %copy-start.1 = (bf16[2048,128]{1,0:T(8,128)(2,1)S(1)}, bf16[2048,128]{1,0:T(8,128)(2,1)}, u32[]{:S(2)}) copy-start(bf16[2048,128]{1,0:T(8,128)(2,1)} %wq_ref.3) | copy-start | bytes 1572868
  87.6 6.1 %copy-start.4 = (bf16[2048,2]{0,1:T(2,128)(2,1)S(1)}, bf16[2048,2]{0,1:T(2,128)(2,1)}, u32[]{:S(2)}) copy-start(bf16[2048,2]{0,1:T(2,128)(2,1)} %param.16) | copy-start | bytes 24580
  87.6 6.1 %copy-start.5 = (bf16[2048,2]{0,1:T(2,128)(2,1)S(1)}, bf16[2048,2]{0,1:T(2,128)(2,1)}, u32[]{:S(2)}) copy-start(bf16[2048,2]{0,1:T(2,128)(2,1)} %param.17) | copy-start | bytes 24580
  89.2 4.5 %collective-permute-start.5 = (f32[8,512]{1,0:T(8,128)S(1)}, f32[8,512]{1,0:T(8,128)S(1)}, u32[]{:S(2)}, u32[]{:S(2)}) collective-permute-start(f32[8,512]{1,0:T(8,128)S(1)} %get-tuple-element.57), channel_id=1, source_target_pairs={{8,0},{16,8},{24,16},{32,24},{40,32},{48,40},{56,48},{64,56},{72,6... | collective-permute-start | bytes 49160 | tf_op jit(solution)/shard_map/ppermute | solution.py:548
  94.3 10.3 %collective-permute-start.6 = (bf16[4,128,256]{2,1,0:T(8,128)(2,1)S(1)}, bf16[4,128,256]{2,1,0:T(8,128)(2,1)S(1)}, u32[]{:S(2)}, u32[]{:S(2)}) collective-permute-start(bf16[4,128,256]{2,1,0:T(8,128)(2,1)S(1)} %shard_map.127), channel_id=1, source_target_pairs={{0,1},{1,0},{2,3},{3,2},{4,5},{5,4},{6,7},{7,6},{8,9},{9,8},{10,11... | collective-permute-start | bytes 786440 | tf_op jit(solution)/shard_map/ppermute | solution.py:526

commit v9 on v7

--- a/solution.py
+++ b/solution.py
@@ -78,11 +78,12 @@
     size = 8
     while size < DH:
         off = (row // (2 * size) == col // (2 * size)) & (row // size != col // size)
+        times = dot3 if size < 32 else dot
         products = [
-            dot3(result, jnp.where(off, strict, 0.0)) for result, strict in zip(results, stricts)
+            times(result, jnp.where(off, strict, 0.0)) for result, strict in zip(results, stricts)
         ]
         results = [
-            result - dot3(product, result) for result, product in zip(results, products)
+            result - times(product, result) for result, product in zip(results, products)
         ]
         size *= 2
     return results
@@ -212,7 +213,7 @@
         gamma = jnp.exp(cum)
         last = cum[DH - 1 : DH, :]
         key_tail = jnp.exp(last - cum) * key
-        both = dot3(inverse, jnp.concatenate([beta * value, (beta * gamma) * key], axis=1))
+        both = dot(inverse, jnp.concatenate([beta * value, (beta * gamma) * key], axis=1))
         mixed = both[:, :DH]
         weighted = both[:, DH:]
         back = dot(cross * gap_ref[head], grad, (0, 0))
@@ -419,6 +420,13 @@
     out_ref[...] = bf(kept_ref[...] + got_ref[...].astype(F32))
 
 
+def total_kernel(shares_ref, out_ref):
+    total = shares_ref[0].astype(F32)
+    for part in range(1, shares_ref.shape[0]):
+        total = total + shares_ref[part].astype(F32)
+    out_ref[...] = bf(total)
+
+
 def call(kernel, outs, scratch=(), specs=None):
     extra = {} if specs is None else {"in_specs": specs}
     return pl.pallas_call(
@@ -549,7 +557,7 @@
     given = between(spread(full, halo, grad_gates, weights, parts // 2, True))
     kept = spread(full, halo, grad_gates, weights, parts // 2, False)
     shares = call(merge_kernel, [(given.shape, BF16)])(kept, given)[0]
-    return jnp.sum(across(shares).astype(F32), axis=0).astype(BF16)
+    return call(total_kernel, [(shares.shape[1:], BF16)])(across(shares))[0]
 
 
 def solution(mesh):

time: 110 us -> 110 us (level)
  no operation moved by 1% of the time
where the time goes in v9:
time: 110 us; the launch traced here: 109 us
  blocking collectives  54.3 us (49%)
  starting transfers between devices  37.3 us (34%)
  Pallas kernels  10.9 us (10%)
  waiting for transfers between devices  5.47 us (5%)
    all_to_all x3, blocking collectives, exchange(): return lax.all_to_all(value, 'ctx', 0, 0, axis_index_groups=groups)  35.3 us
    ppermute x3, starting transfers between devices, onward(): lax.ppermute(value, 'ctx', [(s, t) for s, t in steps if 0 <= t < count])  19 us
    all_to_all x2, blocking collectives, across(): return lax.all_to_all(value, 'tp', 0, 0, axis_index_groups=chips)  19 us
    ppermute x2, starting transfers between devices, between(): return lax.ppermute(value, 'tp', [(t, t ^ 1) for t in range(parts)])  15.7 us
    ppermute x1, waiting for transfers between devices, local(): halo = lax.ppermute(halo, 'ctx', [(s + 1, s) for s in range(count - 1)])  3.18 us
    pallas_call x1, Pallas kernels, slab(): call(slab_kernel, [((4, PACK, DH), BF16), ((DH, 4 * DH), F32), ((2,) + sq...  2.73 us
  transfers between devices with their start and end apart: 7, of which 4 were waited for; matrix products, arithmetic and copies ran while one was open for 0% of the time, Pallas kernels for 3%

profile of v9, /device:TPU:1, one launch (start us, length us, event | category | flops | bytes accessed | tf_op | source)
XLA Modules:
  0.0 109.0 jit_solution(13779583072917857254)
XLA Ops:
  0.0 0.9 broadcast_in_dim.2
  0.9 10.2 %all_to_all.25.x_ref = bf16[4,128,256]{2,1,0:T(8,128)(2,1)S(1)} all-to-all(bf16[4,128,256]{2,1,0:T(8,128)(2,1)S(1)} %broadcast_in_dim.2), channel_id=1, replica_groups={{0,2,4,6},{1,3,5,7},{8,10,12,14},{9,11,13,15},{16,18,20,22},{17,19,21,2..., dimensions={0} | all-to-all | bytes 524288 | tf_op jit(solution)/shard_map/all_to_all | solution.py:531
  11.0 7.7 %collective-permute-start = (bf16[4,128,256]{2,1,0:T(8,128)(2,1)S(1)}, bf16[4,128,256]{2,1,0:T(8,128)(2,1)S(1)}, u32[]{:S(2)}, u32[]{:S(2)}) collective-permute-start(bf16[4,128,256]{2,1,0:T(8,128)(2,1)S(1)} %all_to_all.25.x_ref), channel_id=1, source_target_pairs={{0,1},{1,0},{2,3},{3,2},{4,5},{5,4},{6,7},{7,6},{8,9},{9,8},{10,11... | collective-permute-start | bytes 786440 | tf_op jit(solution)/shard_map/ppermute | solution.py:534
  18.7 1.9 %shard_map.118 = (f32[128,512]{1,0:T(8,128)S(1)}, f32[128,128]{1,0:T(8,128)S(1)}, f32[8,512]{1,0:T(8,128)S(1)}, f32[2,128,128]{2,1,0:T(8,128)S(1)}, bf16[4,256,5...) custom-call(bf16[4,128,256]{2,1,0:T(8,128)(2,1)S(1)} %all_to_all.25.x_ref, bf16[4,2,256,128]{3,2,1,0:T(8,128)(2,1)} %bitcast.8, ...), custom_call_target="tpu_custom_call" | custom-call | tf_op jit(solution)/shard_map/pallas_call | solution.py:451
  20.6 0.0 collective-permute-done.x_ref
  20.7 0.6 shard_map.119
  21.2 1.3 %collective-permute-start.1 = (bf16[16,512]{1,0:T(8,128)(2,1)S(1)}, bf16[16,512]{1,0:T(8,128)(2,1)S(1)}, u32[]{:S(2)}, u32[]{:S(2)}) collective-permute-start(bf16[16,512]{1,0:T(8,128)(2,1)S(1)} %get-tuple-element.35), channel_id=1, source_target_pairs={{0,8},{8,16},{16,24},{24,32},{32,40},{40,48},{48,56},{56,64},{64,7... | collective-permute-start | bytes 49160 | tf_op jit(solution)/shard_map/ppermute | solution.py:540
  22.5 0.0 copy-start.3
  22.5 0.4 shard_map.120
  22.9 0.5 collective-permute-done.1.tail_ref
  23.4 0.0 copy-done.3
  23.4 2.7 %shard_map.121 = (bf16[4,256,128]{2,1,0:T(8,128)(2,1)S(1)}, f32[128,512]{1,0:T(8,128)S(1)}, f32[2,128,128]{2,1,0:T(8,128)S(1)}, bf16[2,128,128]{2,1,0:T(8,128)(2...) custom-call(bf16[128,512]{1,0:T(8,128)(2,1)S(1)} %get-tuple-element., ...), custom_call_target="tpu_custom_call" | custom-call | tf_op jit(solution)/shard_map/pallas_call | solution.py:476
  26.1 11.3 %all_to_all.26.got_ref.group_ref = bf16[4,256,128]{2,1,0:T(8,128)(2,1)S(1)} all-to-all(bf16[4,256,128]{2,1,0:T(8,128)(2,1)S(1)} %get-tuple-element.41), channel_id=1, replica_groups={{0,8,16,24},{32,40,48,56},{64,72,80,88},{96,104,112,120},{128,136,144,1..., dimensions={0} | all-to-all | bytes 524288 | tf_op jit(solution)/shard_map/all_to_all | solution.py:522
  37.4 0.4 shard_map.122.total_ref
  37.8 8.8 %collective-permute-start.2 = (bf16[256,128]{1,0:T(8,128)(2,1)S(1)}, bf16[256,128]{1,0:T(8,128)(2,1)S(1)}, u32[]{:S(2)}, u32[]{:S(2)}) collective-permute-start(bf16[256,128]{1,0:T(8,128)(2,1)S(1)} %shard_map.122.total_ref), channel_id=1, source_target_pairs={{0,32},{16,48},{32,64},{40,8},{48,80},{56,24},{64,96},{72,40},{80,... | collective-permute-start | bytes 196616 | tf_op jit(solution)/shard_map/ppermute | solution.py:526
  46.6 5.9 %collective-permute-start.4 = (bf16[256,128]{1,0:T(8,128)(2,1)S(1)}, bf16[256,128]{1,0:T(8,128)(2,1)S(1)}, u32[]{:S(2)}, u32[]{:S(2)}) collective-permute-start(bf16[256,128]{1,0:T(8,128)(2,1)S(1)} %shard_map.122.total_ref), channel_id=1, source_target_pairs={{0,96},{16,112},{32,128},{48,144},{64,160},{80,176},{96,192},{104,... | collective-permute-start | bytes 196616 | tf_op jit(solution)/shard_map/ppermute | solution.py:526
  52.6 0.0 collective-permute-done.2.last_ref
  52.6 4.3 %collective-permute-start.3 = (bf16[256,128]{1,0:T(8,128)(2,1)S(1)}, bf16[256,128]{1,0:T(8,128)(2,1)S(1)}, u32[]{:S(2)}, u32[]{:S(2)}) collective-permute-start(bf16[256,128]{1,0:T(8,128)(2,1)S(1)} %collective-permute-done.2.last_ref), channel_id=1, source_target_pairs={{0,32},{16,48},{32,64},{40,8},{48,80},{56,24},{64,96},{72,40},{80,... | collective-permute-start | bytes 196616 | tf_op jit(solution)/shard_map/ppermute | solution.py:526
  56.9 0.0 collective-permute-done.4.first_ref
  56.9 1.3 %collective-permute-done.3.middle_ref = bf16[256,128]{1,0:T(8,128)(2,1)S(1)} collective-permute-done((bf16[256,128]{1,0:T(8,128)(2,1)S(1)}, bf16[256,128]{1,0:T(8,128)(2,1)S(1)}, u32[]{:S(2)}, u32[]{:S(2)}) %collective-permute-start.3) | collective-permute-done | bytes 65568 | tf_op jit(solution)/shard_map/ppermute | solution.py:526
  58.2 0.4 shard_map.123
  58.6 14.4 %all_to_all.27.rows_ref = bf16[4,256,128]{2,1,0:T(8,128)(2,1)S(1)} all-to-all(bf16[4,256,128]{2,1,0:T(8,128)(2,1)S(1)} %get-tuple-element.42), channel_id=1, replica_groups={{0,128,256,384},{8,136,264,392},{16,144,272,400},{24,152,280,408},{32,1..., dimensions={0} | all-to-all | bytes 524288 | tf_op jit(solution)/shard_map/all_to_all | solution.py:522
  73.1 0.0 copy-start.2
  73.1 0.9 shard_map.124
  74.0 0.0 copy-start
  74.0 9.5 %all_to_all.28.states_ref = bf16[4,128,128]{2,1,0:T(8,128)(2,1)S(1)} all-to-all(bf16[4,128,128]{2,1,0:T(8,128)(2,1)S(1)} %shard_map.124), channel_id=1, replica_groups={{0,8,16,24},{32,40,48,56},{64,72,80,88},{96,104,112,120},{128,136,144,1..., dimensions={0} | all-to-all | bytes 262144 | tf_op jit(solution)/shard_map/all_to_all | solution.py:522
  83.6 0.0 copy-start.1
  83.6 0.0 copy-start.4
  83.6 0.0 copy-start.5
  83.6 1.6 %shard_map.125 = (f32[128,512]{1,0:T(8,128)S(1)}, bf16[128,128]{1,0:T(8,128)(2,1)S(1)}, f32[8,512]{1,0:T(8,128)S(1)}) custom-call(bf16[4,128,128]{2,1,0:T(8,128)(2,1)S(1)} %all_to_all.28.states_ref, f32[128,512]{1,0:T(8,128)S(1)} %get-tuple-element.44.pre_ref, f32[2,128,128]{2,1,0:T(8,128)S(1)} %get-tuple-element.45.unit_ref, ...), custom_call_target="tpu_custom_call" | custom-call | tf_op jit(solution)/shard_map/pallas_call | solution.py:489
  85.2 1.3 %collective-permute-start.5 = (f32[8,512]{1,0:T(8,128)S(1)}, f32[8,512]{1,0:T(8,128)S(1)}, u32[]{:S(2)}, u32[]{:S(2)}) collective-permute-start(f32[8,512]{1,0:T(8,128)S(1)} %get-tuple-element.53), channel_id=1, source_target_pairs={{8,0},{16,8},{24,16},{32,24},{40,32},{48,40},{56,48},{64,56},{72,6... | collective-permute-start | bytes 49160 | tf_op jit(solution)/shard_map/ppermute | solution.py:556
  86.5 3.2 %collective-permute-done.5.halo_ref = f32[8,512]{1,0:T(8,128)S(1)} collective-permute-done((f32[8,512]{1,0:T(8,128)S(1)}, f32[8,512]{1,0:T(8,128)S(1)}, u32[]{:S(2)}, u32[]{:S(2)}) %collective-permute-start.5) | collective-permute-done | bytes 16416 | tf_op jit(solution)/shard_map/ppermute | solution.py:556
  89.6 0.0 copy-done.2
  89.6 0.0 copy-done
  89.7 0.0 copy-done.1
  89.7 0.0 copy-done.4
  89.7 0.0 copy-done.5
  89.7 0.6 shard_map.127
  90.3 8.1 %collective-permute-start.6 = (bf16[4,128,256]{2,1,0:T(8,128)(2,1)S(1)}, bf16[4,128,256]{2,1,0:T(8,128)(2,1)S(1)}, u32[]{:S(2)}, u32[]{:S(2)}) collective-permute-start(bf16[4,128,256]{2,1,0:T(8,128)(2,1)S(1)} %shard_map.127), channel_id=1, source_target_pairs={{0,1},{1,0},{2,3},{3,2},{4,5},{5,4},{6,7},{7,6},{8,9},{9,8},{10,11... | collective-permute-start | bytes 786440 | tf_op jit(solution)/shard_map/ppermute | solution.py:534
  98.4 0.6 shard_map.126.kept_ref
  99.0 0.5 collective-permute-done.6.got_ref
  99.6 8.8 %all_to_all.29.shares_ref = bf16[4,128,256]{2,1,0:T(8,128)(2,1)S(1)} all-to-all(bf16[4,128,256]{2,1,0:T(8,128)(2,1)S(1)} %shard_map.128), channel_id=1, replica_groups={{0,2,4,6},{1,3,5,7},{8,10,12,14},{9,11,13,15},{16,18,20,22},{17,19,21,2..., dimensions={0} | all-to-all | bytes 524288 | tf_op jit(solution)/shard_map/all_to_all | solution.py:531
  108.4 0.7 shard_map.129
  (1 shorter events, 0.0 us)
Async XLA Ops:
  11.0 9.6 %collective-permute-start = (bf16[4,128,256]{2,1,0:T(8,128)(2,1)S(1)}, bf16[4,128,256]{2,1,0:T(8,128)(2,1)S(1)}, u32[]{:S(2)}, u32[]{:S(2)}) collective-permute-start(bf16[4,128,256]{2,1,0:T(8,128)(2,1)S(1)} %all_to_all.25.x_ref), channel_id=1, source_target_pairs={{0,1},{1,0},{2,3},{3,2},{4,5},{5,4},{6,7},{7,6},{8,9},{9,8},{10,11... | collective-permute-start | bytes 786440 | tf_op jit(solution)/shard_map/ppermute | solution.py:534
  21.2 2.1 %collective-permute-start.1 = (bf16[16,512]{1,0:T(8,128)(2,1)S(1)}, bf16[16,512]{1,0:T(8,128)(2,1)S(1)}, u32[]{:S(2)}, u32[]{:S(2)}) collective-permute-start(bf16[16,512]{1,0:T(8,128)(2,1)S(1)} %get-tuple-element.35), channel_id=1, source_target_pairs={{0,8},{8,16},{16,24},{24,32},{32,40},{40,48},{48,56},{56,64},{64,7... | collective-permute-start | bytes 49160 | tf_op jit(solution)/shard_map/ppermute | solution.py:540
  22.5 0.9 copy-start.3
  37.8 14.8 %collective-permute-start.2 = (bf16[256,128]{1,0:T(8,128)(2,1)S(1)}, bf16[256,128]{1,0:T(8,128)(2,1)S(1)}, u32[]{:S(2)}, u32[]{:S(2)}) collective-permute-start(bf16[256,128]{1,0:T(8,128)(2,1)S(1)} %shard_map.122.total_ref), channel_id=1, source_target_pairs={{0,32},{16,48},{32,64},{40,8},{48,80},{56,24},{64,96},{72,40},{80,... | collective-permute-start | bytes 196616 | tf_op jit(solution)/shard_map/ppermute | solution.py:526
  46.6 10.2 %collective-permute-start.4 = (bf16[256,128]{1,0:T(8,128)(2,1)S(1)}, bf16[256,128]{1,0:T(8,128)(2,1)S(1)}, u32[]{:S(2)}, u32[]{:S(2)}) collective-permute-start(bf16[256,128]{1,0:T(8,128)(2,1)S(1)} %shard_map.122.total_ref), channel_id=1, source_target_pairs={{0,96},{16,112},{32,128},{48,144},{64,160},{80,176},{96,192},{104,... | collective-permute-start | bytes 196616 | tf_op jit(solution)/shard_map/ppermute | solution.py:526
  52.6 5.6 %collective-permute-start.3 = (bf16[256,128]{1,0:T(8,128)(2,1)S(1)}, bf16[256,128]{1,0:T(8,128)(2,1)S(1)}, u32[]{:S(2)}, u32[]{:S(2)}) collective-permute-start(bf16[256,128]{1,0:T(8,128)(2,1)S(1)} %collective-permute-done.2.last_ref), channel_id=1, source_target_pairs={{0,32},{16,48},{32,64},{40,8},{48,80},{56,24},{64,96},{72,40},{80,... | collective-permute-start | bytes 196616 | tf_op jit(solution)/shard_map/ppermute | solution.py:526
  73.1 16.6 %copy-start.2 = (bf16[2048,128]{1,0:T(8,128)(2,1)S(1)}, bf16[2048,128]{1,0:T(8,128)(2,1)}, u32[]{:S(2)}) copy-start(bf16[2048,128]{1,0:T(8,128)(2,1)} %wk_ref.3) | copy-start | bytes 1572868
  74.0 15.6 %copy-start = (bf16[2048,256]{1,0:T(8,128)(2,1)S(1)}, bf16[2048,256]{1,0:T(8,128)(2,1)}, u32[]{:S(2)}) copy-start(bf16[2048,256]{1,0:T(8,128)(2,1)} %wv_ref.3) | copy-start | bytes 3145732
  83.6 6.1 %copy-start.1 = (bf16[2048,128]{1,0:T(8,128)(2,1)S(1)}, bf16[2048,128]{1,0:T(8,128)(2,1)}, u32[]{:S(2)}) copy-start(bf16[2048,128]{1,0:T(8,128)(2,1)} %wq_ref.3) | copy-start | bytes 1572868
  83.6 6.1 %copy-start.4 = (bf16[2048,2]{0,1:T(2,128)(2,1)S(1)}, bf16[2048,2]{0,1:T(2,128)(2,1)}, u32[]{:S(2)}) copy-start(bf16[2048,2]{0,1:T(2,128)(2,1)} %param.16) | copy-start | bytes 24580
  83.6 6.1 %copy-start.5 = (bf16[2048,2]{0,1:T(2,128)(2,1)S(1)}, bf16[2048,2]{0,1:T(2,128)(2,1)}, u32[]{:S(2)}) copy-start(bf16[2048,2]{0,1:T(2,128)(2,1)} %param.17) | copy-start | bytes 24580
  85.2 4.5 %collective-permute-start.5 = (f32[8,512]{1,0:T(8,128)S(1)}, f32[8,512]{1,0:T(8,128)S(1)}, u32[]{:S(2)}, u32[]{:S(2)}) collective-permute-start(f32[8,512]{1,0:T(8,128)S(1)} %get-tuple-element.53), channel_id=1, source_target_pairs={{8,0},{16,8},{24,16},{32,24},{40,32},{48,40},{56,48},{64,56},{72,6... | collective-permute-start | bytes 49160 | tf_op jit(solution)/shard_map/ppermute | solution.py:556
  90.3 9.2 %collective-permute-start.6 = (bf16[4,128,256]{2,1,0:T(8,128)(2,1)S(1)}, bf16[4,128,256]{2,1,0:T(8,128)(2,1)S(1)}, u32[]{:S(2)}, u32[]{:S(2)}) collective-permute-start(bf16[4,128,256]{2,1,0:T(8,128)(2,1)S(1)} %shard_map.127), channel_id=1, source_target_pairs={{0,1},{1,0},{2,3},{3,2},{4,5},{5,4},{6,7},{7,6},{8,9},{9,8},{10,11... | collective-permute-start | bytes 786440 | tf_op jit(solution)/shard_map/ppermute | solution.py:534

commit v10 on v9

--- a/solution.py
+++ b/solution.py
@@ -223,10 +223,12 @@
         back_ref[head] = back
         ahead = dot(key_tail, both, (0, 0))
         lost = jnp.where(row == col, 1.0 - jnp.exp(last), 0.0) + ahead[:, DH:]
-        send_ref[2 * head, 0:DH] = bf(lost)
-        send_ref[2 * head, DH:] = bf(ahead[:, :DH])
-        send_ref[2 * head + 1, 0:DH] = bf(lost.T)
-        send_ref[2 * head + 1, DH:] = bf(
+        place = 2 * head + core_place()
+        send_ref[place, 0:DH] = bf(lost)
+        send_ref[place, DH:] = bf(ahead[:, :DH])
+        place = 2 * head + 1 - core_place()
+        send_ref[place, 0:DH] = bf(lost.T)
+        send_ref[place, DH:] = bf(
             dot(gamma * query, grad, (0, 0)) - dot(weighted, back, (0, 0))
         )
 
@@ -254,7 +256,7 @@
 
 
 def is_backward():
-    return lax.axis_index("ctx") % 2 == 1
+    return (lax.axis_index("ctx") + core_place()) % 2 == 1
 
 
 def in_order(step, backward):
@@ -314,8 +316,8 @@
     columns = jnp.zeros((DH, DH), F32)
     sides = []
     for head in range(2):
-        state = states_ref[2 * head]
-        after = states_ref[2 * head + 1]
+        state = states_ref[2 * head + core_place()]
+        after = states_ref[2 * head + 1 - core_place()]
         beta = cols[:, head : head + 1]
         cum = cols[:, 2 + head : 3 + head]
         gamma = jnp.exp(cum)
@@ -522,8 +524,12 @@
         return lax.all_to_all(value, "ctx", 0, 0, axis_index_groups=groups)
 
     def onward(value, distance):
-        steps = [(s, s - distance if s % 2 else s + distance) for s in slabs]
-        return lax.ppermute(value, "ctx", [(s, t) for s, t in steps if 0 <= t < count])
+        steps = [
+            (s, s - distance if (s + t) % 2 else s + distance, t)
+            for s in slabs for t in range(parts)
+        ]
+        pairs = [(s * parts + t, d * parts + t) for s, d, t in steps if 0 <= d < count]
+        return lax.ppermute(value, ("ctx", "tp"), pairs)
 
     chips = [[2 * chip + core for chip in range(parts // 2)] for core in range(2)]
 

time: 110 us -> 110 us (level)
  waiting for transfers between devices: 5.47 us -> 20.6 us
  starting transfers between devices: 37.3 us -> 23.3 us
    ppermute x3, waiting for transfers between devices: 1.31 us -> 16.5 us  [onward(): return lax.ppermute(value, ('ctx', 'tp'), pairs)]
    ppermute x3, starting transfers between devices: 19 us -> 3.86 us  [onward(): return lax.ppermute(value, ('ctx', 'tp'), pairs)]
    ppermute x2, starting transfers between devices: 15.7 us -> 16.9 us  [between(): return lax.ppermute(value, 'tp', [(t, t ^ 1) for t in range(parts)])]
  transfers between devices with their start and end apart: 7 -> 7, of which waited for: 4 -> 6; matrix products, arithmetic and copies ran while one was open for 0% -> 0% of each run, Pallas kernels for 3% -> 3%
where the time goes in v10:
time: 110 us; the launch traced here: 109 us
  blocking collectives  53.4 us (49%)
  starting transfers between devices  23.3 us (21%)
  waiting for transfers between devices  20.6 us (19%)
  Pallas kernels  10.9 us (10%)
    all_to_all x3, blocking collectives, exchange(): return lax.all_to_all(value, 'ctx', 0, 0, axis_index_groups=groups)  34.5 us
    all_to_all x2, blocking collectives, across(): return lax.all_to_all(value, 'tp', 0, 0, axis_index_groups=chips)  19 us
    ppermute x2, starting transfers between devices, between(): return lax.ppermute(value, 'tp', [(t, t ^ 1) for t in range(parts)])  16.9 us
    ppermute x3, waiting for transfers between devices, onward(): return lax.ppermute(value, ('ctx', 'tp'), pairs)  16.5 us
    ppermute x3, starting transfers between devices, onward(): return lax.ppermute(value, ('ctx', 'tp'), pairs)  3.86 us
    ppermute x1, waiting for transfers between devices, local(): halo = lax.ppermute(halo, 'ctx', [(s + 1, s) for s in range(count - 1)])  3.18 us
    pallas_call x1, Pallas kernels, slab(): call(slab_kernel, [((4, PACK, DH), BF16), ((DH, 4 * DH), F32), ((2,) + sq...  2.73 us
  transfers between devices with their start and end apart: 7, of which 6 were waited for; matrix products, arithmetic and copies ran while one was open for 0% of the time, Pallas kernels for 3%

profile of v10, /device:TPU:1, one launch (start us, length us, event | category | flops | bytes accessed | tf_op | source)
XLA Modules:
  0.0 109.4 jit_solution(3607315017267193318)
XLA Ops:
  0.0 0.9 broadcast_in_dim.2
  0.9 10.2 %all_to_all.25.x_ref = bf16[4,128,256]{2,1,0:T(8,128)(2,1)S(1)} all-to-all(bf16[4,128,256]{2,1,0:T(8,128)(2,1)S(1)} %broadcast_in_dim.2), channel_id=1, replica_groups={{0,2,4,6},{1,3,5,7},{8,10,12,14},{9,11,13,15},{16,18,20,22},{17,19,21,2..., dimensions={0} | all-to-all | bytes 524288 | tf_op jit(solution)/shard_map/all_to_all | solution.py:537
  11.0 7.7 %collective-permute-start = (bf16[4,128,256]{2,1,0:T(8,128)(2,1)S(1)}, bf16[4,128,256]{2,1,0:T(8,128)(2,1)S(1)}, u32[]{:S(2)}, u32[]{:S(2)}) collective-permute-start(bf16[4,128,256]{2,1,0:T(8,128)(2,1)S(1)} %all_to_all.25.x_ref), channel_id=1, source_target_pairs={{0,1},{1,0},{2,3},{3,2},{4,5},{5,4},{6,7},{7,6},{8,9},{9,8},{10,11... | collective-permute-start | bytes 786440 | tf_op jit(solution)/shard_map/ppermute | solution.py:540
  18.7 1.9 %shard_map.118 = (f32[128,512]{1,0:T(8,128)S(1)}, f32[128,128]{1,0:T(8,128)S(1)}, f32[8,512]{1,0:T(8,128)S(1)}, f32[2,128,128]{2,1,0:T(8,128)S(1)}, bf16[4,256,5...) custom-call(bf16[4,128,256]{2,1,0:T(8,128)(2,1)S(1)} %all_to_all.25.x_ref, bf16[4,2,256,128]{3,2,1,0:T(8,128)(2,1)} %bitcast.8, ...), custom_call_target="tpu_custom_call" | custom-call | tf_op jit(solution)/shard_map/pallas_call | solution.py:453
  20.6 0.0 collective-permute-done.x_ref
  20.7 0.6 shard_map.119
  21.2 1.3 %collective-permute-start.1 = (bf16[16,512]{1,0:T(8,128)(2,1)S(1)}, bf16[16,512]{1,0:T(8,128)(2,1)S(1)}, u32[]{:S(2)}, u32[]{:S(2)}) collective-permute-start(bf16[16,512]{1,0:T(8,128)(2,1)S(1)} %get-tuple-element.35), channel_id=1, source_target_pairs={{0,8},{8,16},{16,24},{24,32},{32,40},{40,48},{48,56},{56,64},{64,7... | collective-permute-start | bytes 49160 | tf_op jit(solution)/shard_map/ppermute | solution.py:546
  22.5 0.0 copy-start.3
  22.5 0.4 shard_map.120
  22.9 0.5 collective-permute-done.1.tail_ref
  23.4 0.0 copy-done.3
  23.4 2.7 %shard_map.121 = (bf16[4,256,128]{2,1,0:T(8,128)(2,1)S(1)}, f32[128,512]{1,0:T(8,128)S(1)}, f32[2,128,128]{2,1,0:T(8,128)S(1)}, bf16[2,128,128]{2,1,0:T(8,128)(2...) custom-call(bf16[128,512]{1,0:T(8,128)(2,1)S(1)} %get-tuple-element., ...), custom_call_target="tpu_custom_call" | custom-call | tf_op jit(solution)/shard_map/pallas_call | solution.py:478
  26.1 11.3 %all_to_all.26.got_ref.group_ref = bf16[4,256,128]{2,1,0:T(8,128)(2,1)S(1)} all-to-all(bf16[4,256,128]{2,1,0:T(8,128)(2,1)S(1)} %get-tuple-element.41), channel_id=1, replica_groups={{0,8,16,24},{32,40,48,56},{64,72,80,88},{96,104,112,120},{128,136,144,1..., dimensions={0} | all-to-all | bytes 524288 | tf_op jit(solution)/shard_map/all_to_all | solution.py:524
  37.4 0.4 shard_map.122.total_ref
  37.8 1.3 %collective-permute-start.2 = (bf16[256,128]{1,0:T(8,128)(2,1)S(1)}, bf16[256,128]{1,0:T(8,128)(2,1)S(1)}, u32[]{:S(2)}, u32[]{:S(2)}) collective-permute-start(bf16[256,128]{1,0:T(8,128)(2,1)S(1)} %shard_map.122.total_ref), channel_id=1, source_target_pairs={{0,32},{2,34},{4,36},{6,38},{9,41},{11,43},{13,45},{15,47},{16,48}... | collective-permute-start | bytes 196616 | tf_op jit(solution)/shard_map/ppermute | solution.py:532
  39.1 1.3 %collective-permute-start.4 = (bf16[256,128]{1,0:T(8,128)(2,1)S(1)}, bf16[256,128]{1,0:T(8,128)(2,1)S(1)}, u32[]{:S(2)}, u32[]{:S(2)}) collective-permute-start(bf16[256,128]{1,0:T(8,128)(2,1)S(1)} %shard_map.122.total_ref), channel_id=1, source_target_pairs={{0,96},{2,98},{4,100},{6,102},{9,105},{11,107},{13,109},{15,111},{... | collective-permute-start | bytes 196616 | tf_op jit(solution)/shard_map/ppermute | solution.py:532
  40.4 7.9 %collective-permute-done.2.last_ref = bf16[256,128]{1,0:T(8,128)(2,1)S(1)} collective-permute-done((bf16[256,128]{1,0:T(8,128)(2,1)S(1)}, bf16[256,128]{1,0:T(8,128)(2,1)S(1)}, u32[]{:S(2)}, u32[]{:S(2)}) %collective-permute-start.2) | collective-permute-done | bytes 65568 | tf_op jit(solution)/shard_map/ppermute | solution.py:532
  48.3 1.3 %collective-permute-start.3 = (bf16[256,128]{1,0:T(8,128)(2,1)S(1)}, bf16[256,128]{1,0:T(8,128)(2,1)S(1)}, u32[]{:S(2)}, u32[]{:S(2)}) collective-permute-start(bf16[256,128]{1,0:T(8,128)(2,1)S(1)} %collective-permute-done.2.last_ref), channel_id=1, source_target_pairs={{0,32},{2,34},{4,36},{6,38},{9,41},{11,43},{13,45},{15,47},{16,48}... | collective-permute-start | bytes 196616 | tf_op jit(solution)/shard_map/ppermute | solution.py:532
  49.6 7.2 %collective-permute-done.4.first_ref = bf16[256,128]{1,0:T(8,128)(2,1)S(1)} collective-permute-done((bf16[256,128]{1,0:T(8,128)(2,1)S(1)}, bf16[256,128]{1,0:T(8,128)(2,1)S(1)}, u32[]{:S(2)}, u32[]{:S(2)}) %collective-permute-start.4) | collective-permute-done | bytes 65568 | tf_op jit(solution)/shard_map/ppermute | solution.py:532
  56.8 1.4 %collective-permute-done.3.middle_ref = bf16[256,128]{1,0:T(8,128)(2,1)S(1)} collective-permute-done((bf16[256,128]{1,0:T(8,128)(2,1)S(1)}, bf16[256,128]{1,0:T(8,128)(2,1)S(1)}, u32[]{:S(2)}, u32[]{:S(2)}) %collective-permute-start.3) | collective-permute-done | bytes 65568 | tf_op jit(solution)/shard_map/ppermute | solution.py:532
  58.2 0.4 shard_map.123
  58.6 14.1 %all_to_all.27.rows_ref = bf16[4,256,128]{2,1,0:T(8,128)(2,1)S(1)} all-to-all(bf16[4,256,128]{2,1,0:T(8,128)(2,1)S(1)} %get-tuple-element.42), channel_id=1, replica_groups={{0,128,256,384},{8,136,264,392},{16,144,272,400},{24,152,280,408},{32,1..., dimensions={0} | all-to-all | bytes 524288 | tf_op jit(solution)/shard_map/all_to_all | solution.py:524
  72.7 0.0 copy-start.2
  72.7 0.9 shard_map.124
  73.7 0.0 copy-start
  73.7 9.1 %all_to_all.28.states_ref = bf16[4,128,128]{2,1,0:T(8,128)(2,1)S(1)} all-to-all(bf16[4,128,128]{2,1,0:T(8,128)(2,1)S(1)} %shard_map.124), channel_id=1, replica_groups={{0,8,16,24},{32,40,48,56},{64,72,80,88},{96,104,112,120},{128,136,144,1..., dimensions={0} | all-to-all | bytes 262144 | tf_op jit(solution)/shard_map/all_to_all | solution.py:524
  82.8 0.0 copy-start.1
  82.8 0.0 copy-start.4
  82.8 0.0 copy-start.5
  82.8 1.6 %shard_map.125 = (f32[128,512]{1,0:T(8,128)S(1)}, bf16[128,128]{1,0:T(8,128)(2,1)S(1)}, f32[8,512]{1,0:T(8,128)S(1)}) custom-call(bf16[4,128,128]{2,1,0:T(8,128)(2,1)S(1)} %all_to_all.28.states_ref, f32[128,512]{1,0:T(8,128)S(1)} %get-tuple-element.44.pre_ref, f32[2,128,128]{2,1,0:T(8,128)S(1)} %get-tuple-element.45.unit_ref, ...), custom_call_target="tpu_custom_call" | custom-call | tf_op jit(solution)/shard_map/pallas_call | solution.py:491
  84.4 1.3 %collective-permute-start.5 = (f32[8,512]{1,0:T(8,128)S(1)}, f32[8,512]{1,0:T(8,128)S(1)}, u32[]{:S(2)}, u32[]{:S(2)}) collective-permute-start(f32[8,512]{1,0:T(8,128)S(1)} %get-tuple-element.53), channel_id=1, source_target_pairs={{8,0},{16,8},{24,16},{32,24},{40,32},{48,40},{56,48},{64,56},{72,6... | collective-permute-start | bytes 49160 | tf_op jit(solution)/shard_map/ppermute | solution.py:562
  85.7 3.2 %collective-permute-done.5.halo_ref = f32[8,512]{1,0:T(8,128)S(1)} collective-permute-done((f32[8,512]{1,0:T(8,128)S(1)}, f32[8,512]{1,0:T(8,128)S(1)}, u32[]{:S(2)}, u32[]{:S(2)}) %collective-permute-start.5) | collective-permute-done | bytes 16416 | tf_op jit(solution)/shard_map/ppermute | solution.py:562
  88.9 0.0 copy-done.2
  88.9 0.0 copy-done
  88.9 0.0 copy-done.1
  88.9 0.0 copy-done.4
  88.9 0.0 copy-done.5
  88.9 0.6 shard_map.127
  89.5 9.2 %collective-permute-start.6 = (bf16[4,128,256]{2,1,0:T(8,128)(2,1)S(1)}, bf16[4,128,256]{2,1,0:T(8,128)(2,1)S(1)}, u32[]{:S(2)}, u32[]{:S(2)}) collective-permute-start(bf16[4,128,256]{2,1,0:T(8,128)(2,1)S(1)} %shard_map.127), channel_id=1, source_target_pairs={{0,1},{1,0},{2,3},{3,2},{4,5},{5,4},{6,7},{7,6},{8,9},{9,8},{10,11... | collective-permute-start | bytes 786440 | tf_op jit(solution)/shard_map/ppermute | solution.py:540
  98.7 0.6 shard_map.126.kept_ref
  99.4 0.5 collective-permute-done.6.got_ref
  99.9 8.8 %all_to_all.29.shares_ref = bf16[4,128,256]{2,1,0:T(8,128)(2,1)S(1)} all-to-all(bf16[4,128,256]{2,1,0:T(8,128)(2,1)S(1)} %shard_map.128), channel_id=1, replica_groups={{0,2,4,6},{1,3,5,7},{8,10,12,14},{9,11,13,15},{16,18,20,22},{17,19,21,2..., dimensions={0} | all-to-all | bytes 524288 | tf_op jit(solution)/shard_map/all_to_all | solution.py:537
  108.7 0.7 shard_map.129
  (1 shorter events, 0.0 us)
Async XLA Ops:
  11.0 9.6 %collective-permute-start = (bf16[4,128,256]{2,1,0:T(8,128)(2,1)S(1)}, bf16[4,128,256]{2,1,0:T(8,128)(2,1)S(1)}, u32[]{:S(2)}, u32[]{:S(2)}) collective-permute-start(bf16[4,128,256]{2,1,0:T(8,128)(2,1)S(1)} %all_to_all.25.x_ref), channel_id=1, source_target_pairs={{0,1},{1,0},{2,3},{3,2},{4,5},{5,4},{6,7},{7,6},{8,9},{9,8},{10,11... | collective-permute-start | bytes 786440 | tf_op jit(solution)/shard_map/ppermute | solution.py:540
  21.2 2.1 %collective-permute-start.1 = (bf16[16,512]{1,0:T(8,128)(2,1)S(1)}, bf16[16,512]{1,0:T(8,128)(2,1)S(1)}, u32[]{:S(2)}, u32[]{:S(2)}) collective-permute-start(bf16[16,512]{1,0:T(8,128)(2,1)S(1)} %get-tuple-element.35), channel_id=1, source_target_pairs={{0,8},{8,16},{16,24},{24,32},{32,40},{40,48},{48,56},{56,64},{64,7... | collective-permute-start | bytes 49160 | tf_op jit(solution)/shard_map/ppermute | solution.py:546
  22.5 0.9 copy-start.3
  37.8 10.5 %collective-permute-start.2 = (bf16[256,128]{1,0:T(8,128)(2,1)S(1)}, bf16[256,128]{1,0:T(8,128)(2,1)S(1)}, u32[]{:S(2)}, u32[]{:S(2)}) collective-permute-start(bf16[256,128]{1,0:T(8,128)(2,1)S(1)} %shard_map.122.total_ref), channel_id=1, source_target_pairs={{0,32},{2,34},{4,36},{6,38},{9,41},{11,43},{13,45},{15,47},{16,48}... | collective-permute-start | bytes 196616 | tf_op jit(solution)/shard_map/ppermute | solution.py:532
  39.1 17.7 %collective-permute-start.4 = (bf16[256,128]{1,0:T(8,128)(2,1)S(1)}, bf16[256,128]{1,0:T(8,128)(2,1)S(1)}, u32[]{:S(2)}, u32[]{:S(2)}) collective-permute-start(bf16[256,128]{1,0:T(8,128)(2,1)S(1)} %shard_map.122.total_ref), channel_id=1, source_target_pairs={{0,96},{2,98},{4,100},{6,102},{9,105},{11,107},{13,109},{15,111},{... | collective-permute-start | bytes 196616 | tf_op jit(solution)/shard_map/ppermute | solution.py:532
  48.3 9.9 %collective-permute-start.3 = (bf16[256,128]{1,0:T(8,128)(2,1)S(1)}, bf16[256,128]{1,0:T(8,128)(2,1)S(1)}, u32[]{:S(2)}, u32[]{:S(2)}) collective-permute-start(bf16[256,128]{1,0:T(8,128)(2,1)S(1)} %collective-permute-done.2.last_ref), channel_id=1, source_target_pairs={{0,32},{2,34},{4,36},{6,38},{9,41},{11,43},{13,45},{15,47},{16,48}... | collective-permute-start | bytes 196616 | tf_op jit(solution)/shard_map/ppermute | solution.py:532
  72.7 16.1 %copy-start.2 = (bf16[2048,128]{1,0:T(8,128)(2,1)S(1)}, bf16[2048,128]{1,0:T(8,128)(2,1)}, u32[]{:S(2)}) copy-start(bf16[2048,128]{1,0:T(8,128)(2,1)} %wk_ref.3) | copy-start | bytes 1572868
  73.7 15.2 %copy-start = (bf16[2048,256]{1,0:T(8,128)(2,1)S(1)}, bf16[2048,256]{1,0:T(8,128)(2,1)}, u32[]{:S(2)}) copy-start(bf16[2048,256]{1,0:T(8,128)(2,1)} %wv_ref.3) | copy-start | bytes 3145732
  82.8 6.1 %copy-start.1 = (bf16[2048,128]{1,0:T(8,128)(2,1)S(1)}, bf16[2048,128]{1,0:T(8,128)(2,1)}, u32[]{:S(2)}) copy-start(bf16[2048,128]{1,0:T(8,128)(2,1)} %wq_ref.3) | copy-start | bytes 1572868
  82.8 6.1 %copy-start.4 = (bf16[2048,2]{0,1:T(2,128)(2,1)S(1)}, bf16[2048,2]{0,1:T(2,128)(2,1)}, u32[]{:S(2)}) copy-start(bf16[2048,2]{0,1:T(2,128)(2,1)} %param.16) | copy-start | bytes 24580
  82.8 6.1 %copy-start.5 = (bf16[2048,2]{0,1:T(2,128)(2,1)S(1)}, bf16[2048,2]{0,1:T(2,128)(2,1)}, u32[]{:S(2)}) copy-start(bf16[2048,2]{0,1:T(2,128)(2,1)} %param.17) | copy-start | bytes 24580
  84.4 4.5 %collective-permute-start.5 = (f32[8,512]{1,0:T(8,128)S(1)}, f32[8,512]{1,0:T(8,128)S(1)}, u32[]{:S(2)}, u32[]{:S(2)}) collective-permute-start(f32[8,512]{1,0:T(8,128)S(1)} %get-tuple-element.53), channel_id=1, source_target_pairs={{8,0},{16,8},{24,16},{32,24},{40,32},{48,40},{56,48},{64,56},{72,6... | collective-permute-start | bytes 49160 | tf_op jit(solution)/shard_map/ppermute | solution.py:562
  89.5 10.4 %collective-permute-start.6 = (bf16[4,128,256]{2,1,0:T(8,128)(2,1)S(1)}, bf16[4,128,256]{2,1,0:T(8,128)(2,1)S(1)}, u32[]{:S(2)}, u32[]{:S(2)}) collective-permute-start(bf16[4,128,256]{2,1,0:T(8,128)(2,1)S(1)} %shard_map.127), channel_id=1, source_target_pairs={{0,1},{1,0},{2,3},{3,2},{4,5},{5,4},{6,7},{7,6},{8,9},{9,8},{10,11... | collective-permute-start | bytes 786440 | tf_op jit(solution)/shard_map/ppermute | solution.py:540

commit v11 on v9

--- a/solution.py
+++ b/solution.py
@@ -273,19 +273,20 @@
     before = compose(unpack(last_ref), compose(unpack(middle_ref), unpack(first_ref)))
     before_ref[0:DH] = before[0]
     before_ref[DH:] = before[1]
-    wider = pack(compose(unpack(total_ref), before))
-    for place in range(RADIX):
-        wider_ref[place] = wider
-
-
-def states_kernel(rows_ref, before_ref, group_ref, out_ref):
+    wider_ref[...] = pack(compose(unpack(total_ref), before))
+
+
+def rows_kernel(wider_ref, before_ref, got_ref, offset_ref, past_ref):
+    got = unpack(got_ref)
+    offset_ref[...] = bf(apply_map(unpack(wider_ref), got[1]))
+    past = compose((before_ref[0:DH], before_ref[DH:]), got)
+    past_ref[0:DH] = past[0]
+    past_ref[DH:] = past[1]
+
+
+def states_kernel(got_ref, past_ref, group_ref, out_ref):
     backward = is_backward()
-    place = in_order(lax.axis_index("ctx") // (RADIX * RADIX), backward)
-    state = jnp.zeros((DH, DH), F32)
-    for step in range(RADIX - 1):
-        later = apply_map(unpack(rows_ref.at[in_order(step, backward)]), state)
-        state = jnp.where(step < place, later, state)
-    state = apply_map((before_ref[0:DH], before_ref[DH:]), state)
+    state = apply_map((past_ref[0:DH], past_ref[DH:]), got_ref[...].astype(F32))
     for step in range(RADIX):
         spot = in_order(step, backward)
         out_ref[spot] = bf(state)
@@ -516,7 +517,6 @@
     parts = lax.axis_size("tp")
     slabs = range(count)
     group = [[s for s in slabs if s // RADIX == g] for g in range(count // RADIX)]
-    rank = [[s for s in slabs if s % 16 == z] for z in range(16)]
 
     def exchange(value, groups):
         return lax.all_to_all(value, "ctx", 0, 0, axis_index_groups=groups)
@@ -545,10 +545,15 @@
     total = call(group_kernel, [((PACK, DH), BF16)])(got)[0]
     last = onward(total, RADIX)
     earlier = [last, onward(last, RADIX), onward(total, 3 * RADIX)]
-    total, before = call(
-        window_kernel, [((RADIX, PACK, DH), BF16), ((PACK, DH), F32)]
-    )(total, *earlier)
-    states = call(states_kernel, [((RADIX, DH, DH), BF16)])(exchange(total, rank), before, got)[0]
+    packed = (PACK, DH)
+    wider, before = call(window_kernel, [(packed, BF16), (packed, F32)])(total, *earlier)
+    across_rows = RADIX * RADIX
+    offset, past = call(rows_kernel, [((DH, DH), BF16), (packed, F32)])(
+        wider, before, onward(wider, across_rows)
+    )
+    states = call(states_kernel, [((RADIX, DH, DH), BF16)])(
+        onward(offset, 2 * across_rows), past, got
+    )[0]
     states = exchange(states, group)
     full, grad_gates, halo = gradient(
         states, kept, cols, gap, gates, taps, scales, grad_core

time: 110 us -> 112 us (1.018)
  blocking collectives: 54.3 us -> 39.6 us
  starting transfers between devices: 37.3 us -> 51.3 us
  waiting for transfers between devices: 5.47 us -> 7.78 us
    all_to_all x3 -> x2, blocking collectives: 35.3 us -> 20.6 us  [exchange(): return lax.all_to_all(value, 'ctx', 0, 0, axis_index_groups=groups)]
    ppermute x3 -> x5, starting transfers between devices: 19 us -> 32.5 us  [onward(): lax.ppermute(value, 'ctx', [(s, t) for s, t in steps if 0 <= t < count])]
    ppermute x3 -> x5, waiting for transfers between devices: 1.31 us -> 3.62 us  [onward(): lax.ppermute(value, 'ctx', [(s, t) for s, t in steps if 0 <= t < count])]
  transfers between devices with their start and end apart: 7 -> 9, of which waited for: 4 -> 6; matrix products, arithmetic and copies ran while one was open for 0% -> 0% of each run, Pallas kernels for 3% -> 3%
where the time goes in v11:
time: 112 us; the launch traced here: 110 us
  starting transfers between devices  51.3 us (46%)
  blocking collectives  39.6 us (35%)
  Pallas kernels  10.7 us (10%)
  waiting for transfers between devices  7.78 us (7%)
    ppermute x5, starting transfers between devices, onward(): lax.ppermute(value, 'ctx', [(s, t) for s, t in steps if 0 <= t < count])  32.5 us
    all_to_all x2, blocking collectives, exchange(): return lax.all_to_all(value, 'ctx', 0, 0, axis_index_groups=groups)  20.6 us
    all_to_all x2, blocking collectives, across(): return lax.all_to_all(value, 'tp', 0, 0, axis_index_groups=chips)  19 us
    ppermute x2, starting transfers between devices, between(): return lax.ppermute(value, 'tp', [(t, t ^ 1) for t in range(parts)])  16.3 us
    ppermute x5, waiting for transfers between devices, onward(): lax.ppermute(value, 'ctx', [(s, t) for s, t in steps if 0 <= t < count])  3.62 us
    ppermute x1, waiting for transfers between devices, local(): halo = lax.ppermute(halo, 'ctx', [(s + 1, s) for s in range(count - 1)])  3.18 us
    pallas_call x1, Pallas kernels, slab(): call(slab_kernel, [((4, PACK, DH), BF16), ((DH, 4 * DH), F32), ((2,) + sq...  2.73 us
  transfers between devices with their start and end apart: 9, of which 6 were waited for; matrix products, arithmetic and copies ran while one was open for 0% of the time, Pallas kernels for 3%

profile of v11, /device:TPU:1, one launch (start us, length us, event | category | flops | bytes accessed | tf_op | source)
XLA Modules:
  0.0 110.5 jit_solution(13402344641105734614)
XLA Ops:
  0.0 0.9 broadcast_in_dim.2
  0.9 10.2 %all_to_all.20.x_ref = bf16[4,128,256]{2,1,0:T(8,128)(2,1)S(1)} all-to-all(bf16[4,128,256]{2,1,0:T(8,128)(2,1)S(1)} %broadcast_in_dim.2), channel_id=1, replica_groups={{0,2,4,6},{1,3,5,7},{8,10,12,14},{9,11,13,15},{16,18,20,22},{17,19,21,2..., dimensions={0} | all-to-all | bytes 524288 | tf_op jit(solution)/shard_map/all_to_all | solution.py:531
  11.0 7.7 %collective-permute-start = (bf16[4,128,256]{2,1,0:T(8,128)(2,1)S(1)}, bf16[4,128,256]{2,1,0:T(8,128)(2,1)S(1)}, u32[]{:S(2)}, u32[]{:S(2)}) collective-permute-start(bf16[4,128,256]{2,1,0:T(8,128)(2,1)S(1)} %all_to_all.20.x_ref), channel_id=1, source_target_pairs={{0,1},{1,0},{2,3},{3,2},{4,5},{5,4},{6,7},{7,6},{8,9},{9,8},{10,11... | collective-permute-start | bytes 786440 | tf_op jit(solution)/shard_map/ppermute | solution.py:534
  18.7 1.9 %shard_map.118 = (f32[128,512]{1,0:T(8,128)S(1)}, f32[128,128]{1,0:T(8,128)S(1)}, f32[8,512]{1,0:T(8,128)S(1)}, f32[2,128,128]{2,1,0:T(8,128)S(1)}, bf16[4,256,5...) custom-call(bf16[4,128,256]{2,1,0:T(8,128)(2,1)S(1)} %all_to_all.20.x_ref, bf16[4,2,256,128]{3,2,1,0:T(8,128)(2,1)} %bitcast.8, ...), custom_call_target="tpu_custom_call" | custom-call | tf_op jit(solution)/shard_map/pallas_call | solution.py:452
  20.6 0.0 collective-permute-done.x_ref
  20.7 0.6 shard_map.119
  21.2 1.3 %collective-permute-start.1 = (bf16[16,512]{1,0:T(8,128)(2,1)S(1)}, bf16[16,512]{1,0:T(8,128)(2,1)S(1)}, u32[]{:S(2)}, u32[]{:S(2)}) collective-permute-start(bf16[16,512]{1,0:T(8,128)(2,1)S(1)} %get-tuple-element.37), channel_id=1, source_target_pairs={{0,8},{8,16},{16,24},{24,32},{32,40},{40,48},{48,56},{56,64},{64,7... | collective-permute-start | bytes 49160 | tf_op jit(solution)/shard_map/ppermute | solution.py:540
  22.5 0.0 copy-start.3
  22.5 0.4 shard_map.120
  22.9 0.5 collective-permute-done.1.tail_ref
  23.4 0.0 copy-done.3
  23.4 2.7 %shard_map.121 = (bf16[4,256,128]{2,1,0:T(8,128)(2,1)S(1)}, f32[128,512]{1,0:T(8,128)S(1)}, f32[2,128,128]{2,1,0:T(8,128)S(1)}, bf16[2,128,128]{2,1,0:T(8,128)(2...) custom-call(bf16[128,512]{1,0:T(8,128)(2,1)S(1)} %get-tuple-element., ...), custom_call_target="tpu_custom_call" | custom-call | tf_op jit(solution)/shard_map/pallas_call | solution.py:477
  26.1 11.3 %all_to_all.21.got_ref.group_ref = bf16[4,256,128]{2,1,0:T(8,128)(2,1)S(1)} all-to-all(bf16[4,256,128]{2,1,0:T(8,128)(2,1)S(1)} %get-tuple-element.43), channel_id=1, replica_groups={{0,8,16,24},{32,40,48,56},{64,72,80,88},{96,104,112,120},{128,136,144,1..., dimensions={0} | all-to-all | bytes 524288 | tf_op jit(solution)/shard_map/all_to_all | solution.py:522
  37.4 0.4 shard_map.122.total_ref
  37.8 8.8 %collective-permute-start.2 = (bf16[256,128]{1,0:T(8,128)(2,1)S(1)}, bf16[256,128]{1,0:T(8,128)(2,1)S(1)}, u32[]{:S(2)}, u32[]{:S(2)}) collective-permute-start(bf16[256,128]{1,0:T(8,128)(2,1)S(1)} %shard_map.122.total_ref), channel_id=1, source_target_pairs={{0,32},{16,48},{32,64},{40,8},{48,80},{56,24},{64,96},{72,40},{80,... | collective-permute-start | bytes 196616 | tf_op jit(solution)/shard_map/ppermute | solution.py:526
  46.6 5.9 %collective-permute-start.4 = (bf16[256,128]{1,0:T(8,128)(2,1)S(1)}, bf16[256,128]{1,0:T(8,128)(2,1)S(1)}, u32[]{:S(2)}, u32[]{:S(2)}) collective-permute-start(bf16[256,128]{1,0:T(8,128)(2,1)S(1)} %shard_map.122.total_ref), channel_id=1, source_target_pairs={{0,96},{16,112},{32,128},{48,144},{64,160},{80,176},{96,192},{104,... | collective-permute-start | bytes 196616 | tf_op jit(solution)/shard_map/ppermute | solution.py:526
  52.6 0.0 collective-permute-done.2.last_ref
  52.6 4.3 %collective-permute-start.3 = (bf16[256,128]{1,0:T(8,128)(2,1)S(1)}, bf16[256,128]{1,0:T(8,128)(2,1)S(1)}, u32[]{:S(2)}, u32[]{:S(2)}) collective-permute-start(bf16[256,128]{1,0:T(8,128)(2,1)S(1)} %collective-permute-done.2.last_ref), channel_id=1, source_target_pairs={{0,32},{16,48},{32,64},{40,8},{48,80},{56,24},{64,96},{72,40},{80,... | collective-permute-start | bytes 196616 | tf_op jit(solution)/shard_map/ppermute | solution.py:526
  56.9 0.0 collective-permute-done.4.first_ref
  56.9 1.3 %collective-permute-done.3.middle_ref = bf16[256,128]{1,0:T(8,128)(2,1)S(1)} collective-permute-done((bf16[256,128]{1,0:T(8,128)(2,1)S(1)}, bf16[256,128]{1,0:T(8,128)(2,1)S(1)}, u32[]{:S(2)}, u32[]{:S(2)}) %collective-permute-start.3) | collective-permute-done | bytes 65568 | tf_op jit(solution)/shard_map/ppermute | solution.py:526
  58.2 0.4 shard_map.123
  58.6 7.4 %collective-permute-start.5 = (bf16[256,128]{1,0:T(8,128)(2,1)S(1)}, bf16[256,128]{1,0:T(8,128)(2,1)S(1)}, u32[]{:S(2)}, u32[]{:S(2)}) collective-permute-start(bf16[256,128]{1,0:T(8,128)(2,1)S(1)} %get-tuple-element.44.wider_ref), channel_id=1, source_target_pairs={{0,128},{16,144},{32,160},{48,176},{64,192},{80,208},{96,224},{112... | collective-permute-start | bytes 196616 | tf_op jit(solution)/shard_map/ppermute | solution.py:526
  66.1 1.3 %collective-permute-done.5.got_ref = bf16[256,128]{1,0:T(8,128)(2,1)S(1)} collective-permute-done((bf16[256,128]{1,0:T(8,128)(2,1)S(1)}, bf16[256,128]{1,0:T(8,128)(2,1)S(1)}, u32[]{:S(2)}, u32[]{:S(2)}) %collective-permute-start.5) | collective-permute-done | bytes 65568 | tf_op jit(solution)/shard_map/ppermute | solution.py:526
  67.4 0.2 shard_map.124
  67.5 6.0 %collective-permute-start.6 = (bf16[128,128]{1,0:T(8,128)(2,1)S(1)}, bf16[128,128]{1,0:T(8,128)(2,1)S(1)}, u32[]{:S(2)}, u32[]{:S(2)}) collective-permute-start(bf16[128,128]{1,0:T(8,128)(2,1)S(1)} %get-tuple-element.46), channel_id=1, source_target_pairs={{0,256},{16,272},{32,288},{48,304},{64,320},{80,336},{96,352},{112... | collective-permute-start | bytes 98312 | tf_op jit(solution)/shard_map/ppermute | solution.py:526
  73.6 1.0 collective-permute-done.6.got_ref
  74.6 0.0 copy-start
  74.6 0.5 shard_map.125
  75.1 9.3 %all_to_all.22.states_ref = bf16[4,128,128]{2,1,0:T(8,128)(2,1)S(1)} all-to-all(bf16[4,128,128]{2,1,0:T(8,128)(2,1)S(1)} %shard_map.125), channel_id=1, replica_groups={{0,8,16,24},{32,40,48,56},{64,72,80,88},{96,104,112,120},{128,136,144,1..., dimensions={0} | all-to-all | bytes 262144 | tf_op jit(solution)/shard_map/all_to_all | solution.py:522
  84.5 0.0 copy-start.1
  84.5 0.0 copy-start.2
  84.5 0.0 copy-start.4
  84.5 0.0 copy-start.5
  84.5 1.6 %shard_map.126 = (f32[128,512]{1,0:T(8,128)S(1)}, bf16[128,128]{1,0:T(8,128)(2,1)S(1)}, f32[8,512]{1,0:T(8,128)S(1)}) custom-call(bf16[4,128,128]{2,1,0:T(8,128)(2,1)S(1)} %all_to_all.22.states_ref, f32[128,512]{1,0:T(8,128)S(1)} %get-tuple-element.48.pre_ref, f32[2,128,128]{2,1,0:T(8,128)S(1)} %get-tuple-element.49.unit_ref, ...), custom_call_target="tpu_custom_call" | custom-call | tf_op jit(solution)/shard_map/pallas_call | solution.py:490
  86.1 1.3 %collective-permute-start.7 = (f32[8,512]{1,0:T(8,128)S(1)}, f32[8,512]{1,0:T(8,128)S(1)}, u32[]{:S(2)}, u32[]{:S(2)}) collective-permute-start(f32[8,512]{1,0:T(8,128)S(1)} %get-tuple-element.57), channel_id=1, source_target_pairs={{8,0},{16,8},{24,16},{32,24},{40,32},{48,40},{56,48},{64,56},{72,6... | collective-permute-start | bytes 49160 | tf_op jit(solution)/shard_map/ppermute | solution.py:561
  87.4 3.2 %collective-permute-done.7.halo_ref = f32[8,512]{1,0:T(8,128)S(1)} collective-permute-done((f32[8,512]{1,0:T(8,128)S(1)}, f32[8,512]{1,0:T(8,128)S(1)}, u32[]{:S(2)}, u32[]{:S(2)}) %collective-permute-start.7) | collective-permute-done | bytes 16416 | tf_op jit(solution)/shard_map/ppermute | solution.py:561
  90.5 0.0 copy-done
  90.5 0.0 copy-done.1
  90.5 0.0 copy-done.2
  90.5 0.0 copy-done.4
  90.6 0.0 copy-done.5
  90.6 0.6 shard_map.128
  91.2 8.6 %collective-permute-start.8 = (bf16[4,128,256]{2,1,0:T(8,128)(2,1)S(1)}, bf16[4,128,256]{2,1,0:T(8,128)(2,1)S(1)}, u32[]{:S(2)}, u32[]{:S(2)}) collective-permute-start(bf16[4,128,256]{2,1,0:T(8,128)(2,1)S(1)} %shard_map.128), channel_id=1, source_target_pairs={{0,1},{1,0},{2,3},{3,2},{4,5},{5,4},{6,7},{7,6},{8,9},{9,8},{10,11... | collective-permute-start | bytes 786440 | tf_op jit(solution)/shard_map/ppermute | solution.py:534
  99.8 0.6 shard_map.127.kept_ref
  100.4 0.5 collective-permute-done.8.got_ref
  101.0 8.8 %all_to_all.23.shares_ref = bf16[4,128,256]{2,1,0:T(8,128)(2,1)S(1)} all-to-all(bf16[4,128,256]{2,1,0:T(8,128)(2,1)S(1)} %shard_map.129), channel_id=1, replica_groups={{0,2,4,6},{1,3,5,7},{8,10,12,14},{9,11,13,15},{16,18,20,22},{17,19,21,2..., dimensions={0} | all-to-all | bytes 524288 | tf_op jit(solution)/shard_map/all_to_all | solution.py:531
  109.8 0.7 shard_map.130
  (1 shorter events, 0.0 us)
Async XLA Ops:
  11.0 9.6 %collective-permute-start = (bf16[4,128,256]{2,1,0:T(8,128)(2,1)S(1)}, bf16[4,128,256]{2,1,0:T(8,128)(2,1)S(1)}, u32[]{:S(2)}, u32[]{:S(2)}) collective-permute-start(bf16[4,128,256]{2,1,0:T(8,128)(2,1)S(1)} %all_to_all.20.x_ref), channel_id=1, source_target_pairs={{0,1},{1,0},{2,3},{3,2},{4,5},{5,4},{6,7},{7,6},{8,9},{9,8},{10,11... | collective-permute-start | bytes 786440 | tf_op jit(solution)/shard_map/ppermute | solution.py:534
  21.2 2.1 %collective-permute-start.1 = (bf16[16,512]{1,0:T(8,128)(2,1)S(1)}, bf16[16,512]{1,0:T(8,128)(2,1)S(1)}, u32[]{:S(2)}, u32[]{:S(2)}) collective-permute-start(bf16[16,512]{1,0:T(8,128)(2,1)S(1)} %get-tuple-element.37), channel_id=1, source_target_pairs={{0,8},{8,16},{16,24},{24,32},{32,40},{40,48},{48,56},{56,64},{64,7... | collective-permute-start | bytes 49160 | tf_op jit(solution)/shard_map/ppermute | solution.py:540
  22.5 0.9 copy-start.3
  37.8 14.8 %collective-permute-start.2 = (bf16[256,128]{1,0:T(8,128)(2,1)S(1)}, bf16[256,128]{1,0:T(8,128)(2,1)S(1)}, u32[]{:S(2)}, u32[]{:S(2)}) collective-permute-start(bf16[256,128]{1,0:T(8,128)(2,1)S(1)} %shard_map.122.total_ref), channel_id=1, source_target_pairs={{0,32},{16,48},{32,64},{40,8},{48,80},{56,24},{64,96},{72,40},{80,... | collective-permute-start | bytes 196616 | tf_op jit(solution)/shard_map/ppermute | solution.py:526
  46.6 10.2 %collective-permute-start.4 = (bf16[256,128]{1,0:T(8,128)(2,1)S(1)}, bf16[256,128]{1,0:T(8,128)(2,1)S(1)}, u32[]{:S(2)}, u32[]{:S(2)}) collective-permute-start(bf16[256,128]{1,0:T(8,128)(2,1)S(1)} %shard_map.122.total_ref), channel_id=1, source_target_pairs={{0,96},{16,112},{32,128},{48,144},{64,160},{80,176},{96,192},{104,... | collective-permute-start | bytes 196616 | tf_op jit(solution)/shard_map/ppermute | solution.py:526
  52.6 5.6 %collective-permute-start.3 = (bf16[256,128]{1,0:T(8,128)(2,1)S(1)}, bf16[256,128]{1,0:T(8,128)(2,1)S(1)}, u32[]{:S(2)}, u32[]{:S(2)}) collective-permute-start(bf16[256,128]{1,0:T(8,128)(2,1)S(1)} %collective-permute-done.2.last_ref), channel_id=1, source_target_pairs={{0,32},{16,48},{32,64},{40,8},{48,80},{56,24},{64,96},{72,40},{80,... | collective-permute-start | bytes 196616 | tf_op jit(solution)/shard_map/ppermute | solution.py:526
  58.6 8.7 %collective-permute-start.5 = (bf16[256,128]{1,0:T(8,128)(2,1)S(1)}, bf16[256,128]{1,0:T(8,128)(2,1)S(1)}, u32[]{:S(2)}, u32[]{:S(2)}) collective-permute-start(bf16[256,128]{1,0:T(8,128)(2,1)S(1)} %get-tuple-element.44.wider_ref), channel_id=1, source_target_pairs={{0,128},{16,144},{32,160},{48,176},{64,192},{80,208},{96,224},{112... | collective-permute-start | bytes 196616 | tf_op jit(solution)/shard_map/ppermute | solution.py:526
  67.5 7.0 %collective-permute-start.6 = (bf16[128,128]{1,0:T(8,128)(2,1)S(1)}, bf16[128,128]{1,0:T(8,128)(2,1)S(1)}, u32[]{:S(2)}, u32[]{:S(2)}) collective-permute-start(bf16[128,128]{1,0:T(8,128)(2,1)S(1)} %get-tuple-element.46), channel_id=1, source_target_pairs={{0,256},{16,272},{32,288},{48,304},{64,320},{80,336},{96,352},{112... | collective-permute-start | bytes 98312 | tf_op jit(solution)/shard_map/ppermute | solution.py:526
  74.6 16.0 %copy-start = (bf16[2048,256]{1,0:T(8,128)(2,1)S(1)}, bf16[2048,256]{1,0:T(8,128)(2,1)}, u32[]{:S(2)}) copy-start(bf16[2048,256]{1,0:T(8,128)(2,1)} %wv_ref.3) | copy-start | bytes 3145732
  84.5 6.1 %copy-start.1 = (bf16[2048,128]{1,0:T(8,128)(2,1)S(1)}, bf16[2048,128]{1,0:T(8,128)(2,1)}, u32[]{:S(2)}) copy-start(bf16[2048,128]{1,0:T(8,128)(2,1)} %wq_ref.3) | copy-start | bytes 1572868
  84.5 6.1 %copy-start.2 = (bf16[2048,128]{1,0:T(8,128)(2,1)S(1)}, bf16[2048,128]{1,0:T(8,128)(2,1)}, u32[]{:S(2)}) copy-start(bf16[2048,128]{1,0:T(8,128)(2,1)} %wk_ref.3) | copy-start | bytes 1572868
  84.5 6.1 %copy-start.4 = (bf16[2048,2]{0,1:T(2,128)(2,1)S(1)}, bf16[2048,2]{0,1:T(2,128)(2,1)}, u32[]{:S(2)}) copy-start(bf16[2048,2]{0,1:T(2,128)(2,1)} %param.16) | copy-start | bytes 24580
  84.5 6.1 %copy-start.5 = (bf16[2048,2]{0,1:T(2,128)(2,1)S(1)}, bf16[2048,2]{0,1:T(2,128)(2,1)}, u32[]{:S(2)}) copy-start(bf16[2048,2]{0,1:T(2,128)(2,1)} %param.17) | copy-start | bytes 24580
  86.1 4.5 %collective-permute-start.7 = (f32[8,512]{1,0:T(8,128)S(1)}, f32[8,512]{1,0:T(8,128)S(1)}, u32[]{:S(2)}, u32[]{:S(2)}) collective-permute-start(f32[8,512]{1,0:T(8,128)S(1)} %get-tuple-element.57), channel_id=1, source_target_pairs={{8,0},{16,8},{24,16},{32,24},{40,32},{48,40},{56,48},{64,56},{72,6... | collective-permute-start | bytes 49160 | tf_op jit(solution)/shard_map/ppermute | solution.py:561
  91.2 9.8 %collective-permute-start.8 = (bf16[4,128,256]{2,1,0:T(8,128)(2,1)S(1)}, bf16[4,128,256]{2,1,0:T(8,128)(2,1)S(1)}, u32[]{:S(2)}, u32[]{:S(2)}) collective-permute-start(bf16[4,128,256]{2,1,0:T(8,128)(2,1)S(1)} %shard_map.128), channel_id=1, source_target_pairs={{0,1},{1,0},{2,3},{3,2},{4,5},{5,4},{6,7},{7,6},{8,9},{9,8},{10,11... | collective-permute-start | bytes 786440 | tf_op jit(solution)/shard_map/ppermute | solution.py:534
